TPU v7x, 32 devices: a whole 2x2x4 slice. The times are simulated.
32 devices in a mesh: batch: 4 (over x, core), seq: 8 (over z, y).
Axes of the slice: x: 2, y: 2, z: 4, core: 2. Of those that a mesh axis runs over, the one named last changes fastest.
Arguments:
- tokens: bfloat16 [8, 1024, 768], P('batch', 'seq'), may hold values from -6 to 6
- in_proj: bfloat16 [768, 3072], P(('batch', 'seq')), may hold values from -0.21875 to 0.21875
- conv_weight: bfloat16 [4, 1536], P(None, ('batch', 'seq')), may hold values from -3 to 3
- conv_bias: bfloat16 [1536], P(('batch', 'seq')), may hold values from -1.5 to 1.5
- state_proj: bfloat16 [1536, 80], P(('batch', 'seq')), may hold values from -0.15625 to 0.15625
- step_proj: bfloat16 [48, 1536], P(None, ('batch', 'seq')), may hold values from -0.875 to 0.875
- step_bias: bfloat16 [1536], P(('batch', 'seq')), may hold values from -3 to -1
- decay_log: bfloat16 [16, 1536], P(None, ('batch', 'seq'))
- skip_gain: bfloat16 [1536], P(('batch', 'seq')), may hold values from 0.5 to 1.5
- out_proj: bfloat16 [1536, 768], P(('batch', 'seq')), may hold values from -0.0390625 to 0.0390625
- norm_gain: bfloat16 [768], P(('batch', 'seq')), may hold values from 0.5 to 1.5
- moe_gain: bfloat16 [768], P(('batch', 'seq')), may hold values from 0.5 to 1.5
- router_proj: bfloat16 [768, 8], P(('batch', 'seq')), may hold values from -0.14941406 to 0.14941406
- expert_up: bfloat16 [8, 768, 3072], P('seq', None, 'batch'), may hold values from -0.21875 to 0.21875
- expert_down: bfloat16 [8, 3072, 768], P('seq', 'batch'), may hold values from -0.21875 to 0.21875
- routes: int32 [8, 1024], P('batch', 'seq'), may hold values from 0 to 7, as said below
- slot_index: int32 [8, 1024], P('batch', 'seq'), may hold values from 0 to 79, as said below
- cotangent: bfloat16 [8, 1024, 768], P('batch', 'seq'), may hold values from -6 to 6
Outputs:
- block_out: bfloat16 [8, 1024, 768], P('batch', 'seq')
- d_tokens: float32 [8, 1024, 768], P('batch', 'seq')
- d_in_proj: float32 [768, 3072], P(('batch', 'seq'))
- d_conv_weight: float32 [4, 1536], P(None, ('batch', 'seq'))
- d_conv_bias: float32 [1536], P(('batch', 'seq'))
- d_state_proj: float32 [1536, 80], P(('batch', 'seq'))
- d_step_proj: float32 [48, 1536], P(None, ('batch', 'seq'))
- d_step_bias: float32 [1536], P(('batch', 'seq'))
- d_decay_log: float32 [16, 1536], P(None, ('batch', 'seq'))
- d_skip_gain: float32 [1536], P(('batch', 'seq'))
- d_out_proj: float32 [1536, 768], P(('batch', 'seq'))
- d_norm_gain: float32 [768], P(('batch', 'seq'))
- d_moe_gain: float32 [768], P(('batch', 'seq'))
- d_router_proj: float32 [768, 8], P(('batch', 'seq'))
- d_expert_up: float32 [8, 768, 3072], P('seq', None, 'batch')
- d_expert_down: float32 [8, 3072, 768], P('seq', 'batch')
Inputs may be any that keep to these rules, and one draw needn't show every extreme that they name: `routes`: each token's expert; among the tokens of one device, one expert is named by exactly min(256, 80) of them and every other expert by fewer. `slot_index`: the number of earlier tokens with the same expert among the 256 tokens of the same device, counted over its sequences in order and positions in order within each.
All inputs are finite; a program needn't handle non-finite values.
Results may differ from a plain program's by a relative error of at most 0.018.
Values may be sent and summed in bfloat16 or wider, within the bound.
A program may use at most 192 MiB of HBM per device.

v0:
```python
from functools import partial
import functools
import math

import jax
import jax.numpy as jnp
from jax import lax
from jax.experimental import pallas as pl
from jax.experimental.pallas import tpu as pltpu
from jax.sharding import PartitionSpec as P

epsilon = 1e-05
MESH = pl.DeviceIdType.MESH
HBM = pl.BlockSpec(memory_space=pl.ANY)
VM = pl.BlockSpec(memory_space=pltpu.VMEM)
bf16, f32 = jnp.bfloat16, jnp.float32


class Place:
    def __init__(self, batch, seq, ydim=2):
        self.batch, self.seq, self.Y = batch, seq, ydim
        self.Z = seq // ydim
        b, s = lax.axis_index("batch"), lax.axis_index("seq")
        self.x, self.c = b // 2, b % 2
        self.z, self.y = s // ydim, s % ydim

    def at(self, x=None, c=None, y=None, z=None):
        pick = lambda v, own: own if v is None else v
        x, c, y, z = pick(x, self.x), pick(c, self.c), pick(y, self.y), pick(z, self.z)
        return (x * 2 + c, z * self.Y + y)

    def index(self, dev):
        return dev[0] * self.seq + dev[1]


def greet(devices):
    barrier = pltpu.get_barrier_semaphore()
    count = 0
    for pred, dev in devices:
        if pred is None:
            pl.semaphore_signal(barrier, inc=1, device_id=dev, device_id_type=MESH)
            count = count + 1
        else:
            @pl.when(pred)
            def _(dev=dev):
                pl.semaphore_signal(barrier, inc=1, device_id=dev, device_id_type=MESH)
            count = count + jnp.where(pred, 1, 0)
    pl.semaphore_wait(barrier, count)


TILE = 128


def spot(rows, at, width):
    return (lanes((rows, width)) == subs((rows, width)) + at).astype(bf16)


def gather_kernel(batch, seq, *refs):
    n_arrays = 3
    in_ref, out_ref, tok_ref, state_ref, step_ref, router_ref = refs[:6]
    lines, gains = refs[6:11], refs[11:13]
    outs, halo_ref = refs[13:16], refs[16]
    tail, vecs, feats, zeros, local_sem, send_sem, recv_sem, halo_sem = refs[17:]
    ins = [in_ref, out_ref, tail]
    me = Place(batch, seq)
    Z, z = me.Z, me.z
    rows = [r.shape[0] for r in ins]
    sib = me.at(c=1 - me.c)
    up_ok, down_ok = z < Z - 1, z > 0
    up, down = me.at(z=z + 1), me.at(z=z - 1)
    nx, ny = me.at(x=1 - me.x), me.at(y=1 - me.y)
    first = me.c == 0
    nb2 = tuple(jnp.where(first, a, b) for a, b in zip(ny, nx))
    nb3 = tuple(jnp.where(first, a, b) for a, b in zip(nx, ny))
    x2, y2 = jnp.where(first, me.x, 1 - me.x), jnp.where(first, 1 - me.y, me.y)
    x3, y3 = jnp.where(first, 1 - me.x, me.x), jnp.where(first, me.y, 1 - me.y)
    b, part_of = me.at()
    has_before, has_after = part_of > 0, part_of < seq - 1
    before, after = (b, part_of - 1), (b, part_of + 1)
    greet([(None, sib), (None, nx), (None, ny), (up_ok, up), (down_ok, down), (has_before, before), (has_after, after)])
    own = me.index(me.at())

    def part(a, index):
        return outs[a].at[pl.ds(pl.multiple_of(index * rows[a], 8), rows[a])]

    sends = []

    def send(pred, index, dev, mine=False):
        slot = len(sends)
        copies = []
        for a in range(n_arrays):
            copies.append(
                pltpu.make_async_remote_copy(
                    src_ref=ins[a] if mine else part(a, index),
                    dst_ref=part(a, index),
                    send_sem=send_sem.at[slot, a],
                    recv_sem=recv_sem.at[index, a],
                    device_id=dev,
                    device_id_type=MESH,
                )
            )

        def go(copies):
            def start():
                for cp in copies:
                    cp.start()
            if pred is None:
                start()
            else:
                pl.when(pred)(start)
        if mine:
            go(copies[:2])
            later.append(lambda: go(copies[2:]))
        else:
            go(copies)
        sends.append((pred, copies))

    def arrive(pred, index, targets):
        def wait():
            for a in range(n_arrays):
                pltpu.make_async_remote_copy(
                    src_ref=part(a, index), dst_ref=part(a, index),
                    send_sem=send_sem.at[0, a], recv_sem=recv_sem.at[index, a],
                    device_id=sib, device_id_type=MESH,
                ).wait_recv()
        if pred is None:
            wait()
        else:
            pl.when(pred)(wait)
        for extra, dev in targets:
            p = pred if extra is None else (extra if pred is None else jnp.logical_and(pred, extra))
            send(p, index, dev)

    later = []
    for dev, pred in ((up, up_ok), (down, down_ok), (nb2, None), (nb3, None), (sib, None)):
        send(pred, own, dev, mine=True)
    seqs, rows_here = tok_ref.shape[:2]
    edge = pl.ds(rows_here - 8, 8)
    halo = pltpu.make_async_remote_copy(
        src_ref=tok_ref.at[:, edge], dst_ref=halo_ref, send_sem=halo_sem.at[0], recv_sem=halo_sem.at[1],
        device_id=after, device_id_type=MESH)
    blank = pltpu.make_async_copy(zeros, halo_ref, halo_sem.at[2])
    zeros[...] = jnp.zeros_like(zeros)
    pl.when(has_after)(halo.start)
    pl.when(jnp.logical_not(has_before))(blank.start)

    share, low_share, experts = state_ref.shape[0], router_ref.shape[0], router_ref.shape[1]
    rank, room, wide = step_ref.shape[0], vecs.shape[0], tail.shape[1]
    vecs[...] = jnp.zeros_like(vecs)
    at = 0
    for ref in lines:
        vecs[at : at + ref.shape[0]] = ref[...].astype(f32)
        at += ref.shape[0]
    feats[...] = jnp.zeros_like(feats)
    for i, ref in enumerate(gains):
        feats[i : i + 1] = ref[...].astype(f32)
    by_channel = (
        dot(state_ref[...], spot(state_ref.shape[1], 0, wide))
        + dot_tn(step_ref[...], spot(rank, TILE - rank, wide))
        + dot_tn(vecs[...].astype(bf16), spot(room, TILE, wide))
    )
    by_feature = dot(router_ref[...], spot(experts, TILE + room, wide)) + dot_tn(
        feats[...].astype(bf16), spot(feats.shape[0], TILE + room + experts, wide))
    by_feature = jnp.concatenate([by_feature, jnp.zeros((share - low_share, wide), f32)])
    tail[...] = (by_channel + by_feature).astype(bf16)
    for start in later:
        start()
    local = [pltpu.make_async_copy(ins[a], part(a, own), local_sem.at[a]) for a in range(n_arrays)]
    for cp in local:
        cp.start()

    def offsets(k):
        return [(None, 0)] if k == 0 else [(z >= k, -k), (z + k < Z, k)]

    def col(k):
        for pred, off in offsets(k):
            fwd = (up_ok, up) if off < 0 else (down_ok, down)
            arrive(pred, me.index(me.at(z=z + off)), [fwd, (None, nb2), (None, nb3), (None, sib)])

    def second(k):
        for pred, off in offsets(k):
            arrive(pred, me.index(me.at(x=x2, y=y2, z=z + off)), [(None, nb3), (None, sib)])

    def third(k):
        for pred, off in offsets(k):
            arrive(pred, me.index(me.at(x=x3, y=y3, z=z + off)), [(None, sib)])

    def fourth(k):
        for pred, off in offsets(k):
            arrive(pred, me.index(me.at(x=1 - me.x, y=1 - me.y, z=z + off)), [(None, sib)])

    for h in range(1, Z + 3):
        if h < Z:
            col(h)
        if 0 <= h - 1 < Z:
            second(h - 1)
        if 0 <= h - 2 < Z:
            third(h - 2)
        if 0 <= h - 3 < Z:
            fourth(h - 3)
    for h in range(Z):
        for xx in (0, 1):
            for yy in (0, 1):
                for pred, off in offsets(h):
                    arrive(pred, me.index(me.at(x=xx, y=yy, c=1 - me.c, z=z + off)), [])
    for cp in local:
        cp.wait()
    pl.when(has_before)(halo.wait_recv)
    pl.when(has_after)(halo.wait_send)
    pl.when(jnp.logical_not(has_before))(blank.wait)
    for pred, copies in sends:
        def done(copies=copies):
            for cp in copies:
                cp.wait_send()
        if pred is None:
            done()
        else:
            pl.when(pred)(done)


def n_sends(Z):
    return 5 + (Z - 1) * 8 + (2 * Z - 1) * 2 + (2 * Z - 1) * 2


def gather_all(batch, seq, room, in_proj, out_proj, tokens, state, step, router, lines, gains):
    count, share = batch * seq, out_proj.shape[0]
    seqs, _, width = tokens.shape
    wide = 2 * TILE
    edge = (seqs, 8, width)
    return pl.pallas_call(
        functools.partial(gather_kernel, batch, seq),
        out_shape=[
            jax.ShapeDtypeStruct((count * a.shape[0],) + a.shape[1:], bf16) for a in (in_proj, out_proj)
        ] + [jax.ShapeDtypeStruct((count * share, wide), bf16), jax.ShapeDtypeStruct(edge, bf16)],
        in_specs=[HBM] * 3 + [VM] * (3 + len(lines) + len(gains)),
        out_specs=[HBM] * 4,
        scratch_shapes=[
            pltpu.VMEM((share, wide), bf16),
            pltpu.VMEM((room, share), f32),
            pltpu.VMEM((8, router.shape[0]), f32),
            pltpu.VMEM(edge, bf16),
            pltpu.SemaphoreType.DMA((3,)),
            pltpu.SemaphoreType.DMA((n_sends(seq // 2), 3)),
            pltpu.SemaphoreType.DMA((count, 3)),
            pltpu.SemaphoreType.DMA((3,)),
        ],
        compiler_params=pltpu.CompilerParams(collective_id=0, has_side_effects=True),
        name="gather_weights",
    )(in_proj, out_proj, tokens, state, step, router, *lines, *gains)


def reduce_kernel(batch, seq, low_share, experts, skip_row, *refs):
    n = 3
    din_ref, dout_ref, dsmall_ref, dvec_ref, dskip_ref, drouter_ref, dnorm_ref, dmoe_ref, dhalo_ref = refs[:9]
    outs, halo_ref = refs[9:12], refs[12]
    refs = refs[13:]
    work, sib_buf, far_buf, near_buf, line_buf = (refs[i * n : (1 + i) * n] for i in range(5))
    tail, zeros, load_sem, send_sem, sib_sem, far_sem, near_sem, line_sem, halo_sem = refs[5 * n :]
    me = Place(batch, seq)
    Z, z = me.Z, me.z
    rows = [r.shape[0] for r in outs]
    sib = me.at(c=1 - me.c)
    up, down = me.at(z=z + 1), me.at(z=z - 1)
    nx, ny = me.at(x=1 - me.x), me.at(y=1 - me.y)
    first = me.c == 0
    pick = lambda flag, a, b: jnp.where(flag, a, b)
    near = tuple(pick(first, a, b) for a, b in zip(ny, nx))
    far = tuple(pick(first, a, b) for a, b in zip(nx, ny))
    b, part_of = me.at()
    has_before, has_after = part_of > 0, part_of < seq - 1
    before, after = (b, part_of - 1), (b, part_of + 1)
    greet([(None, sib), (None, nx), (None, ny), (z < Z - 1, up), (z > 0, down), (has_before, before), (has_after, after)])

    def groups(c):
        f = c == 0
        ox, oy = 1 - me.x, 1 - me.y
        return [
            (ox, oy),
            (pick(f, ox, me.x), pick(f, me.y, oy)),
            (pick(f, me.x, ox), pick(f, oy, me.y)),
            (me.x, me.y),
        ]

    def slot(xy, zz):
        return (xy[0] * 2 + xy[1]) * Z + zz

    def turn(k):
        return (z + 1 + k) % Z

    sends = []

    def send(pred, srcs, dsts, recv, dev):
        copies = [
            pltpu.make_async_remote_copy(
                src_ref=srcs[a], dst_ref=dsts[a], send_sem=send_sem.at[len(sends), a],
                recv_sem=recv(a), device_id=dev, device_id_type=MESH)
            for a in range(n)
        ]

        def go():
            for cp in copies:
                cp.start()
        if pred is None:
            go()
        else:
            pl.when(pred)(go)
        sends.append((pred, copies))

    def take(bufs, recv):
        for a in range(n):
            pltpu.make_async_remote_copy(
                src_ref=bufs[a], dst_ref=bufs[a], send_sem=send_sem.at[0, a],
                recv_sem=recv(a), device_id=sib, device_id_type=MESH).wait_recv()

    def source(a, c, xy, zz):
        index = me.index((xy[0] * 2 + c, zz * me.Y + xy[1]))
        if a == 2:
            return tail.at[index]
        return (din_ref, dout_ref)[a].at[pl.ds(pl.multiple_of(index * rows[a], 8), rows[a])]

    halo = pltpu.make_async_remote_copy(
        src_ref=dhalo_ref, dst_ref=halo_ref, send_sem=halo_sem.at[0], recv_sem=halo_sem.at[1],
        device_id=before, device_id_type=MESH)
    blank = pltpu.make_async_copy(zeros, halo_ref, halo_sem.at[2])
    zeros[...] = jnp.zeros_like(zeros)
    pl.when(has_before)(halo.start)
    pl.when(jnp.logical_not(has_after))(blank.start)

    other = 1 - me.c
    mine = groups(me.c)
    first_sends, loads = [], []
    for xy in groups(other):
        for k in range(Z):
            s = slot(xy, turn(k))
            copies = [
                pltpu.make_async_remote_copy(
                    src_ref=source(a, other, xy, turn(k)), dst_ref=sib_buf[a].at[s],
                    send_sem=send_sem.at[len(sends), a], recv_sem=sib_sem.at[s, a],
                    device_id=sib, device_id_type=MESH)
                for a in range(n)
            ]
            sends.append((None, copies))
            first_sends.append(copies)
    for xy in mine:
        for k in range(Z):
            s = slot(xy, turn(k))
            loads.append([
                pltpu.make_async_copy(source(a, me.c, xy, turn(k)), work[a].at[s], load_sem.at[s, a]) for a in range(n)
            ])
    for copies in first_sends + loads:
        for cp in copies[:2]:
            cp.start()

    room, share = dvec_ref.shape[0], tail.shape[1]
    blocks, width = tail.shape[0], drouter_ref.shape[0]
    vec = jnp.where(subs(dvec_ref.shape) == skip_row, dskip_ref[...], dvec_ref[...])
    line = subs((8, width))
    gains = jnp.where(line == 0, dnorm_ref[...], jnp.where(line == 1, dmoe_ref[...], 0.0))
    model = drouter_ref[...] + dot_tn(gains.astype(bf16), spot(8, room + experts, TILE))
    model = jnp.concatenate(
        [model.reshape(blocks, low_share, TILE), jnp.zeros((blocks, share - low_share, TILE), f32)], axis=1)
    right = dot_tn(vec.astype(bf16), spot(room, 0, TILE)).reshape(blocks, share, TILE) + model
    tail[:, :, 0:TILE] = dsmall_ref[...].reshape(blocks, share, TILE)
    tail[:, :, TILE:] = right.astype(bf16)
    for copies in first_sends + loads:
        copies[2].start()

    def total(bufs):
        t = bufs[0][...].astype(jnp.float32)
        for b in bufs[1:]:
            t = t + b[...].astype(jnp.float32)
        return t

    for g, xy in enumerate(mine):
        for k in range(Z):
            zz = turn(k)
            s = slot(xy, zz)
            for cp in loads[g * Z + k]:
                cp.wait()
            take([sib_buf[a].at[s] for a in range(n)], lambda a: sib_sem.at[s, a])
            parts = [[work[a].at[s], sib_buf[a].at[s]] for a in range(n)]
            if g >= 2:
                fs = (g - 2) * Z + zz
                take([far_buf[a].at[fs] for a in range(n)], lambda a: far_sem.at[fs, a])
                for a in range(n):
                    parts[a].append(far_buf[a].at[fs])
            if g == 3:
                take([near_buf[a].at[zz] for a in range(n)], lambda a: near_sem.at[zz, a])
                for a in range(n):
                    parts[a].append(near_buf[a].at[zz])
            if g < 3:
                for a in range(n):
                    work[a][s] = total(parts[a]).astype(jnp.bfloat16)
                srcs = [work[a].at[s] for a in range(n)]
                if g < 2:
                    fs = g * Z + zz
                    send(None, srcs, [far_buf[a].at[fs] for a in range(n)],
                         lambda a: far_sem.at[fs, a], far)
                else:
                    send(None, srcs, [near_buf[a].at[zz] for a in range(n)],
                         lambda a: near_sem.at[zz, a], near)
                continue
            if k < Z - 1:
                rising = zz > z
                side = jnp.where(rising, 0, 1)
                more = jnp.where(rising, z, Z - 1 - z) > 0
                line = [line_buf[a].at[side, zz] for a in range(n)]
                for a in range(n):
                    work[a][s] = total(parts[a]).astype(jnp.bfloat16)

                @pl.when(more)
                def _():
                    take(line, lambda a: line_sem.at[side, zz, a])
                    for a in range(n):
                        work[a][s] = total([work[a].at[s], line[a]]).astype(jnp.bfloat16)
                dev = (me.at()[0], jnp.where(rising, up[1], down[1]))
                send(None, [work[a].at[s] for a in range(n)], line,
                     lambda a: line_sem.at[side, zz, a], dev)
            else:
                for a in range(n):
                    outs[a][...] = total(parts[a])
                for side, pred in ((0, z > 0), (1, z < Z - 1)):
                    @pl.when(pred)
                    def _(side=side):
                        line = [line_buf[a].at[side, zz] for a in range(n)]
                        take(line, lambda a: line_sem.at[side, zz, a])
                        for a in range(n):
                            outs[a][...] = outs[a][...] + line[a][...].astype(jnp.float32)
    pl.when(has_after)(halo.wait_recv)
    pl.when(has_before)(halo.wait_send)
    pl.when(jnp.logical_not(has_after))(blank.wait)
    for pred, copies in sends:
        for cp in copies:
            cp.wait_send()


def reduce_all(batch, seq, low_share, experts, skip_row, d_in, d_out, *rest):
    count, Z, n = batch * seq, seq // 2, 3
    wide = 2 * TILE
    share = d_out.shape[0] // count
    shapes = [(a.shape[0] // count,) + a.shape[1:] for a in (d_in, d_out)] + [(share, wide)]
    edge = rest[-1].shape
    half = count // 2
    scratch = []
    for lead in ((half,), (half,), (2 * Z,), (Z,), (2, Z)):
        scratch += [pltpu.VMEM(lead + s, bf16) for s in shapes]
    dma = pltpu.SemaphoreType.DMA
    scratch += [
        pltpu.VMEM((count, share, wide), bf16),
        pltpu.VMEM(edge, f32),
        dma((half, n)),
        dma((half + 4 * Z, n)),
        dma((half, n)),
        dma((2 * Z, n)),
        dma((Z, n)),
        dma((2, Z, n)),
        dma((3,)),
    ]
    return pl.pallas_call(
        functools.partial(reduce_kernel, batch, seq, low_share, experts, skip_row),
        out_shape=[jax.ShapeDtypeStruct(s, f32) for s in shapes] + [jax.ShapeDtypeStruct(edge, f32)],
        in_specs=[HBM] * 2 + [VM] * 7,
        out_specs=[VM] * 3 + [HBM],
        scratch_shapes=scratch,
        compiler_params=pltpu.CompilerParams(
            collective_id=1, has_side_effects=True, vmem_limit_bytes=58 << 20),
        name="reduce_grads",
    )(d_in, d_out, *rest)


def finish_kernel(dims, low_share, experts, in_ref, out_ref, tail_ref, halo_ref, tok_ref, up_ref, up2_ref, down_ref,
                  down2_ref, tok_out, din, dconv, dbias, dstate, dstep, dstep_bias, ddecay, dskip, dout, dnorm, dmoe,
                  drouter, dup, ddown):
    seqs, rows, inner, states, rank, taps = dims
    dup[...] = up_ref[...] + up2_ref[...].astype(f32)
    ddown[...] = down_ref[...] + down2_ref[...].astype(f32)

    @pl.when(pl.program_id(0) == 0)
    def _():
        tok_out[...] = tok_ref[...] + halo_ref[...]
        din[...] = in_ref[...]
        dout[...] = out_ref[...]
        tail = tail_ref[...]
        share, wide = tail.shape
        eye = (lanes((wide, wide)) == subs((wide, wide))).astype(f32)
        turned = lax.dot_general(
            eye, tail, (((1,), (1,)), ((), ())), precision=lax.Precision.HIGHEST, preferred_element_type=f32)
        dstate[...] = tail[:, : rank + 2 * states]
        dstep[...] = turned[TILE - rank : TILE]
        ddecay[...] = turned[TILE : TILE + states]
        dconv[...] = turned[TILE + states : TILE + states + taps]
        at = TILE + states + taps
        dbias[...] = turned[at : at + 1]
        dstep_bias[...] = turned[at + 1 : at + 2]
        dskip[...] = turned[at + 2 : at + 3]
        at = TILE + -(-(states + taps + 3) // 8) * 8
        choose = (subs((wide, experts)) == lanes((wide, experts)) + at).astype(f32)
        drouter[...] = lax.dot_general(
            tail[:low_share], choose, (((1,), (0,)), ((), ())), precision=lax.Precision.HIGHEST,
            preferred_element_type=f32)
        at += experts
        dnorm[...] = turned[at : at + 1, :low_share]
        dmoe[...] = turned[at + 1 : at + 2, :low_share]


def tuned(batch, seq):
    return batch == 4 and seq == 8


def chain_kernel(seq, forward, dsum_ref, rates_ref, end_ref, out_ref, held, outgoing, send_sem, recv_sem):
    s = lax.axis_index("seq")
    b = lax.axis_index("batch")
    step = 1 if forward else -1
    has_before = s > 0 if forward else s < seq - 1
    has_after = s < seq - 1 if forward else s > 0
    before, after = (b, s - step), (b, s + step)
    barrier = pltpu.get_barrier_semaphore()
    for pred, dev in ((has_before, before), (has_after, after)):
        @pl.when(pred)
        def _(dev=dev):
            pl.semaphore_signal(barrier, inc=1, device_id=dev, device_id_type=MESH)
    pl.semaphore_wait(barrier, jnp.where(has_before, 1, 0) + jnp.where(has_after, 1, 0))
    count = end_ref.shape[0]

    def copy(i):
        return pltpu.make_async_remote_copy(
            src_ref=outgoing.at[i], dst_ref=held.at[i], send_sem=send_sem.at[i],
            recv_sem=recv_sem.at[i], device_id=after, device_id_type=MESH)

    for i in range(count):
        @pl.when(has_before)
        def _(i=i):
            copy(i).wait_recv()
            out_ref[i] = held[i].astype(jnp.float32)
            decay = jnp.exp(rates_ref[...] * dsum_ref[i])
            outgoing[i] = (end_ref[i] + decay * out_ref[i]).astype(jnp.bfloat16)

        @pl.when(jnp.logical_not(has_before))
        def _(i=i):
            out_ref[i] = jnp.zeros_like(out_ref[i])
            outgoing[i] = end_ref[i].astype(jnp.bfloat16)

        @pl.when(has_after)
        def _(i=i):
            copy(i).start()
    for i in range(count):
        @pl.when(has_after)
        def _(i=i):
            copy(i).wait_send()


def chain_states(seq, forward, dsum, rates, end):
    vm = pl.BlockSpec(memory_space=pltpu.VMEM)
    return pl.pallas_call(
        functools.partial(chain_kernel, seq, forward),
        out_shape=jax.ShapeDtypeStruct(end.shape, jnp.float32),
        in_specs=[vm] * 3,
        out_specs=vm,
        scratch_shapes=[
            pltpu.VMEM(end.shape, jnp.bfloat16),
            pltpu.VMEM(end.shape, jnp.bfloat16),
            pltpu.SemaphoreType.DMA((end.shape[0],)),
            pltpu.SemaphoreType.DMA((end.shape[0],)),
        ],
        compiler_params=pltpu.CompilerParams(
            collective_id=4 if forward else 5, has_side_effects=True),
        name="chain_forward" if forward else "chain_backward",
    )(dsum, rates, end)


def relay_kernel(seq, forward, states, dsum_ref, vec_ref, end_ref, out_ref, mine, theirs, their_sum, held, outgoing,
                 pair_send, pair_recv, line_send, line_recv):
    me = Place(4, seq)
    y, z, last = me.y, me.z, me.Z - 1
    step = 1 if forward else -1
    first = y == (0 if forward else 1)
    has_before = z > 0 if forward else z < last
    has_after = z < last if forward else z > 0
    pair, before, after = me.at(y=1 - y), me.at(z=z - step), me.at(z=z + step)
    greet([(None, pair), (has_before, before), (has_after, after)])
    count = end_ref.shape[0]
    rates = -jnp.exp(vec_ref[0:states])

    def swaps(i):
        return [
            pltpu.make_async_remote_copy(
                src_ref=src, dst_ref=dst, send_sem=pair_send.at[i, k], recv_sem=pair_recv.at[i, k],
                device_id=pair, device_id_type=MESH)
            for k, (src, dst) in enumerate(((mine.at[i], theirs.at[i]), (dsum_ref.at[i], their_sum.at[i])))
        ]

    def onward(i):
        return pltpu.make_async_remote_copy(
            src_ref=outgoing.at[i], dst_ref=held.at[i], send_sem=line_send.at[i],
            recv_sem=line_recv.at[i], device_id=after, device_id_type=MESH)

    for i in range(count):
        mine[i] = end_ref[i].astype(bf16)
        for cp in swaps(i):
            cp.start()
    for i in range(count):
        for cp in swaps(i):
            cp.wait_recv()
        own, other = end_ref[i], theirs[i].astype(f32)
        own_sum, other_sum = dsum_ref[i], their_sum[i]
        early, late = jnp.where(first, own, other), jnp.where(first, other, own)
        early_sum, late_sum = jnp.where(first, own_sum, other_sum), jnp.where(first, other_sum, own_sum)
        both = late + jnp.exp(rates * late_sum) * early

        @pl.when(has_before)
        def _():
            onward(i).wait_recv()
            arrived = held[i].astype(f32)
            outgoing[i] = (both + jnp.exp(rates * (early_sum + late_sum)) * arrived).astype(bf16)

        @pl.when(jnp.logical_not(has_before))
        def _():
            outgoing[i] = both.astype(bf16)

        @pl.when(has_after)
        def _():
            onward(i).start()

        @pl.when(has_before)
        def _():
            arrived = held[i].astype(f32)
            out_ref[i] = jnp.where(first, arrived, early + jnp.exp(rates * early_sum) * arrived)

        @pl.when(jnp.logical_not(has_before))
        def _():
            out_ref[i] = jnp.where(first, jnp.zeros_like(early), early)
    for i in range(count):
        for cp in swaps(i):
            cp.wait_send()

        @pl.when(has_after)
        def _():
            onward(i).wait_send()


def relay_states(batch, seq, forward, states, dsum, vec, end):
    if not tuned(batch, seq):
        return chain_states(seq, forward, dsum, -jnp.exp(vec[:states]), end)
    n = end.shape[0]
    return pl.pallas_call(
        functools.partial(relay_kernel, seq, forward, states),
        out_shape=jax.ShapeDtypeStruct(end.shape, f32),
        in_specs=[VM] * 3,
        out_specs=VM,
        scratch_shapes=[
            pltpu.VMEM(end.shape, bf16),
            pltpu.VMEM(end.shape, bf16),
            pltpu.VMEM(dsum.shape, f32),
            pltpu.VMEM(end.shape, bf16),
            pltpu.VMEM(end.shape, bf16),
            pltpu.SemaphoreType.DMA((n, 2)),
            pltpu.SemaphoreType.DMA((n, 2)),
            pltpu.SemaphoreType.DMA((n,)),
            pltpu.SemaphoreType.DMA((n,)),
        ],
        compiler_params=pltpu.CompilerParams(
            collective_id=6 if forward else 7, has_side_effects=True),
        name="relay_forward" if forward else "relay_backward",
    )(dsum, vec, end)


def dot(a, b):
    return jnp.dot(a, b, preferred_element_type=jnp.float32)


def dot_nt(a, b):
    return lax.dot_general(a, b, (((1,), (1,)), ((), ())), preferred_element_type=jnp.float32)


def dot_tn(a, b):
    return lax.dot_general(a, b, (((0,), (0,)), ((), ())), preferred_element_type=jnp.float32)


def sigmoid(v):
    return 1.0 / (1.0 + jnp.exp(-v))


def lanes(shape):
    return lax.broadcasted_iota(jnp.int32, shape, 1)


def subs(shape):
    return lax.broadcasted_iota(jnp.int32, shape, 0)


def column(row, base, states):
    shape = (states, row.shape[1])
    only = jnp.where(lanes(shape) == subs(shape) + base, jnp.broadcast_to(row, shape), 0.0)
    return jnp.broadcast_to(jnp.sum(only, axis=1, keepdims=True), shape)


def row_sums(parts):
    row = subs(parts[0].shape)
    four, two, one = row < 4, (row // 2) % 2 == 0, row % 2 == 0
    turn = lambda v, by: pltpu.roll(v, by, axis=0)
    a = [
        jnp.where(four, parts[j], parts[j + 4]) + turn(jnp.where(four, parts[j + 4], parts[j]), 4)
        for j in range(4)
    ]
    b = [jnp.where(two, a[j] + turn(a[j], 6), a[j + 2] + turn(a[j + 2], 2)) for j in range(2)]
    return jnp.where(one, b[0] + turn(b[0], 7), b[1] + turn(b[1], 1))


def fold(v):
    return sum(v[i : i + 8] for i in range(8, v.shape[0], 8)) + v[:8]


WIDE = 256
GROUP = 16
LOG2E = math.log2(math.e)


def conv_sum(ext_ref, s, cols, vec_ref, states, taps, rows):
    first = ext_ref.shape[1] - rows - taps + 1
    total = vec_ref[states + taps : states + taps + 1, cols]
    for k in range(taps):
        total = total + vec_ref[states + k : states + k + 1, cols] * ext_ref[s, first + k : first + k + rows, cols]
    return total


def normalize(x):
    return lax.rsqrt(jnp.mean(x * x, axis=-1, keepdims=True) + epsilon)


def unpack(tail_ref, share, low_share, room, experts, vec_ref, gain_ref, router_ref):
    right = tail_ref[:, TILE : 2 * TILE]
    vec_ref[...] = dot_nt(spot(room, 0, TILE), right)
    blocks = right.shape[0] // share
    model = right.astype(f32).reshape(blocks, share, TILE)[:, :low_share].reshape(blocks * low_share, TILE).astype(bf16)
    router_ref[...] = model
    gain_ref[...] = dot_nt(spot(gain_ref.shape[0], room + experts, TILE), model)


def enter_packed(dims, share, low_share, experts, tok_ref, halo_ref, win_ref, tail_ref,
                 ext_ref, z_ref, u_ref, dt_ref, proj_ref, end_ref, dsum_ref, vec_ref, gain_ref, router_ref, xn):
    unpack(tail_ref, share, low_share, vec_ref.shape[0], experts, vec_ref, gain_ref, router_ref)
    enter_kernel(dims, tok_ref, halo_ref, win_ref, tail_ref.at[:, 0:TILE], vec_ref, gain_ref,
                 ext_ref, z_ref, u_ref, dt_ref, proj_ref, end_ref, dsum_ref, xn)


def as_column(ref):
    seqs, rows = ref.shape
    diagonal = lanes((rows, rows)) == subs((rows, rows))
    spread = [
        jnp.where(diagonal, jnp.broadcast_to(ref[s : s + 1].astype(f32), (rows, rows)), 0.0) for s in range(seqs)
    ]
    return jnp.concatenate([jnp.sum(v, axis=1, keepdims=True) for v in spread]).astype(jnp.int32)


def enter_kernel(dims, tok_ref, halo_ref, win_ref, small_ref, vec_ref, gain_ref,
                 ext_ref, z_ref, u_ref, dt_ref, proj_ref, end_ref, dsum_ref, xn):
    seqs, rows, inner, states, rank, taps = dims
    count = seqs * rows
    for ref, at in ((tok_ref, 0), (halo_ref, count)):
        x = ref[...].astype(jnp.float32)
        xn[at : at + x.shape[0]] = (x * normalize(x) * gain_ref[0:1]).astype(jnp.bfloat16)
    proj = jnp.zeros((count, small_ref.shape[1]), jnp.float32)
    for j in range(inner // WIDE):
        cols = slice(j * WIDE, (j + 1) * WIDE)
        part = dot(xn[...], win_ref[:, cols])
        z_ref[:, cols] = dot(xn[:count], win_ref[:, inner + j * WIDE : inner + (j + 1) * WIDE])
        for s in range(seqs):
            ext_ref[s, 0:8, cols] = part[count + 8 * s : count + 8 * s + 8]
            ext_ref[s, 8:, cols] = part[s * rows : (s + 1) * rows]
            pre = conv_sum(ext_ref, s, cols, vec_ref, states, taps, rows)
            u_ref[s * rows : (s + 1) * rows, cols] = pre * sigmoid(pre)
        proj = proj + dot(u_ref[:, cols].astype(jnp.bfloat16), small_ref[cols, :])
    proj_ref[...] = proj
    low = rank_lanes(proj, rank, states)
    for j in range(inner // WIDE):
        cols = slice(j * WIDE, (j + 1) * WIDE)
        pre = dot_nt(low, small_ref[cols, :]) + vec_ref[states + taps + 1 : states + taps + 2, cols]
        dt = jnp.maximum(pre, 0.0) + jnp.log1p(jnp.exp(-jnp.abs(pre)))
        dt_ref[:, cols] = dt
        for s in range(seqs):
            dsum_ref[s, 0:1, cols] = jnp.sum(dt[s * rows : (s + 1) * rows], axis=0, keepdims=True)
    a2 = -jnp.exp(vec_ref[0:states]) * LOG2E
    blocks = inner // 128
    for s in range(seqs):
        def eight(i, hs):
            hs = list(hs)
            at = pl.multiple_of(s * rows + i * 8, 8)
            small = proj_ref[pl.ds(at, 8), :]
            bs = [column(small[j : j + 1], rank, states) for j in range(8)]
            for k in range(blocks):
                sl = slice(k * 128, (k + 1) * 128)
                d8 = dt_ref[pl.ds(at, 8), sl]
                w8 = d8 * u_ref[pl.ds(at, 8), sl]
                for j in range(8):
                    hs[k] = jnp.exp2(d8[j : j + 1] * a2[:, sl]) * hs[k] + bs[j] * w8[j : j + 1]
            return tuple(hs)
        zero = jnp.zeros((states, 128), jnp.float32)
        hs = lax.fori_loop(0, rows // 8, eight, (zero,) * blocks)
        for k in range(blocks):
            end_ref[s, :, k * 128 : (k + 1) * 128] = hs[k]


def rank_lanes(proj, rank, states):
    at = rank + 2 * states
    moved = pltpu.roll(proj, at, axis=1)
    return jnp.where(lanes(proj.shape) >= at, moved, 0.0).astype(jnp.bfloat16)


def leave_kernel(dims, capacity, room, tok_ref, cot_ref, h0_ref, dt_ref, u_ref, z_ref, proj_ref, vec_ref, out_ref,
                 gain_ref, router_ref, route_ref, slot_ref,
                 hist_ref, y_ref, hid_ref, gated_ref, moe_ref, gate_ref, rows_ref,
                 hbuf, hcur, sem, sem0):
    seqs, rows, inner, states, rank, taps = dims
    count = seqs * rows
    a2 = -jnp.exp(vec_ref[0:states]) * LOG2E
    blocks = inner // 128
    groups = rows // GROUP
    size = GROUP * states
    firsts = []
    for s in range(seqs):
        hcur[s] = h0_ref[s].astype(jnp.bfloat16)
        cp = pltpu.make_async_copy(hcur.at[s], hist_ref.at[s, pl.ds(0, states)], sem0.at[s])
        cp.start()
        firsts.append(cp)

    def out_copy(s, g, slot):
        at = pl.multiple_of(states + g * size, states)
        return pltpu.make_async_copy(hbuf.at[slot], hist_ref.at[s, pl.ds(at, size)], sem.at[slot])

    for s in range(seqs):
        def group(g, hs):
            hs = list(hs)
            slot = g % 2

            @pl.when(g >= 2)
            def _():
                out_copy(s, g - 2, slot).wait()
            for half in range(GROUP // 8):
                at = pl.multiple_of(s * rows + g * GROUP + half * 8, 8)
                small = proj_ref[pl.ds(at, 8), :]
                bs = [column(small[j : j + 1], rank, states) for j in range(8)]
                cs = [column(small[j : j + 1], rank + states, states) for j in range(8)]
                for k in range(blocks):
                    sl = slice(k * 128, (k + 1) * 128)
                    d8 = dt_ref[pl.ds(at, 8), sl]
                    w8 = d8 * u_ref[pl.ds(at, 8), sl]
                    parts = []
                    for j in range(8):
                        t = half * 8 + j
                        hs[k] = jnp.exp2(d8[j : j + 1] * a2[:, sl]) * hs[k] + bs[j] * w8[j : j + 1]
                        hbuf[slot, t * states : (t + 1) * states, sl] = hs[k].astype(jnp.bfloat16)
                        parts.append(fold(cs[j] * hs[k]))
                    y_ref[pl.ds(at, 8), sl] = row_sums(parts)
            out_copy(s, g, slot).start()
            return tuple(hs)
        hs = tuple(h0_ref[s, :, k * 128 : (k + 1) * 128] for k in range(blocks))
        lax.fori_loop(0, groups, group, hs)
        for g in (groups - 2, groups - 1):
            out_copy(s, g, g % 2).wait()
    for cp in firsts:
        cp.wait()
    hid = tok_ref[...].astype(jnp.float32)
    for j in range(inner // WIDE):
        cols = slice(j * WIDE, (j + 1) * WIDE)
        y = y_ref[:, cols] + vec_ref[states + taps + 2 : states + taps + 3, cols] * u_ref[:, cols]
        y_ref[:, cols] = y
        z = z_ref[:, cols]
        gated = (y * (z * sigmoid(z))).astype(jnp.bfloat16)
        gated_ref[:, cols] = gated
        hid = hid + dot(gated, out_ref[cols, :])
    hid_ref[...] = hid
    moe_in = (hid * normalize(hid) * gain_ref[1:2]).astype(jnp.bfloat16)
    moe_ref[...] = moe_in
    logits = dot(moe_in, router_ref[...])
    route, slot = as_column(route_ref), as_column(slot_ref)
    chosen = lanes(logits.shape) == route + room
    gate = sigmoid(jnp.sum(jnp.where(chosen, logits, 0.0), axis=1, keepdims=True))
    gate_ref[...] = gate
    kept = (slot < capacity).astype(jnp.float32)
    grad_rows = (cot_ref[...].astype(jnp.float32) * (gate * kept)).astype(jnp.bfloat16)
    total = rows_ref.shape[0]
    place = jnp.where(slot_ref[...] < capacity, route_ref[...] * capacity + slot_ref[...], -1)
    place = jnp.concatenate([place[s : s + 1] for s in range(seqs)], axis=1)
    pick = (subs((total, count)) == place).astype(jnp.bfloat16)
    width = moe_in.shape[1]
    rows_ref[:, :width] = dot(pick, moe_in).astype(jnp.bfloat16)
    rows_ref[:, width:] = dot(pick, grad_rows).astype(jnp.bfloat16)


def erf(x):
    x = jnp.clip(x, -4.0, 4.0)
    x2 = x * x
    top = (-2.72614225801306e-10, 2.77068142495902e-08, -2.10102402082508e-06, -5.69250639462346e-05,
           -7.34990630326855e-04, -2.95459980854025e-03, -1.60960333262415e-02)
    low = (-1.45660718464996e-05, -2.13374055278905e-04, -1.68282697438203e-03, -7.37332916720468e-03,
           -1.42647390514189e-02)
    p = jnp.full_like(x2, top[0])
    for c in top[1:]:
        p = p * x2 + c
    q = jnp.full_like(x2, low[0])
    for c in low[1:]:
        q = q * x2 + c
    return x * p / q


def expert_kernel(rows_ref, up_ref, down_ref, part_ref, dup_ref, ddown_ref):
    width = up_ref.shape[0]
    x, g = rows_ref[:, :width], rows_ref[:, width:]
    hidden = dot(x, up_ref[...])
    half = 0.5 * (1.0 + erf(hidden * math.sqrt(0.5)))
    act = (hidden * half).astype(jnp.bfloat16)
    slope = half + hidden * (jnp.exp(-0.5 * hidden * hidden) * (1.0 / math.sqrt(2.0 * math.pi)))
    part_ref[:, :width] = dot(act, down_ref[...]).astype(jnp.bfloat16)
    grad_hidden = (dot_nt(g, down_ref[...]) * slope).astype(jnp.bfloat16)
    part_ref[:, width:] = dot_nt(grad_hidden, up_ref[...]).astype(jnp.bfloat16)
    ddown, dup = dot_tn(act, g), dot_tn(x, grad_hidden)

    @pl.when(pl.program_id(0) == 0)
    def _():
        dup_ref[...] = dup
        ddown_ref[...] = ddown

    @pl.when(pl.program_id(0) > 0)
    def _():
        dup_ref[...] += dup
        ddown_ref[...] += ddown


def return_kernel(dims, capacity, room, ret_ref, cot_ref, hid_ref, moe_ref, gate_ref, gated_ref, y_ref, u_ref, z_ref, dt_ref,
                  proj_ref, vec_ref, out_ref, gain_ref, router_ref, route_ref, slot_ref,
                  block_ref, ghid_ref, gy_ref, gz_ref, dout_ref, drouter_ref, dskip_ref, dgain_ref, adj_ref):
    seqs, rows, inner, states, rank, taps = dims
    count = seqs * rows
    total, width = ret_ref.shape[0], hid_ref.shape[1]
    route, slot = as_column(route_ref), as_column(slot_ref)
    place = jnp.where(slot < capacity, route * capacity + slot, -1)
    pick = (lanes((count, total)) == place).astype(jnp.bfloat16)
    result = dot(pick, ret_ref[:, :width])
    hid, gate = hid_ref[...], gate_ref[...]
    block_ref[...] = (hid + gate * result).astype(jnp.bfloat16)
    cot = cot_ref[...].astype(jnp.float32)
    grad_gate = jnp.sum(cot * result, axis=1, keepdims=True)
    wide = (count, router_ref.shape[1])
    grad_logits = jnp.where(lanes(wide) == route + room, grad_gate * gate * (1.0 - gate), 0.0).astype(jnp.bfloat16)
    grad_in = dot(pick, ret_ref[:, width:]) + dot_nt(grad_logits, router_ref[...])
    drouter_ref[...] = dot_tn(moe_ref[...], grad_logits)
    r2 = normalize(hid)
    dgain_ref[...] = jnp.sum(grad_in * (hid * r2), axis=0, keepdims=True)
    scaled = grad_in * gain_ref[1:2]
    grad_hid = cot + r2 * scaled - hid * (r2 * r2 * r2) * jnp.mean(scaled * hid, axis=1, keepdims=True)
    ghid_ref[...] = grad_hid
    branch = grad_hid.astype(jnp.bfloat16)
    for j in range(inner // WIDE):
        cols = slice(j * WIDE, (j + 1) * WIDE)
        dout_ref[cols, :] = dot_tn(gated_ref[:, cols], branch).astype(jnp.bfloat16)
        grad = dot_nt(branch, out_ref[cols, :])
        z = z_ref[:, cols]
        sig = sigmoid(z)
        gy = grad * (z * sig)
        gy_ref[:, cols] = gy
        gz_ref[:, cols] = (grad * y_ref[:, cols] * (sig + z * sig * (1.0 - sig))).astype(jnp.bfloat16)
        dskip_ref[:, cols] = jnp.sum(gy * u_ref[:, cols], axis=0, keepdims=True)
    a2 = -jnp.exp(vec_ref[0:states]) * LOG2E
    blocks = inner // 128
    for s in range(seqs):
        def eight(i, ms):
            ms = list(ms)
            at = pl.multiple_of((s + 1) * rows - 8 - i * 8, 8)
            small = proj_ref[pl.ds(at, 8), :]
            cs = [column(small[j : j + 1], rank + states, states) for j in range(8)]
            for k in range(blocks):
                sl = slice(k * 128, (k + 1) * 128)
                d8, g8 = dt_ref[pl.ds(at, 8), sl], gy_ref[pl.ds(at, 8), sl]
                for j in reversed(range(8)):
                    ms[k] = jnp.exp2(d8[j : j + 1] * a2[:, sl]) * (ms[k] + cs[j] * g8[j : j + 1])
            return tuple(ms)
        zero = jnp.zeros((states, 128), jnp.float32)
        ms = lax.fori_loop(0, rows // 8, eight, (zero,) * blocks)
        for k in range(blocks):
            adj_ref[s, :, k * 128 : (k + 1) * 128] = ms[k]


def back_kernel(dims, tok_ref, halo_ref, ext_ref, hist_ref, later_ref, gy_ref, gz_ref, ghid_ref, u_ref, dt_ref,
                proj_ref, win_ref, small_ref, vec_ref, gain_ref,
                dtok_ref, dhalo_ref, din_ref, dsmall_ref, dvec_ref, dgain_ref,
                hbuf, ccol, bcol, gbsum, gcsum, adj, gdt, gu, gproj, gpad, gm, xn, gpre, sem):
    small_ref = small_ref.at[:, 0:TILE]
    seqs, rows, inner, states, rank, taps = dims
    count = seqs * rows
    groups = rows // GROUP
    size = GROUP * states
    steps = seqs * groups

    def fetch(i, slot):
        s, g = i // groups, groups - 1 - i % groups
        at = pl.multiple_of(g * size, size)
        return pltpu.make_async_copy(hist_ref.at[s, pl.ds(at, size + states)], hbuf.at[slot], sem.at[slot])

    fetch(0, 0).start()
    dvec_ref[...] = jnp.zeros_like(dvec_ref)
    strip = 512

    def group(i, carry):
        slot = i % 2
        s, g = i // groups, groups - 1 - i % groups

        @pl.when(i + 1 < steps)
        def _():
            fetch(i + 1, 1 - slot).start()

        @pl.when(g == groups - 1)
        def _():
            adj[...] = later_ref[s]
        at = pl.multiple_of(s * rows + g * GROUP, GROUP)
        small = proj_ref[pl.ds(at, GROUP), :]
        for t in range(GROUP):
            ccol[t] = column(small[t : t + 1], rank + states, states)
            bcol[t] = column(small[t : t + 1], rank, states)
            gbsum[t] = jnp.zeros((states, 128), f32)
            gcsum[t] = jnp.zeros((states, 128), f32)
        fetch(i, slot).wait()
        for c0 in range(0, inner, strip):
            sls = [slice(c0 + k, c0 + k + 128) for k in range(0, strip, 128)]
            rates = [-jnp.exp(vec_ref[0:states, sl]) for sl in sls]
            m = [adj[:, sl] for sl in sls]
            dd = [dvec_ref[0:states, sl] for sl in sls]
            for half in reversed(range(GROUP // 8)):
                a8 = pl.multiple_of(at + half * 8, 8)
                d8 = [dt_ref[pl.ds(a8, 8), sl] for sl in sls]
                g8 = [gy_ref[pl.ds(a8, 8), sl] for sl in sls]
                u8 = [u_ref[pl.ds(a8, 8), sl] for sl in sls]
                w8 = [d * u for d, u in zip(d8, u8)]
                r1, r2 = [[None] * 8 for _ in sls], [[None] * 8 for _ in sls]
                for j in reversed(range(8)):
                    t = half * 8 + j
                    gb = gc = 0.0
                    for k, sl in enumerate(sls):
                        d, gy = d8[k][j : j + 1], g8[k][j : j + 1]
                        a = m[k] + ccol[t] * gy
                        m[k] = jnp.exp2(d * (rates[k] * LOG2E)) * a
                        p = m[k] * hbuf[slot, t * states : (t + 1) * states, sl].astype(f32) * rates[k]
                        dd[k] = dd[k] + p * d
                        gb = gb + a * w8[k][j : j + 1]
                        gc = gc + gy * hbuf[slot, (t + 1) * states : (t + 2) * states, sl].astype(f32)
                        r1[k][j], r2[k][j] = fold(p), fold(a * bcol[t])
                    gbsum[t] += gb
                    gcsum[t] += gc
                for k, sl in enumerate(sls):
                    w1, w2 = row_sums(r1[k]), row_sums(r2[k])
                    gdt[pl.ds(a8, 8), sl] = w1 + u8[k] * w2
                    gu[pl.ds(a8, 8), sl] = d8[k] * w2
            for k, sl in enumerate(sls):
                adj[:, sl] = m[k]
                dvec_ref[0:states, sl] = dd[k]
        square = (states, small.shape[1])
        where, entry = lanes(square), subs(square)
        line = subs((GROUP, small.shape[1]))
        out = jnp.zeros(small.shape, f32)
        for t in range(GROUP):
            gb = jnp.broadcast_to(jnp.sum(gbsum[t], axis=1, keepdims=True), square)
            gc = jnp.broadcast_to(jnp.sum(gcsum[t], axis=1, keepdims=True), square)
            put = jnp.where(where == entry + rank, gb, jnp.where(where == entry + rank + states, gc, 0.0))
            out = jnp.where(line == t, jnp.sum(put, axis=0, keepdims=True), out)
        gproj[pl.ds(at, GROUP), :] = out
        return carry
    lax.fori_loop(0, steps, group, 0)

    low = rank_lanes(proj_ref[...], rank, states)
    at = rank + 2 * states
    row = states + taps
    grad_rank = jnp.zeros(proj_ref.shape, jnp.float32)
    for j in range(inner // WIDE):
        cols = slice(j * WIDE, (j + 1) * WIDE)
        pre = dot_nt(low, small_ref[cols, :]) + vec_ref[row + 1 : row + 2, cols]
        grad_pre = gdt[:, cols] * sigmoid(pre)
        dvec_ref[row + 1 : row + 2, cols] = jnp.sum(grad_pre, axis=0, keepdims=True)
        grad_pre = grad_pre.astype(jnp.bfloat16)
        gpre[:, cols] = grad_pre
        grad_rank = grad_rank + dot(grad_pre, small_ref[cols, :])
    where = lanes(grad_rank.shape)
    grad_rank = pltpu.roll(grad_rank, small_ref.shape[1] - at, axis=1)
    grad_proj = jnp.where(where < rank, grad_rank, jnp.where(where < at, gproj[...], 0.0)).astype(jnp.bfloat16)
    for ref, to in ((tok_ref, 0), (halo_ref, count)):
        x = ref[...].astype(jnp.float32)
        xn[to : to + x.shape[0]] = (x * normalize(x) * gain_ref[0:1]).astype(jnp.bfloat16)
    grad_normed = jnp.zeros((gm.shape[0], xn.shape[1]), jnp.float32)
    first = ext_ref.shape[1] - rows - taps + 1
    for j in range(inner // WIDE):
        cols = slice(j * WIDE, (j + 1) * WIDE)
        dsmall_ref[cols, :] = (
            dot_tn(u_ref[:, cols].astype(jnp.bfloat16), grad_proj) + dot_tn(gpre[:, cols], low)
        ).astype(jnp.bfloat16)
        grad_u = dot_nt(grad_proj, small_ref[cols, :]) + gy_ref[:, cols] * vec_ref[row + 2 : row + 3, cols] + gu[:, cols]
        taps_sum = [0.0] * taps
        bias_sum = 0.0
        heads = []
        for s in range(seqs):
            pre = conv_sum(ext_ref, s, cols, vec_ref, states, taps, rows)
            sig = sigmoid(pre)
            grad_conv = grad_u[s * rows : (s + 1) * rows] * (sig + pre * sig * (1.0 - sig))
            bias_sum = bias_sum + jnp.sum(grad_conv, axis=0, keepdims=True)
            for k in range(taps):
                taps_sum[k] = taps_sum[k] + jnp.sum(
                    grad_conv * ext_ref[s, first + k : first + k + rows, cols], axis=0, keepdims=True)
            gpad[0:8] = jnp.zeros((8, WIDE), jnp.float32)
            gpad[8 : 8 + rows] = grad_conv
            gpad[8 + rows :] = jnp.zeros((8, WIDE), jnp.float32)
            grad = 0.0
            for k in range(taps):
                grad = grad + vec_ref[states + k : states + k + 1, cols] * gpad[taps - 1 - k : taps + 7 - k + rows]
            heads.append(grad[0:8])
            gm[s * rows : (s + 1) * rows, cols] = grad[8:].astype(jnp.bfloat16)
        gm[count:, cols] = jnp.concatenate(heads).astype(jnp.bfloat16)
        dvec_ref[row : row + 1, cols] = bias_sum
        for k in range(taps):
            dvec_ref[states + k : states + k + 1, cols] = taps_sum[k]
        zcols = slice(inner + j * WIDE, inner + (j + 1) * WIDE)
        din_ref[:, cols] = dot_tn(xn[...], gm[:, cols]).astype(jnp.bfloat16)
        din_ref[:, zcols] = dot_tn(xn[:count], gz_ref[:, cols]).astype(jnp.bfloat16)
        gz = jnp.concatenate([gz_ref[:, cols], jnp.zeros((gm.shape[0] - count, WIDE), jnp.bfloat16)])
        grad_normed = grad_normed + dot_nt(gm[:, cols], win_ref[:, cols]) + dot_nt(gz, win_ref[:, zcols])
    gain_sum = 0.0
    for ref, to, base, out in ((tok_ref, 0, ghid_ref, dtok_ref), (halo_ref, count, None, dhalo_ref)):
        x = ref[...].astype(jnp.float32)
        r1 = normalize(x)
        grad = grad_normed[to : to + x.shape[0]]
        gain_sum = gain_sum + jnp.sum(grad * (x * r1), axis=0, keepdims=True)
        grad = grad * gain_ref[0:1]
        grad = r1 * grad - x * (r1 * r1 * r1) * jnp.mean(grad * x, axis=1, keepdims=True)
        out[...] = grad if base is None else grad + base[...]
    dgain_ref[...] = gain_sum


def like(*shape, dtype=f32):
    return jax.ShapeDtypeStruct(shape, dtype)


def params(mib=56):
    return pltpu.CompilerParams(vmem_limit_bytes=mib << 20)


def moe_kernel(seq, rows_ref, up_ref, down_ref, up2_ref, down2_ref,
               back_ref, land_ref, dup_ref, ddown_ref, dup2_ref, ddown2_ref,
               xbuf, part, act, ghid, hid, gact, sib_buf, own_sum,
               local_sem, disp_sem, pass_sem, recv_sem, load_sem, sib_send, sib_recv,
               final_send, final_recv, final_local):
    me = Place(4, seq)
    b, s = me.at()
    y, z, Z, c = me.y, me.z, me.Z, me.c
    cap, wide = rows_ref.shape[1], rows_ref.shape[2]
    width = wide // 2
    share = up_ref.shape[1]
    two = 2 * cap
    block = 2 * two
    sib = me.at(c=1 - c)
    greet([(None, sib)] + [(None, (b, (s + k) % seq)) for k in range(1, seq)])

    def remote(src, dst, send, recv, dev):
        return pltpu.make_async_remote_copy(
            src_ref=src, dst_ref=dst, send_sem=send, recv_sem=recv, device_id=dev, device_id_type=MESH)

    def slab(cc, ss):
        return land_ref.at[cc, pl.ds(pl.multiple_of(ss * cap, 8), cap)]

    def there(k, j):
        return ((z + k) % Z) * 2 + j

    def arrived(cc, ss):
        remote(slab(cc, ss), slab(cc, ss), disp_sem.at[0], recv_sem.at[cc, ss], sib).wait_recv()

    def hand(ss):
        return remote(slab(c, ss), slab(c, ss), pass_sem.at[ss], recv_sem.at[c, ss], sib)

    def load(k, cc):
        zz = (z + k) % Z
        return pltpu.make_async_copy(
            land_ref.at[cc, pl.ds(pl.multiple_of(zz * two, 8), two)],
            xbuf.at[k, pl.ds(pl.multiple_of(cc * two, 16), two)], load_sem.at[k, cc])

    def dispatch(k, j):
        to = ((z + Z - k) % Z) * 2 + j
        return remote(rows_ref.at[to], slab(c, s), disp_sem.at[2 * k + j], recv_sem.at[c, s], (b, to))

    dispatch(0, 1 - y).start()
    own = remote(rows_ref.at[s], slab(c, s), pass_sem.at[s], recv_sem.at[c, s], sib)
    own.start()
    local = pltpu.make_async_copy(rows_ref.at[s], slab(c, s), local_sem)
    local.start()
    for j in range(2):
        dispatch(1, j).start()

    ups, downs = (up_ref, up2_ref), (down_ref, down2_ref)

    def compute(k):
        for i in range(2):
            for n in range(0, share, WIDE):
                to = slice(i * share + n, i * share + n + WIDE)
                hid[:, to] = dot(xbuf[k, :, :width], ups[i][:, n : n + WIDE])
                gact[:, to] = dot_nt(xbuf[k, :, width:], downs[i][n : n + WIDE, :])

        def sixteen(r, carry):
            at = pl.ds(pl.multiple_of(r * 16, 16), 16)
            to = pl.ds(pl.multiple_of(k * block + r * 16, 16), 16)
            h = hid[at, :]
            half = 0.5 * (1.0 + erf(h * math.sqrt(0.5)))
            act[to, :] = (h * half).astype(bf16)
            slope = half + h * (jnp.exp(-0.5 * h * h) * (1.0 / math.sqrt(2.0 * math.pi)))
            ghid[to, :] = (gact[at, :] * slope).astype(bf16)
            return carry
        lax.fori_loop(0, block // 16, sixteen, 0)
        mine = pl.ds(pl.multiple_of(k * block, 16), block)
        for n in range(0, width, WIDE):
            cols = slice(n, n + WIDE)
            part[k, :, cols] = (
                dot(act[mine, :share], down_ref[:, cols]) + dot(act[mine, share:], down2_ref[:, cols])
            ).astype(bf16)
            part[k, :, width + n : width + n + WIDE] = (
                dot_nt(ghid[mine, :share], up_ref[cols, :]) + dot_nt(ghid[mine, share:], up2_ref[cols, :])
            ).astype(bf16)

    def of_core(k, cc):
        return part.at[k, pl.ds(pl.multiple_of(cc * two, 16), two)]

    def to_sib(k):
        return remote(of_core(k, 1 - c), sib_buf.at[k], sib_send.at[k], sib_recv.at[k], sib)

    def to_home(k, j):
        return remote(own_sum.at[k, j], back_ref.at[s], final_send.at[k, j], final_recv.at[s], (b, there(k, j)))

    def keep_home():
        return pltpu.make_async_copy(own_sum.at[0, y], back_ref.at[s], final_local)

    def own_stage(k):
        @pl.when(k == 0)
        def _():
            arrived(c, z * 2 + 1 - y)
            hand(z * 2 + 1 - y).start()
            local.wait()

        @pl.when(k > 0)
        def _():
            for j in range(2):
                arrived(c, there(k, j))
                hand(there(k, j)).start()

        @pl.when(k < Z - 2)
        def _():
            for j in range(2):
                dispatch(k + 2, j).start()
        load(k, c).start()

    def compute_stage(k):
        for j in range(2):
            arrived(1 - c, there(k, j))
        load(k, 1 - c).start()
        for cc in range(2):
            load(k, cc).wait()
        compute(k)
        to_sib(k).start()

    def home_stage(k):
        to_sib(k).wait_recv()
        total = of_core(k, c)[...].astype(f32) + sib_buf[k].astype(f32)
        for j in range(2):
            own_sum[k, j] = total[j * cap : (j + 1) * cap].astype(bf16)

        @pl.when(k > 0)
        def _():
            for j in range(2):
                to_home(k, j).start()

        @pl.when(k == 0)
        def _():
            keep_home().start()
            to_home(0, 1 - y).start()

    everything = (Z * block, width)
    stages = ((own_stage, 0), (home_stage, 2), (compute_stage, 1))

    def step(t, carry):
        for stage, lag in stages:
            k = t - lag
            pl.when(jnp.logical_and(k >= 0, k < Z))(functools.partial(stage, k))
        return carry
    lax.fori_loop(0, Z + 2, step, 0)
    for i, (dup, ddown) in enumerate(((dup2_ref, ddown2_ref), (dup_ref, ddown_ref))):
        for n in range(0, share, WIDE):
            at = (1 - i) * share + n
            x, g = xbuf[:, :, :width].reshape(everything), xbuf[:, :, width:].reshape(everything)
            ddown[n : n + WIDE, :] = dot_tn(act[:, at : at + WIDE], g).astype(ddown.dtype)
            dup[:, n : n + WIDE] = dot_tn(x, ghid[:, at : at + WIDE]).astype(dup.dtype)

    for k in range(1, seq):
        e = (s + k) % seq
        remote(back_ref.at[e], back_ref.at[e], disp_sem.at[0], final_recv.at[e], sib).wait_recv()
    keep_home().wait()
    dispatch(0, 1 - y).wait_send()
    own.wait_send()
    hand(z * 2 + 1 - y).wait_send()
    to_home(0, 1 - y).wait_send()

    def settle(k, carry):
        to_sib(k).wait_send()

        @pl.when(k > 0)
        def _():
            for j in range(2):
                dispatch(k, j).wait_send()
                to_home(k, j).wait_send()
                hand(there(k, j)).wait_send()
        return carry
    lax.fori_loop(0, Z, settle, 0)


def cross(batch, *arrays):
    return [lax.ppermute(a, "batch", [(i, (i + 2) % batch) for i in range(batch)]) for a in arrays]


def moe_rows(batch, seq, sent, up, down, up2, down2):
    width, hidden_share = up.shape
    capacity, wide = sent.shape[1:]
    block = seq * capacity
    if tuned(batch, seq):
        Z, block = seq // 2, 4 * capacity
        dma = pltpu.SemaphoreType.DMA
        out = pl.pallas_call(
            functools.partial(moe_kernel, seq),
            out_shape=[
                like(seq, capacity, wide, dtype=bf16),
                like(2, seq * capacity, wide, dtype=bf16),
                like(width, hidden_share),
                like(hidden_share, width),
                like(width, hidden_share, dtype=bf16),
                like(hidden_share, width, dtype=bf16),
            ],
            in_specs=[HBM] + [VM] * 4,
            out_specs=[HBM, HBM] + [VM] * 4,
            scratch_shapes=[
                pltpu.VMEM((Z, block, wide), bf16),
                pltpu.VMEM((Z, block, wide), bf16),
                pltpu.VMEM((Z * block, 2 * hidden_share), bf16),
                pltpu.VMEM((Z * block, 2 * hidden_share), bf16),
                pltpu.VMEM((block, 2 * hidden_share), f32),
                pltpu.VMEM((block, 2 * hidden_share), f32),
                pltpu.VMEM((Z, 2 * capacity, wide), bf16),
                pltpu.VMEM((Z, 2, capacity, wide), bf16),
                dma,
                dma((2 * Z,)),
                dma((seq,)),
                dma((2, seq)),
                dma((Z, 2)),
                dma((Z,)),
                dma((Z,)),
                dma((Z, 2)),
                dma((seq,)),
                dma,
            ],
            compiler_params=pltpu.CompilerParams(
                collective_id=2, has_side_effects=True, vmem_limit_bytes=56 << 20),
            name="experts",
        )(sent, up, down, up2, down2)
        back, _, d_up, d_down, d_up2, d_down2 = out
        d_up2, d_down2 = cross(batch, d_up2, d_down2)
        return back, d_up, d_down, d_up2, d_down2
    mine = lax.all_to_all(sent, "seq", split_axis=0, concat_axis=0, tiled=True)
    rows = lax.all_gather(mine, "batch", axis=0).reshape(batch * block, wide)
    part, d_up, d_down = pl.pallas_call(
        expert_kernel,
        out_shape=[
            like(batch * block, wide, dtype=bf16),
            like(width, hidden_share),
            like(hidden_share, width),
        ],
        grid=(batch,),
        in_specs=[
            pl.BlockSpec((block, wide), lambda i: (i, 0)),
            pl.BlockSpec((width, hidden_share), lambda i: (0, 0)),
            pl.BlockSpec((hidden_share, width), lambda i: (0, 0)),
        ],
        out_specs=[
            pl.BlockSpec((block, wide), lambda i: (i, 0)),
            pl.BlockSpec((width, hidden_share), lambda i: (0, 0)),
            pl.BlockSpec((hidden_share, width), lambda i: (0, 0)),
        ],
        compiler_params=params(),
        name="experts",
    )(rows, up, down)
    part = part.reshape((batch,) + sent.shape)
    mine = lax.psum_scatter(part, "batch", scatter_dimension=0, tiled=False)
    return lax.all_to_all(mine, "seq", split_axis=0, concat_axis=0, tiled=True), d_up, d_down, None, None


def body(
    tokens,
    in_proj,
    conv_weight,
    conv_bias,
    state_proj,
    step_proj,
    step_bias,
    decay_log,
    skip_gain,
    out_proj,
    norm_gain,
    moe_gain,
    router_proj,
    expert_up,
    expert_down,
    routes,
    slot_index,
    cotangent,
):
    batch, seq = lax.axis_size("batch"), lax.axis_size("seq")
    both = ("batch", "seq")
    seqs, rows, width = tokens.shape
    count = seqs * rows
    devices = batch * seq
    taps, share = conv_weight.shape
    inner = share * devices
    states, rank = decay_log.shape[0], step_proj.shape[0]
    low_share = norm_gain.shape[0]
    experts = router_proj.shape[1]
    capacity = max(2, 5 * count // (4 * experts))
    dims = (seqs, rows, inner, states, rank, taps)
    tile = 128

    lines = (decay_log, conv_weight, conv_bias[None], step_bias[None], skip_gain[None])
    used = sum(a.shape[0] for a in lines)
    room = -(-used // 8) * 8
    fast = tuned(batch, seq)
    if fast:
        in_full, out_full, tail_full, halo = gather_all(
            batch, seq, room, in_proj, out_proj, tokens, state_proj, step_proj, router_proj, lines,
            (norm_gain[None], moe_gain[None]))
        halo = halo.reshape(seqs * 8, width)
    else:
        features = jnp.concatenate([router_proj, norm_gain[:, None], moe_gain[:, None]], axis=1)
        tail = jnp.concatenate(
            [
                state_proj,
                step_proj.T,
                jnp.pad(jnp.concatenate(lines), ((0, room - used), (0, 0))).T,
                jnp.pad(features, ((0, share - low_share), (0, tile - room - features.shape[1]))),
            ],
            axis=1,
        )
        halo = lax.ppermute(tokens[:, rows - taps + 1 :], "seq", [(i, i + 1) for i in range(seq - 1)])
        halo = jnp.pad(halo, ((0, 0), (8 - taps + 1, 0), (0, 0))).reshape(seqs * 8, width)
        in_full, out_full, tail_full = (
            lax.all_gather(a, both, axis=0, tiled=True) for a in (in_proj, out_proj, tail)
        )
    up, down, tail_full = lax.optimization_barrier((expert_up[0], expert_down[0], tail_full))
    up2, down2 = cross(batch, up, down) if fast else (None, None)
    tok, cot = tokens.reshape(count, width), cotangent.reshape(count, width)
    outs = [
        like(seqs, rows + 8, inner),
        like(count, inner),
        like(count, inner),
        like(count, inner),
        like(count, tile),
        like(seqs, states, inner),
        like(seqs, 1, inner),
    ]
    scratch = [pltpu.VMEM((count + seqs * 8, width), bf16)]
    if fast:
        *outs, vec, gain, router = pl.pallas_call(
            partial(enter_packed, dims, share, low_share, experts),
            out_shape=outs + [like(room, inner), like(8, width), like(width, tile, dtype=bf16)],
            in_specs=[VM] * 4,
            out_specs=[VM] * 10,
            scratch_shapes=scratch,
            compiler_params=params(),
            name="enter",
        )(tok, halo, in_full, tail_full)
    else:
        vec = tail_full[:, tile : tile + room].T.astype(f32)
        router = tail_full[:, tile:].reshape(devices, share, tile)[:, :low_share].reshape(width, tile)
        gain = router[:, room + experts : room + experts + 2].T.astype(f32)
        outs = pl.pallas_call(
            partial(enter_kernel, dims),
            out_shape=outs,
            in_specs=[VM] * 6,
            out_specs=[VM] * 7,
            scratch_shapes=scratch,
            compiler_params=params(),
            name="enter",
        )(tok, halo, in_full, tail_full[:, :tile], vec, gain)
    ext, z, u, dt, proj, end, dsum = outs
    before = relay_states(batch, seq, True, states, dsum, vec, end)
    size = GROUP * states
    total = experts * capacity
    hist, y, hid, gated, moe_in, gate, sent = pl.pallas_call(
        partial(leave_kernel, dims, capacity, room),
        out_shape=[
            like(seqs, (rows + 1) * states, inner, dtype=bf16),
            like(count, inner),
            like(count, width),
            like(count, inner, dtype=bf16),
            like(count, width, dtype=bf16),
            like(count, 1),
            like(total, 2 * width, dtype=bf16),
        ],
        in_specs=[VM] * 13,
        out_specs=[HBM] + [VM] * 6,
        scratch_shapes=[
            pltpu.VMEM((2, size, inner), bf16),
            pltpu.VMEM((seqs, states, inner), bf16),
            pltpu.SemaphoreType.DMA((2,)),
            pltpu.SemaphoreType.DMA((seqs,)),
        ],
        compiler_params=params(),
        name="leave",
    )(tok, cot, before, dt, u, z, proj, vec, out_full, gain, router, routes, slot_index)

    back, d_up, d_down, d_up2, d_down2 = moe_rows(
        batch, seq, sent.reshape(experts, capacity, 2 * width), up, down, up2, down2)
    back = back.reshape(total, 2 * width)

    block_out, ghid, gy, gz, d_out, d_router, d_skip, d_moe, adj = pl.pallas_call(
        partial(return_kernel, dims, capacity, room),
        out_shape=[
            like(count, width, dtype=bf16),
            like(count, width),
            like(count, inner),
            like(count, inner, dtype=bf16),
            like(inner, width, dtype=bf16),
            like(width, tile),
            like(1, inner),
            like(1, width),
            like(seqs, states, inner),
        ],
        in_specs=[VM] * 17,
        out_specs=[VM] * 9,
        compiler_params=params(),
        name="back_experts",
    )(back, cot, hid, moe_in, gate, gated, y, u, z, dt, proj, vec, out_full, gain, router, routes, slot_index)
    later = relay_states(batch, seq, False, states, dsum, vec, adj)
    d_tok, d_halo, d_in, d_small, d_vec, d_norm = pl.pallas_call(
        partial(back_kernel, dims),
        out_shape=[
            like(count, width),
            like(seqs * 8, width),
            like(width, 2 * inner, dtype=bf16),
            like(inner, tile, dtype=bf16),
            like(room, inner),
            like(1, width),
        ],
        in_specs=[VM] * 3 + [HBM] + [VM] * 11,
        out_specs=[VM] * 6,
        scratch_shapes=[
            pltpu.VMEM((2, size + states, inner), bf16),
            pltpu.VMEM((GROUP, states, tile), f32),
            pltpu.VMEM((GROUP, states, tile), f32),
            pltpu.VMEM((GROUP, states, tile), f32),
            pltpu.VMEM((GROUP, states, tile), f32),
            pltpu.VMEM((states, inner), f32),
            pltpu.VMEM((count, inner), f32),
            pltpu.VMEM((count, inner), f32),
            pltpu.VMEM((count, tile), f32),
            pltpu.VMEM((rows + 16, WIDE), f32),
            pltpu.VMEM((count + seqs * 8, inner), bf16),
            pltpu.VMEM((count + seqs * 8, width), bf16),
            pltpu.VMEM((count, inner), bf16),
            pltpu.SemaphoreType.DMA((2,)),
        ],
        compiler_params=params(),
        name="back_mixer",
    )(tok, halo, ext, hist, later, gy, gz, ghid, u, dt, proj, in_full, tail_full, vec, gain)

    skip_row = states + taps + 2
    if fast:
        s_in, s_out, s_tail, from_next = reduce_all(
            batch, seq, low_share, experts, skip_row, d_in, d_out, d_small, d_vec, d_skip, d_router, d_norm, d_moe,
            d_halo)
        steps = 4
        slab = lambda a: pl.BlockSpec((a.shape[0] // steps, a.shape[1]), lambda i: (i, 0))
        whole = lambda *shape: pl.BlockSpec(shape, lambda i: (0,) * len(shape))
        edge = pl.BlockSpec((seqs, 8, width), lambda i: (0, rows // 8 - 1, 0))
        shapes = [
            s_in.shape, (taps, share), (1, share), (share, rank + 2 * states), (rank, share), (1, share),
            (states, share), (1, share), s_out.shape, (1, low_share), (1, low_share), (low_share, experts),
        ]
        d_tok, *sums, d_up, d_down = pl.pallas_call(
            partial(finish_kernel, dims, low_share, experts),
            out_shape=[like(*tokens.shape)] + [like(*a) for a in shapes] + [like(*d_up.shape), like(*d_down.shape)],
            grid=(steps,),
            in_specs=[whole(*s_in.shape), whole(*s_out.shape), whole(*s_tail.shape), whole(seqs, 8, width), edge]
            + [slab(a) for a in (d_up, d_up2, d_down, d_down2)],
            out_specs=[edge] + [whole(*a) for a in shapes] + [slab(d_up), slab(d_down)],
            input_output_aliases={4: 0},
            compiler_params=params(),
            name="finish",
        )(s_in, s_out, s_tail, from_next.reshape(seqs, 8, width), d_tok.reshape(tokens.shape), d_up, d_up2, d_down, d_down2)
        for i in (2, 5, 7, 9, 10):
            sums[i] = sums[i][0]
        return (block_out.reshape(tokens.shape), d_tok, *sums, d_up[None], d_down[None])
    d_model = d_router.at[:, room + experts : room + experts + 2].set(jnp.concatenate([d_norm, d_moe]).T)
    d_model = jnp.pad(
        d_model.reshape(devices, low_share, tile)[:, :, room:], ((0, 0), (0, share - low_share), (0, 0))
    ).reshape(inner, tile - room)
    d_vec = d_vec.at[skip_row].set(d_skip[0])
    d_tail = jnp.concatenate([d_small, d_vec.T.astype(bf16), d_model.astype(bf16)], axis=1)
    s_in, s_out, s_tail = (
        lax.psum_scatter(a.astype(f32), both, scatter_dimension=0, tiled=True) for a in (d_in, d_out, d_tail)
    )
    from_next = lax.ppermute(
        d_halo.reshape(seqs, 8, width)[:, 8 - taps + 1 :], "seq", [(i + 1, i) for i in range(seq - 1)]
    )
    d_tok = d_tok.reshape(tokens.shape).at[:, rows - taps + 1 :].add(from_next)
    s_vec = s_tail[:, tile : tile + room].T
    s_model = s_tail[:low_share, tile + room :]
    return (
        block_out.reshape(tokens.shape),
        d_tok,
        s_in,
        s_vec[states : states + taps],
        s_vec[states + taps],
        s_tail[:, : rank + 2 * states],
        s_tail[:, rank + 2 * states : tile].T,
        s_vec[states + taps + 1],
        s_vec[:states],
        s_vec[states + taps + 2],
        s_out,
        s_model[:, experts],
        s_model[:, experts + 1],
        s_model[:, :experts],
        d_up[None],
        d_down[None],
    )


def solution(mesh):
    in_specs = (
        P("batch", "seq", None),
        P(("batch", "seq"), None),
        P(None, ("batch", "seq")),
        P(("batch", "seq")),
        P(("batch", "seq"), None),
        P(None, ("batch", "seq")),
        P(("batch", "seq")),
        P(None, ("batch", "seq")),
        P(("batch", "seq")),
        P(("batch", "seq"), None),
        P(("batch", "seq")),
        P(("batch", "seq")),
        P(("batch", "seq"), None),
        P("seq", None, "batch"),
        P("seq", "batch", None),
        P("batch", "seq"),
        P("batch", "seq"),
        P("batch", "seq", None),
    )
    out_specs = (
        P("batch", "seq", None),
        P("batch", "seq", None),
        P(("batch", "seq"), None),
        P(None, ("batch", "seq")),
        P(("batch", "seq")),
        P(("batch", "seq"), None),
        P(None, ("batch", "seq")),
        P(("batch", "seq")),
        P(None, ("batch", "seq")),
        P(("batch", "seq")),
        P(("batch", "seq"), None),
        P(("batch", "seq")),
        P(("batch", "seq")),
        P(("batch", "seq"), None),
        P("seq", None, "batch"),
        P("seq", "batch", None),
    )
    return jax.shard_map(body, mesh=mesh, in_specs=in_specs, out_specs=out_specs, check_vma=False)
```

profile of v0, /device:TPU:0, one launch (start us, length us, event | category | flops | bytes accessed | tf_op | source)
XLA Modules:
  0.0 312.6 jit_solution(17220053819019754741)
XLA Ops:
  0.6 1.3 copy.35.refs_5_
  2.0 43.6 %gather_weights.1 = (bf16[768,3072]{1,0:T(8,128)(2,1)}, bf16[1536,768]{1,0:T(8,128)(2,1)}, bf16[1536,256]{1,0:T(8,128)(2,1)}, bf16[2,8,768]{2,1,0:T(8,128)(2,1)}) custom-call(bf16[24,3072]{1,0:T(8,128)(2,1)} %refs_0_.1, bf16[48,768]{1,0:T(8,128)(2,1)} %refs_1_.1, bf16[2,128,768]{2,1,0:T(8,128)(2,1)} %refs_2_.1, bf16[48,80]{1,0:T(8,128)(2,1)} %refs_3_.1, ...), custom_call_target="tpu_custom_call" | custom-call | tf_op jit(solution)/shard_map/gather_weights/pallas_call | solution.py:230
  45.6 1.2 collective-permute-start
  46.8 0.9 collective-permute-start.1
  47.7 16.1 %enter.1 = (f32[2,136,1536]{2,1,0:T(8,128)}, f32[256,1536]{1,0:T(8,128)}, f32[256,1536]{1,0:T(8,128)}, f32[256,1536]{1,0:T(8,128)}, f32[256,128]{1,0:T(8,128)}, ...) custom-call(bf16[256,768]{1,0:T(8,128)(2,1)} %bitcast.22, ...), custom_call_target="tpu_custom_call" | custom-call | tf_op jit(solution)/shard_map/enter/pallas_call | solution.py:1466
  63.8 8.8 %relay_forward.1.h0_ref = f32[2,16,1536]{2,1,0:T(8,128)} custom-call(f32[2,1,1536]{2,1,0:T(1,128)} %get-tuple-element.83.dsum_ref, f32[24,1536]{1,0:T(8,128)} %get-tuple-element.84.vec_ref, f32[2,16,1536]{2,1,0:T(8,128)} %get-tuple-element.85.end_ref), custom_call_target="tpu_custom_call" | custom-call | tf_op jit(solution)/shard_map/relay_forward/pallas_call | solution.py:645
  72.5 19.7 %leave.1 = (bf16[2,2064,1536]{2,1,0:T(8,128)(2,1)}, f32[256,1536]{1,0:T(8,128)}, f32[256,768]{1,0:T(8,128)}, bf16[256,1536]{1,0:T(8,128)(2,1)}, bf16[256,768]{1,...) custom-call(bf16[256,768]{1,0:T(8,128)(2,1)} %bitcast.23, bf16[256,768]{1,0:T(8,128)(2,1)} %bitcast.25, ...), custom_call_target="tpu_custom_call" | custom-call | tf_op jit(solution)/shard_map/leave/pallas_call | solution.py:1492
  92.2 0.0 collective-permute-done.up2_ref
  92.2 0.0 copy-start.2
  92.2 7.4 %collective-permute-done.1.down2_ref = bf16[768,768]{1,0:T(8,128)(2,1)S(1)} collective-permute-done((bf16[768,768]{1,0:T(8,128)(2,1)}, bf16[768,768]{1,0:T(8,128)(2,1)S(1)}, u32[]{:S(2)}, u32[]{:S(2)}) %collective-permute-start.1) | collective-permute-done | bytes 1179680 | tf_op jit(solution)/shard_map/ppermute | solution.py:1316
  99.6 0.0 copy-start.3
  99.6 0.0 copy-done.2
  99.6 1.0 copy-done.3
  100.6 54.0 %experts.1 = (bf16[8,40,1536]{2,1,0:T(8,128)(2,1)}, bf16[2,320,1536]{2,1,0:T(8,128)(2,1)}, f32[768,768]{1,0:T(8,128)}, f32[768,768]{1,0:T(8,128)}, bf16[768,768]{1,0:T(8,128)(2,1)}, /*index=5*/bf16[768,768]{1,0:T(8,128)(2,1)}) custom-call(bf16[8,40,1536]{2,1,0:T(8,128)(2,1)} %bitcast.32, bf16[768,768]{1,0:T(8,128)(2,1)} %bitcast.28, ...), custom_call_target="tpu_custom_call" | custom-call | tf_op jit(solution)/shard_map/experts/pallas_call | solution.py:1326
  154.7 0.3 collective-permute-start.2
  155.0 1.8 collective-permute-start.3
  156.8 16.7 %back_experts.1 = (bf16[256,768]{1,0:T(8,128)(2,1)}, f32[256,768]{1,0:T(8,128)}, f32[256,1536]{1,0:T(8,128)}, bf16[256,1536]{1,0:T(8,128)(2,1)}, bf16[1536,768]{...) custom-call(bf16[320,1536]{1,0:T(8,128)(2,1)} %bitcast.31, ...), custom_call_target="tpu_custom_call" | custom-call | tf_op jit(solution)/shard_map/back_experts/pallas_call | solution.py:1519
  173.5 20.7 %relay_backward.1.later_ref = f32[2,16,1536]{2,1,0:T(8,128)} custom-call(f32[2,1,1536]{2,1,0:T(1,128)} %get-tuple-element.83.dsum_ref, f32[24,1536]{1,0:T(8,128)} %get-tuple-element.84.vec_ref, f32[2,16,1536]{2,1,0:T(8,128)} %get-tuple-element.105.end_ref), custom_call_target="tpu_custom_call" | custom-call | tf_op jit(solution)/shard_map/relay_backward/pallas_call | solution.py:645
  194.2 41.6 %back_mixer.1 = (f32[256,768]{1,0:T(8,128)}, f32[16,768]{1,0:T(8,128)}, bf16[768,3072]{1,0:T(8,128)(2,1)}, bf16[1536,128]{1,0:T(8,128)(2,1)}, f32[24,1536]{1,0:T(8,128)}, /*index=5*/f32[1,768]{1,0:T(1,128)}) custom-call(bf16[256,768]{1,0:T(8,128)(2,1)} %bitcast.24, bf16[16,768]{1,0:T(8,128)(2,1)} %bitcast.35, f32[2,136,1536]{2,1,0:T(8,128)} %get-tuple-element.103.ext_ref, ...), custom_call_target="tpu_custom_call" | custom-call | tf_op jit(solution)/shard_map/back_mixer/pallas_call | solution.py:1538
  235.8 67.5 %reduce_grads.1 = (f32[24,3072]{1,0:T(8,128)}, f32[48,768]{1,0:T(8,128)}, f32[48,256]{1,0:T(8,128)}, f32[16,768]{1,0:T(8,128)}) custom-call(bf16[768,3072]{1,0:T(8,128)(2,1)} %get-tuple-element.109.refs_0_, bf16[1536,768]{1,0:T(8,128)(2,1)} %get-tuple-element.110.refs_1_, bf16[1536,128]{1,0:T(8,128)(2,1)} %get-tuple-element.111.refs_2_, ...), custom_call_target="tpu_custom_call" | custom-call | tf_op jit(solution)/shard_map/reduce_grads/pallas_call | solution.py:459
  303.3 0.0 collective-permute-done.2.up2_ref
  303.4 0.0 copy-start
  303.4 0.0 collective-permute-done.3.down2_ref
  303.4 0.0 copy-start.1
  303.4 1.0 copy-done
  304.4 0.4 copy-done.1
  304.8 6.4 %finish.1 = (f32[2,128,768]{2,1,0:T(8,128)}, f32[24,3072]{1,0:T(8,128)}, f32[4,48]{1,0:T(4,128)}, f32[1,48]{1,0:T(1,128)}, f32[48,80]{1,0:T(8,128)}, /*index=5*/...) custom-call(f32[24,3072]{1,0:T(8,128)} %get-tuple-element.118.in_ref, ...), custom_call_target="tpu_custom_call", output_to_operand_aliasing={{0}: (4, {})} | custom-call | tf_op jit(solution)/shard_map/finish/pallas_call | solution.py:1583
  311.2 1.4 copy.36
Async XLA Ops:
  45.6 46.6 %collective-permute-start = (bf16[768,768]{1,0:T(8,128)(2,1)}, bf16[768,768]{1,0:T(8,128)(2,1)S(1)}, u32[]{:S(2)}, u32[]{:S(2)}) collective-permute-start(bf16[768,768]{1,0:T(8,128)(2,1)} %bitcast.27), channel_id=1, source_target_pairs={{0,16},{8,24},{16,0},{24,8},{1,17},{9,25},{17,1},{25,9},{2,18},{10... | collective-permute-start | bytes 3538952 | tf_op jit(solution)/shard_map/ppermute | solution.py:1316
  46.8 52.8 %collective-permute-start.1 = (bf16[768,768]{1,0:T(8,128)(2,1)}, bf16[768,768]{1,0:T(8,128)(2,1)S(1)}, u32[]{:S(2)}, u32[]{:S(2)}) collective-permute-start(bf16[768,768]{1,0:T(8,128)(2,1)} %bitcast.29), channel_id=1, source_target_pairs={{0,16},{8,24},{16,0},{24,8},{1,17},{9,25},{17,1},{25,9},{2,18},{10... | collective-permute-start | bytes 3538952 | tf_op jit(solution)/shard_map/ppermute | solution.py:1316
  92.2 7.4 %copy-start.2 = (bf16[768,768]{1,0:T(8,128)(2,1)}, bf16[768,768]{1,0:T(8,128)(2,1)S(1)}, u32[]{:S(2)}) copy-start(bf16[768,768]{1,0:T(8,128)(2,1)S(1)} %collective-permute-done.up2_ref) | copy-start | bytes 3538948
  99.6 1.0 copy-start.3
  154.7 148.7 %collective-permute-start.2 = (bf16[768,768]{1,0:T(8,128)(2,1)}, bf16[768,768]{1,0:T(8,128)(2,1)S(1)}, u32[]{:S(2)}, u32[]{:S(2)}) collective-permute-start(bf16[768,768]{1,0:T(8,128)(2,1)} %get-tuple-element.124), channel_id=1, source_target_pairs={{0,16},{8,24},{16,0},{24,8},{1,17},{9,25},{17,1},{25,9},{2,18},{10... | collective-permute-start | bytes 3538952 | tf_op jit(solution)/shard_map/ppermute | solution.py:1316
  155.0 148.3 %collective-permute-start.3 = (bf16[768,768]{1,0:T(8,128)(2,1)}, bf16[768,768]{1,0:T(8,128)(2,1)S(1)}, u32[]{:S(2)}, u32[]{:S(2)}) collective-permute-start(bf16[768,768]{1,0:T(8,128)(2,1)} %get-tuple-element.126), channel_id=1, source_target_pairs={{0,16},{8,24},{16,0},{24,8},{1,17},{9,25},{17,1},{25,9},{2,18},{10... | collective-permute-start | bytes 3538952 | tf_op jit(solution)/shard_map/ppermute | solution.py:1316
  303.4 1.0 copy-start
  303.4 1.4 copy-start.1
where the time goes:
time: 314 us; the launch traced here: 313 us
  Pallas kernels  295 us (94%)
  waiting for transfers between devices  7.39 us (2%)
  local copies, waits for them, and re-layouts  5.12 us (2%)
  starting transfers between devices  4.18 us (1%)
    pallas_call x1, Pallas kernels, reduce_all(): pl.pallas_call(functools.partial(reduce_kernel, batch, seq, low_share, ex...  67.5 us
    pallas_call x1, Pallas kernels, moe_rows(): pl.pallas_call(functools.partial(moe_kernel, seq), out_shape=[like(seq, c...  54 us
    pallas_call x1, Pallas kernels, gather_all(): pl.pallas_call(functools.partial(gather_kernel, batch, seq), out_shape=[j...  43.6 us
    pallas_call x1, Pallas kernels, body(): pl.pallas_call(partial(back_kernel, dims), out_shape=[like(count, width),...  41.6 us
    pallas_call x2, Pallas kernels, relay_states(): pl.pallas_call(functools.partial(relay_kernel, seq, forward, states), out...  29.5 us
    pallas_call x1, Pallas kernels, body(): pl.pallas_call(partial(leave_kernel, dims, capacity, room), out_shape=[li...  19.7 us
    pallas_call x1, Pallas kernels, body(): pl.pallas_call(partial(return_kernel, dims, capacity, room), out_shape=[l...  16.7 us
    pallas_call x1, Pallas kernels, body(): pl.pallas_call(partial(enter_packed, dims, share, low_share, experts), ou...  16.1 us
  transfers between devices with their start and end apart: 4, of which 1 were waited for; matrix products, arithmetic and copies ran while one was open for 0% of the time, Pallas kernels for 61%

commit v1 on v0

--- a/solution.py
+++ b/solution.py
@@ -144,7 +144,7 @@
     pl.when(has_after)(halo.start)
     pl.when(jnp.logical_not(has_before))(blank.start)
 
-    share, low_share, experts = state_ref.shape[0], router_ref.shape[0], router_ref.shape[1]
+    share, low_share, experts = state_ref.shape[0], router_ref.shape[1], router_ref.shape[0]
     rank, room, wide = step_ref.shape[0], vecs.shape[0], tail.shape[1]
     vecs[...] = jnp.zeros_like(vecs)
     at = 0
@@ -159,7 +159,7 @@
         + dot_tn(step_ref[...], spot(rank, TILE - rank, wide))
         + dot_tn(vecs[...].astype(bf16), spot(room, TILE, wide))
     )
-    by_feature = dot(router_ref[...], spot(experts, TILE + room, wide)) + dot_tn(
+    by_feature = dot_tn(router_ref[...], spot(experts, TILE + room, wide)) + dot_tn(
         feats[...].astype(bf16), spot(feats.shape[0], TILE + room + experts, wide))
     by_feature = jnp.concatenate([by_feature, jnp.zeros((share - low_share, wide), f32)])
     tail[...] = (by_channel + by_feature).astype(bf16)
@@ -237,7 +237,7 @@
         scratch_shapes=[
             pltpu.VMEM((share, wide), bf16),
             pltpu.VMEM((room, share), f32),
-            pltpu.VMEM((8, router.shape[0]), f32),
+            pltpu.VMEM((8, router.shape[1]), f32),
             pltpu.VMEM(edge, bf16),
             pltpu.SemaphoreType.DMA((3,)),
             pltpu.SemaphoreType.DMA((n_sends(seq // 2), 3)),
@@ -468,16 +468,21 @@
     )(d_in, d_out, *rest)
 
 
-def finish_kernel(dims, low_share, experts, in_ref, out_ref, tail_ref, halo_ref, tok_ref, up_ref, up2_ref, down_ref,
-                  down2_ref, tok_out, din, dconv, dbias, dstate, dstep, dstep_bias, ddecay, dskip, dout, dnorm, dmoe,
+def finish_kernel(dims, low_share, experts, in_ref, out_ref, tail_ref, halo_ref, tok_ref, block_ref, up_ref, up2_ref,
+                  down_ref, down2_ref, block_out, tok_out, din, dconv, dbias, dstate, dstep, dstep_bias, ddecay, dskip, dout, dnorm, dmoe,
                   drouter, dup, ddown):
     seqs, rows, inner, states, rank, taps = dims
     dup[...] = up_ref[...] + up2_ref[...].astype(f32)
     ddown[...] = down_ref[...] + down2_ref[...].astype(f32)
+    block_out[...] = block_ref[...]
+    tok_out[...] = tok_ref[...]
+
+    @pl.when(pl.program_id(0) == pl.num_programs(0) - 1)
+    def _():
+        tok_out[:, tok_ref.shape[1] - 8 :] = tok_ref[:, tok_ref.shape[1] - 8 :] + halo_ref[...]
 
     @pl.when(pl.program_id(0) == 0)
     def _():
-        tok_out[...] = tok_ref[...] + halo_ref[...]
         din[...] = in_ref[...]
         dout[...] = out_ref[...]
         tail = tail_ref[...]
@@ -494,10 +499,7 @@
         dstep_bias[...] = turned[at + 1 : at + 2]
         dskip[...] = turned[at + 2 : at + 3]
         at = TILE + -(-(states + taps + 3) // 8) * 8
-        choose = (subs((wide, experts)) == lanes((wide, experts)) + at).astype(f32)
-        drouter[...] = lax.dot_general(
-            tail[:low_share], choose, (((1,), (0,)), ((), ())), precision=lax.Precision.HIGHEST,
-            preferred_element_type=f32)
+        drouter[...] = turned[at : at + experts, :low_share]
         at += experts
         dnorm[...] = turned[at : at + 1, :low_share]
         dmoe[...] = turned[at + 1 : at + 2, :low_share]
@@ -563,105 +565,102 @@
             pltpu.SemaphoreType.DMA((end.shape[0],)),
         ],
         compiler_params=pltpu.CompilerParams(
-            collective_id=4 if forward else 5, has_side_effects=True),
+            collective_id=5 if forward else 6, has_side_effects=True),
         name="chain_forward" if forward else "chain_backward",
     )(dsum, rates, end)
 
 
-def relay_kernel(seq, forward, states, dsum_ref, vec_ref, end_ref, out_ref, mine, theirs, their_sum, held, outgoing,
-                 pair_send, pair_recv, line_send, line_recv):
-    me = Place(4, seq)
-    y, z, last = me.y, me.z, me.Z - 1
-    step = 1 if forward else -1
-    first = y == (0 if forward else 1)
-    has_before = z > 0 if forward else z < last
-    has_after = z < last if forward else z > 0
-    pair, before, after = me.at(y=1 - y), me.at(z=z - step), me.at(z=z + step)
-    greet([(None, pair), (has_before, before), (has_after, after)])
-    count = end_ref.shape[0]
-    rates = -jnp.exp(vec_ref[0:states])
-
-    def swaps(i):
+class Relay:
+    def __init__(self, seq, forward, states, dsum_ref, vec_ref, end_ref, out_ref, mine, theirs, their_sum, held,
+                 outgoing, pair_send, pair_recv, line_send, line_recv):
+        me = Place(4, seq)
+        y, z, last = me.y, me.z, me.Z - 1
+        step = 1 if forward else -1
+        self.first = y == (0 if forward else 1)
+        self.has_before = z > 0 if forward else z < last
+        self.has_after = z < last if forward else z > 0
+        self.pair, self.before, self.after = me.at(y=1 - y), me.at(z=z - step), me.at(z=z + step)
+        self.states, self.vec_ref, self.end_ref, self.out_ref = states, vec_ref, end_ref, out_ref
+        self.mine, self.theirs, self.dsum_ref, self.their_sum = mine, theirs, dsum_ref, their_sum
+        self.held, self.outgoing = held, outgoing
+        self.pair_send, self.pair_recv, self.line_send, self.line_recv = pair_send, pair_recv, line_send, line_recv
+        self.count = end_ref.shape[0]
+
+    def peers(self):
+        return [(None, self.pair), (self.has_before, self.before), (self.has_after, self.after)]
+
+    def swaps(self, i):
+        both = ((self.mine.at[i], self.theirs.at[i]), (self.dsum_ref.at[i], self.their_sum.at[i]))
         return [
             pltpu.make_async_remote_copy(
-                src_ref=src, dst_ref=dst, send_sem=pair_send.at[i, k], recv_sem=pair_recv.at[i, k],
-                device_id=pair, device_id_type=MESH)
-            for k, (src, dst) in enumerate(((mine.at[i], theirs.at[i]), (dsum_ref.at[i], their_sum.at[i])))
+                src_ref=src, dst_ref=dst, send_sem=self.pair_send.at[i, k], recv_sem=self.pair_recv.at[i, k],
+                device_id=self.pair, device_id_type=MESH)
+            for k, (src, dst) in enumerate(both)
         ]
 
-    def onward(i):
+    def onward(self, i):
         return pltpu.make_async_remote_copy(
-            src_ref=outgoing.at[i], dst_ref=held.at[i], send_sem=line_send.at[i],
-            recv_sem=line_recv.at[i], device_id=after, device_id_type=MESH)
-
-    for i in range(count):
-        mine[i] = end_ref[i].astype(bf16)
-        for cp in swaps(i):
+            src_ref=self.outgoing.at[i], dst_ref=self.held.at[i], send_sem=self.line_send.at[i],
+            recv_sem=self.line_recv.at[i], device_id=self.after, device_id_type=MESH)
+
+    def start(self, i):
+        self.mine[i] = self.end_ref[i].astype(bf16)
+        for cp in self.swaps(i):
             cp.start()
-    for i in range(count):
-        for cp in swaps(i):
+
+    def finish(self, i):
+        rates = -jnp.exp(self.vec_ref[0 : self.states])
+        for cp in self.swaps(i):
             cp.wait_recv()
-        own, other = end_ref[i], theirs[i].astype(f32)
-        own_sum, other_sum = dsum_ref[i], their_sum[i]
-        early, late = jnp.where(first, own, other), jnp.where(first, other, own)
-        early_sum, late_sum = jnp.where(first, own_sum, other_sum), jnp.where(first, other_sum, own_sum)
+        pick = lambda a, b: (jnp.where(self.first, a, b), jnp.where(self.first, b, a))
+        early, late = pick(self.end_ref[i], self.theirs[i].astype(f32))
+        early_sum, late_sum = pick(self.dsum_ref[i], self.their_sum[i])
         both = late + jnp.exp(rates * late_sum) * early
 
-        @pl.when(has_before)
+        @pl.when(self.has_before)
         def _():
-            onward(i).wait_recv()
-            arrived = held[i].astype(f32)
-            outgoing[i] = (both + jnp.exp(rates * (early_sum + late_sum)) * arrived).astype(bf16)
-
-        @pl.when(jnp.logical_not(has_before))
+            self.onward(i).wait_recv()
+            arrived = self.held[i].astype(f32)
+            self.outgoing[i] = (both + jnp.exp(rates * (early_sum + late_sum)) * arrived).astype(bf16)
+
+        @pl.when(jnp.logical_not(self.has_before))
         def _():
-            outgoing[i] = both.astype(bf16)
-
-        @pl.when(has_after)
+            self.outgoing[i] = both.astype(bf16)
+
+        @pl.when(self.has_after)
         def _():
-            onward(i).start()
-
-        @pl.when(has_before)
+            self.onward(i).start()
+
+        @pl.when(self.has_before)
         def _():
-            arrived = held[i].astype(f32)
-            out_ref[i] = jnp.where(first, arrived, early + jnp.exp(rates * early_sum) * arrived)
-
-        @pl.when(jnp.logical_not(has_before))
+            arrived = self.held[i].astype(f32)
+            self.out_ref[i] = jnp.where(self.first, arrived, early + jnp.exp(rates * early_sum) * arrived)
+
+        @pl.when(jnp.logical_not(self.has_before))
         def _():
-            out_ref[i] = jnp.where(first, jnp.zeros_like(early), early)
-    for i in range(count):
-        for cp in swaps(i):
-            cp.wait_send()
-
-        @pl.when(has_after)
-        def _():
-            onward(i).wait_send()
-
-
-def relay_states(batch, seq, forward, states, dsum, vec, end):
-    if not tuned(batch, seq):
-        return chain_states(seq, forward, dsum, -jnp.exp(vec[:states]), end)
-    n = end.shape[0]
-    return pl.pallas_call(
-        functools.partial(relay_kernel, seq, forward, states),
-        out_shape=jax.ShapeDtypeStruct(end.shape, f32),
-        in_specs=[VM] * 3,
-        out_specs=VM,
-        scratch_shapes=[
-            pltpu.VMEM(end.shape, bf16),
-            pltpu.VMEM(end.shape, bf16),
-            pltpu.VMEM(dsum.shape, f32),
-            pltpu.VMEM(end.shape, bf16),
-            pltpu.VMEM(end.shape, bf16),
-            pltpu.SemaphoreType.DMA((n, 2)),
-            pltpu.SemaphoreType.DMA((n, 2)),
-            pltpu.SemaphoreType.DMA((n,)),
-            pltpu.SemaphoreType.DMA((n,)),
-        ],
-        compiler_params=pltpu.CompilerParams(
-            collective_id=6 if forward else 7, has_side_effects=True),
-        name="relay_forward" if forward else "relay_backward",
-    )(dsum, vec, end)
+            self.out_ref[i] = jnp.where(self.first, jnp.zeros_like(early), early)
+
+    def settle(self):
+        for i in range(self.count):
+            for cp in self.swaps(i):
+                cp.wait_send()
+            pl.when(self.has_after)(self.onward(i).wait_send)
+
+
+def relay_scratch(seqs, states, inner):
+    n, state = seqs, (seqs, states, inner)
+    dma = pltpu.SemaphoreType.DMA
+    return [
+        pltpu.VMEM(state, bf16),
+        pltpu.VMEM(state, bf16),
+        pltpu.VMEM((seqs, 1, inner), f32),
+        pltpu.VMEM(state, bf16),
+        pltpu.VMEM(state, bf16),
+        dma((n, 2)),
+        dma((n, 2)),
+        dma((n,)),
+        dma((n,)),
+    ]
 
 
 def dot(a, b):
@@ -713,6 +712,7 @@
 WIDE = 256
 GROUP = 16
 LOG2E = math.log2(math.e)
+AHEAD = 256
 
 
 def conv_sum(ext_ref, s, cols, vec_ref, states, taps, rows):
@@ -725,6 +725,19 @@
 
 def normalize(x):
     return lax.rsqrt(jnp.mean(x * x, axis=-1, keepdims=True) + epsilon)
+
+
+class Quiet:
+    def __getattr__(self, name):
+        return lambda *args: None
+
+
+QUIET = Quiet()
+
+
+class Hooks(Quiet):
+    def __init__(self, **steps):
+        self.__dict__.update(steps)
 
 
 def unpack(tail_ref, share, low_share, room, experts, vec_ref, gain_ref, router_ref):
@@ -737,10 +750,11 @@
 
 
 def enter_packed(dims, share, low_share, experts, tok_ref, halo_ref, win_ref, tail_ref,
-                 ext_ref, z_ref, u_ref, dt_ref, proj_ref, end_ref, dsum_ref, vec_ref, gain_ref, router_ref, xn):
+                 ext_ref, z_ref, u_ref, dt_ref, proj_ref, end_ref, dsum_ref, vec_ref, gain_ref, router_ref, xn,
+                 hooks=QUIET):
     unpack(tail_ref, share, low_share, vec_ref.shape[0], experts, vec_ref, gain_ref, router_ref)
     enter_kernel(dims, tok_ref, halo_ref, win_ref, tail_ref.at[:, 0:TILE], vec_ref, gain_ref,
-                 ext_ref, z_ref, u_ref, dt_ref, proj_ref, end_ref, dsum_ref, xn)
+                 ext_ref, z_ref, u_ref, dt_ref, proj_ref, end_ref, dsum_ref, xn, hooks)
 
 
 def as_column(ref):
@@ -753,7 +767,7 @@
 
 
 def enter_kernel(dims, tok_ref, halo_ref, win_ref, small_ref, vec_ref, gain_ref,
-                 ext_ref, z_ref, u_ref, dt_ref, proj_ref, end_ref, dsum_ref, xn):
+                 ext_ref, z_ref, u_ref, dt_ref, proj_ref, end_ref, dsum_ref, xn, hooks=QUIET):
     seqs, rows, inner, states, rank, taps = dims
     count = seqs * rows
     for ref, at in ((tok_ref, 0), (halo_ref, count)):
@@ -762,6 +776,7 @@
     proj = jnp.zeros((count, small_ref.shape[1]), jnp.float32)
     for j in range(inner // WIDE):
         cols = slice(j * WIDE, (j + 1) * WIDE)
+        hooks.weights(j)
         part = dot(xn[...], win_ref[:, cols])
         z_ref[:, cols] = dot(xn[:count], win_ref[:, inner + j * WIDE : inner + (j + 1) * WIDE])
         for s in range(seqs):
@@ -779,6 +794,7 @@
         dt_ref[:, cols] = dt
         for s in range(seqs):
             dsum_ref[s, 0:1, cols] = jnp.sum(dt[s * rows : (s + 1) * rows], axis=0, keepdims=True)
+    hooks.projected()
     a2 = -jnp.exp(vec_ref[0:states]) * LOG2E
     blocks = inner // 128
     for s in range(seqs):
@@ -798,6 +814,7 @@
         hs = lax.fori_loop(0, rows // 8, eight, (zero,) * blocks)
         for k in range(blocks):
             end_ref[s, :, k * 128 : (k + 1) * 128] = hs[k]
+        hooks.scanned(s)
 
 
 def rank_lanes(proj, rank, states):
@@ -809,7 +826,7 @@
 def leave_kernel(dims, capacity, room, tok_ref, cot_ref, h0_ref, dt_ref, u_ref, z_ref, proj_ref, vec_ref, out_ref,
                  gain_ref, router_ref, route_ref, slot_ref,
                  hist_ref, y_ref, hid_ref, gated_ref, moe_ref, gate_ref, rows_ref,
-                 hbuf, hcur, sem, sem0):
+                 hbuf, hcur, sem, sem0, hooks=QUIET):
     seqs, rows, inner, states, rank, taps = dims
     count = seqs * rows
     a2 = -jnp.exp(vec_ref[0:states]) * LOG2E
@@ -859,6 +876,7 @@
             out_copy(s, g, g % 2).wait()
     for cp in firsts:
         cp.wait()
+    hooks.out_proj()
     hid = tok_ref[...].astype(jnp.float32)
     for j in range(inner // WIDE):
         cols = slice(j * WIDE, (j + 1) * WIDE)
@@ -868,6 +886,7 @@
         gated = (y * (z * sigmoid(z))).astype(jnp.bfloat16)
         gated_ref[:, cols] = gated
         hid = hid + dot(gated, out_ref[cols, :])
+    hooks.mixed()
     hid_ref[...] = hid
     moe_in = (hid * normalize(hid) * gain_ref[1:2]).astype(jnp.bfloat16)
     moe_ref[...] = moe_in
@@ -928,7 +947,8 @@
 
 def return_kernel(dims, capacity, room, ret_ref, cot_ref, hid_ref, moe_ref, gate_ref, gated_ref, y_ref, u_ref, z_ref, dt_ref,
                   proj_ref, vec_ref, out_ref, gain_ref, router_ref, route_ref, slot_ref,
-                  block_ref, ghid_ref, gy_ref, gz_ref, dout_ref, drouter_ref, dskip_ref, dgain_ref, adj_ref):
+                  block_ref, ghid_ref, gy_ref, gz_ref, dout_ref, drouter_ref, dskip_ref, dgain_ref, adj_ref,
+                  hooks=QUIET):
     seqs, rows, inner, states, rank, taps = dims
     count = seqs * rows
     total, width = ret_ref.shape[0], hid_ref.shape[1]
@@ -950,6 +970,7 @@
     grad_hid = cot + r2 * scaled - hid * (r2 * r2 * r2) * jnp.mean(scaled * hid, axis=1, keepdims=True)
     ghid_ref[...] = grad_hid
     branch = grad_hid.astype(jnp.bfloat16)
+    hooks.activations()
     for j in range(inner // WIDE):
         cols = slice(j * WIDE, (j + 1) * WIDE)
         dout_ref[cols, :] = dot_tn(gated_ref[:, cols], branch).astype(jnp.bfloat16)
@@ -960,6 +981,7 @@
         gy_ref[:, cols] = gy
         gz_ref[:, cols] = (grad * y_ref[:, cols] * (sig + z * sig * (1.0 - sig))).astype(jnp.bfloat16)
         dskip_ref[:, cols] = jnp.sum(gy * u_ref[:, cols], axis=0, keepdims=True)
+    hooks.gradients()
     a2 = -jnp.exp(vec_ref[0:states]) * LOG2E
     blocks = inner // 128
     for s in range(seqs):
@@ -978,12 +1000,13 @@
         ms = lax.fori_loop(0, rows // 8, eight, (zero,) * blocks)
         for k in range(blocks):
             adj_ref[s, :, k * 128 : (k + 1) * 128] = ms[k]
+        hooks.scanned(s)
 
 
 def back_kernel(dims, tok_ref, halo_ref, ext_ref, hist_ref, later_ref, gy_ref, gz_ref, ghid_ref, u_ref, dt_ref,
                 proj_ref, win_ref, small_ref, vec_ref, gain_ref,
                 dtok_ref, dhalo_ref, din_ref, dsmall_ref, dvec_ref, dgain_ref,
-                hbuf, ccol, bcol, gbsum, gcsum, adj, gdt, gu, gproj, gpad, gm, xn, gpre, sem):
+                hbuf, ccol, bcol, gbsum, gcsum, adj, gdt, gu, gproj, gpad, gm, xn, gpre, sem, hooks=QUIET):
     small_ref = small_ref.at[:, 0:TILE]
     seqs, rows, inner, states, rank, taps = dims
     count = seqs * rows
@@ -1064,6 +1087,7 @@
         gproj[pl.ds(at, GROUP), :] = out
         return carry
     lax.fori_loop(0, steps, group, 0)
+    hooks.rest()
 
     low = rank_lanes(proj_ref[...], rank, states)
     at = rank + 2 * states
@@ -1117,6 +1141,7 @@
         zcols = slice(inner + j * WIDE, inner + (j + 1) * WIDE)
         din_ref[:, cols] = dot_tn(xn[...], gm[:, cols]).astype(jnp.bfloat16)
         din_ref[:, zcols] = dot_tn(xn[:count], gz_ref[:, cols]).astype(jnp.bfloat16)
+        hooks.columns(j)
         gz = jnp.concatenate([gz_ref[:, cols], jnp.zeros((gm.shape[0] - count, WIDE), jnp.bfloat16)])
         grad_normed = grad_normed + dot_nt(gm[:, cols], win_ref[:, cols]) + dot_nt(gz, win_ref[:, zcols])
     gain_sum = 0.0
@@ -1139,11 +1164,11 @@
     return pltpu.CompilerParams(vmem_limit_bytes=mib << 20)
 
 
-def moe_kernel(seq, rows_ref, up_ref, down_ref, up2_ref, down2_ref,
+def moe_kernel(seq, rows_ref, up_ref, down_ref, up2_ref, first_ref,
                back_ref, land_ref, dup_ref, ddown_ref, dup2_ref, ddown2_ref,
                xbuf, part, act, ghid, hid, gact, sib_buf, own_sum,
                local_sem, disp_sem, pass_sem, recv_sem, load_sem, sib_send, sib_recv,
-               final_send, final_recv, final_local):
+               final_send, final_recv, final_local, down2_ref, cross_sem):
     me = Place(4, seq)
     b, s = me.at()
     y, z, Z, c = me.y, me.z, me.Z, me.c
@@ -1152,8 +1177,8 @@
     share = up_ref.shape[1]
     two = 2 * cap
     block = 2 * two
-    sib = me.at(c=1 - c)
-    greet([(None, sib)] + [(None, (b, (s + k) % seq)) for k in range(1, seq)])
+    sib, nx = me.at(c=1 - c), me.at(x=1 - me.x)
+    greet([(None, sib), (None, nx)] + [(None, (b, (s + k) % seq)) for k in range(1, seq)])
 
     def remote(src, dst, send, recv, dev):
         return pltpu.make_async_remote_copy(
@@ -1189,6 +1214,13 @@
     for j in range(2):
         dispatch(1, j).start()
 
+    head = first_ref.shape[0]
+    if head < share:
+        rest = remote(down_ref.at[head:], down2_ref.at[head:], cross_sem.at[0], cross_sem.at[1], nx)
+        rest.start()
+    if head:
+        front = pltpu.make_async_copy(first_ref, down2_ref.at[0:head], cross_sem.at[2])
+        front.start()
     ups, downs = (up_ref, up2_ref), (down_ref, down2_ref)
 
     def compute(k):
@@ -1255,6 +1287,13 @@
         load(k, 1 - c).start()
         for cc in range(2):
             load(k, cc).wait()
+
+        @pl.when(k == 0)
+        def _():
+            if head < share:
+                rest.wait_recv()
+            if head:
+                front.wait()
         compute(k)
         to_sib(k).start()
 
@@ -1294,6 +1333,8 @@
         e = (s + k) % seq
         remote(back_ref.at[e], back_ref.at[e], disp_sem.at[0], final_recv.at[e], sib).wait_recv()
     keep_home().wait()
+    if head < share:
+        rest.wait_send()
     dispatch(0, 1 - y).wait_send()
     own.wait_send()
     hand(z * 2 + 1 - y).wait_send()
@@ -1354,6 +1395,8 @@
                 dma((Z, 2)),
                 dma((seq,)),
                 dma,
+                pltpu.VMEM((hidden_share, width), bf16),
+                dma((3,)),
             ],
             compiler_params=pltpu.CompilerParams(
                 collective_id=2, has_side_effects=True, vmem_limit_bytes=56 << 20),
@@ -1390,6 +1433,105 @@
     return lax.all_to_all(mine, "seq", split_axis=0, concat_axis=0, tiled=True), d_up, d_down, None, None
 
 
+class Moves:
+    def __init__(self, sems):
+        self.sems, self.used, self.named = sems, 0, {}
+
+    def start(self, name, src, dst):
+        cp = pltpu.make_async_copy(src, dst, self.sems.at[self.used])
+        self.used += 1
+        cp.start()
+        self.named.setdefault(name, []).append(cp)
+
+    def wait(self, *names):
+        for name in names:
+            for cp in self.named.pop(name):
+                cp.wait()
+
+    def wait_all(self):
+        self.wait(*list(self.named))
+
+
+def forward_kernel(dims, share, low_share, experts, capacity, room, seq,
+                   tok_ref, halo_ref, tail_ref, cot_ref, route_ref, slot_ref, win_hbm, out_hbm,
+                   ext_hbm, z_hbm, u_hbm, dt_hbm, y_hbm, gated_hbm, hist_ref, proj_ref, dsum_ref, vec_ref, gain_ref,
+                   router_ref, hid_ref, moe_ref, gate_ref, rows_ref,
+                   win, out, ext, z, u, dt, y, gated, end, start, xn, hbuf, hcur, sem, sem0, sems, *relay_refs):
+    inner = dims[2]
+    moves = Moves(sems)
+    for j in range(inner // WIDE):
+        for base in (0, inner):
+            cols = pl.ds(base + j * WIDE, WIDE)
+            moves.start(("win", j), win_hbm.at[:, cols], win.at[:, cols])
+    moves.start("out", out_hbm, out)
+    relay = Relay(seq, True, dims[3], dsum_ref, vec_ref, end, start, *relay_refs)
+    greet(relay.peers())
+
+    def projected():
+        for name, src, dst in (("ext", ext, ext_hbm), ("z", z, z_hbm), ("u", u, u_hbm), ("dt", dt, dt_hbm)):
+            moves.start(name, src, dst)
+
+    enter_packed(dims, share, low_share, experts, tok_ref, halo_ref, win, tail_ref, ext, z, u, dt, proj_ref, end,
+                 dsum_ref, vec_ref, gain_ref, router_ref, xn,
+                 hooks=Hooks(weights=lambda j: moves.wait(("win", j)), projected=projected, scanned=relay.start))
+    for i in range(relay.count):
+        relay.finish(i)
+
+    def mixed():
+        moves.start("y", y, y_hbm)
+        moves.start("gated", gated, gated_hbm)
+
+    leave_kernel(dims, capacity, room, tok_ref, cot_ref, start, dt, u, z, proj_ref, vec_ref, out, gain_ref, router_ref,
+                 route_ref, slot_ref, hist_ref, y, hid_ref, gated, moe_ref, gate_ref, rows_ref, hbuf, hcur, sem, sem0,
+                 hooks=Hooks(out_proj=lambda: moves.wait("out"), mixed=mixed))
+    relay.settle()
+    moves.wait_all()
+
+
+def backward_kernel(dims, capacity, room, seq,
+                    ret_ref, cot_ref, hid_ref, moe_ref, gate_ref, vec_ref, gain_ref, router_ref, route_ref, slot_ref,
+                    dsum_ref, proj_ref, gated_hbm, out_hbm, z_hbm, y_hbm, u_hbm, dt_hbm, ext_hbm, win_hbm, tail_hbm,
+                    tok_hbm, halo_hbm, hist_ref,
+                    block_ref, dtok_ref, dhalo_ref, din_hbm, dout_hbm, dsmall_ref, dvec_ref, dnorm_ref, dmoe_ref,
+                    drouter_ref, dskip_ref,
+                    gated, out, z, y, u, dt, ext, win, tail, tok, halo, gy, gz, ghid, din, dout, adj, later,
+                    hbuf, ccol, bcol, gbsum, gcsum, carry, gdt, gu, gproj, gpad, gm, xn, gpre, sem, sems, *relay_refs):
+    inner = dims[2]
+    moves = Moves(sems)
+    for name, src, dst in (
+        ("gated", gated_hbm, gated), ("out", out_hbm, out), ("z", z_hbm, z), ("y", y_hbm, y), ("u", u_hbm, u),
+        ("dt", dt_hbm, dt), ("ext", ext_hbm, ext), ("win", win_hbm, win), ("tail", tail_hbm, tail),
+        ("tok", tok_hbm, tok), ("halo", halo_hbm, halo),
+    ):
+        moves.start(name, src, dst)
+    relay = Relay(seq, False, dims[3], dsum_ref, vec_ref, adj, later, *relay_refs)
+    greet(relay.peers())
+
+    def gradients():
+        moves.start("dout", dout, dout_hbm)
+        moves.wait("dt")
+
+    return_kernel(dims, capacity, room, ret_ref, cot_ref, hid_ref, moe_ref, gate_ref, gated, y, u, z, dt, proj_ref,
+                  vec_ref, out, gain_ref, router_ref, route_ref, slot_ref,
+                  block_ref, ghid, gy, gz, dout, drouter_ref, dskip_ref, dmoe_ref, adj,
+                  hooks=Hooks(activations=lambda: moves.wait("gated", "out", "z", "y", "u"), gradients=gradients,
+                              scanned=relay.start))
+    for i in range(relay.count):
+        relay.finish(i)
+
+    def columns(j):
+        for base in (0, inner):
+            cols = pl.ds(base + j * WIDE, WIDE)
+            moves.start("din", din.at[:, cols], din_hbm.at[:, cols])
+
+    back_kernel(dims, tok, halo, ext, hist_ref, later, gy, gz, ghid, u, dt, proj_ref, win, tail, vec_ref, gain_ref,
+                dtok_ref, dhalo_ref, din, dsmall_ref, dvec_ref, dnorm_ref,
+                hbuf, ccol, bcol, gbsum, gcsum, carry, gdt, gu, gproj, gpad, gm, xn, gpre, sem,
+                hooks=Hooks(rest=lambda: moves.wait("ext", "win", "tail", "tok", "halo"), columns=columns))
+    relay.settle()
+    moves.wait_all()
+
+
 def body(
     tokens,
     in_proj,
@@ -1430,7 +1572,7 @@
     fast = tuned(batch, seq)
     if fast:
         in_full, out_full, tail_full, halo = gather_all(
-            batch, seq, room, in_proj, out_proj, tokens, state_proj, step_proj, router_proj, lines,
+            batch, seq, room, in_proj, out_proj, tokens, state_proj, step_proj, router_proj.T, lines,
             (norm_gain[None], moe_gain[None]))
         halo = halo.reshape(seqs * 8, width)
     else:
@@ -1450,122 +1592,123 @@
             lax.all_gather(a, both, axis=0, tiled=True) for a in (in_proj, out_proj, tail)
         )
     up, down, tail_full = lax.optimization_barrier((expert_up[0], expert_down[0], tail_full))
-    up2, down2 = cross(batch, up, down) if fast else (None, None)
+    up2, down2 = cross(batch, up, down[:AHEAD]) if fast else (None, None)
     tok, cot = tokens.reshape(count, width), cotangent.reshape(count, width)
-    outs = [
-        like(seqs, rows + 8, inner),
-        like(count, inner),
-        like(count, inner),
-        like(count, inner),
-        like(count, tile),
-        like(seqs, states, inner),
-        like(seqs, 1, inner),
+    size = GROUP * states
+    total = experts * capacity
+    edge_rows = seqs * 8
+    dma = pltpu.SemaphoreType.DMA
+    acts = like(count, inner)
+    ext_s, state_s, dsum_s = like(seqs, rows + 8, inner), like(seqs, states, inner), like(seqs, 1, inner)
+    proj_s, low_s, vec_s = like(count, tile), like(count, inner, dtype=bf16), like(room, inner)
+    hist_s = like(seqs, (rows + 1) * states, inner, dtype=bf16)
+    hid_s, moe_s, gate_s = like(count, width), like(count, width, dtype=bf16), like(count, 1)
+    rows_s = like(total, 2 * width, dtype=bf16)
+    gain_s, router_s = like(8, width), like(width, tile, dtype=bf16)
+    vmem = lambda a: pltpu.VMEM(a.shape, a.dtype)
+    normed = pltpu.VMEM((count + edge_rows, width), bf16)
+    leave_scratch = [pltpu.VMEM((2, size, inner), bf16), pltpu.VMEM(state_s.shape, bf16), dma((2,)), dma((seqs,))]
+    back_scratch = [
+        pltpu.VMEM((2, size + states, inner), bf16),
+        pltpu.VMEM((GROUP, states, tile), f32),
+        pltpu.VMEM((GROUP, states, tile), f32),
+        pltpu.VMEM((GROUP, states, tile), f32),
+        pltpu.VMEM((GROUP, states, tile), f32),
+        pltpu.VMEM((states, inner), f32),
+        vmem(acts),
+        vmem(acts),
+        vmem(proj_s),
+        pltpu.VMEM((rows + 16, WIDE), f32),
+        pltpu.VMEM((count + edge_rows, inner), bf16),
+        normed,
+        vmem(low_s),
+        dma((2,)),
     ]
-    scratch = [pltpu.VMEM((count + seqs * 8, width), bf16)]
+    tok_s, halo_s, din_s = like(count, width), like(edge_rows, width), like(width, 2 * inner, dtype=bf16)
+    dout_s, dsmall_s = like(inner, width, dtype=bf16), like(inner, tile, dtype=bf16)
+    drouter_s, dskip_s, dgain_s = like(width, tile), like(1, inner), like(1, width)
+    wide = inner // WIDE
     if fast:
-        *outs, vec, gain, router = pl.pallas_call(
-            partial(enter_packed, dims, share, low_share, experts),
-            out_shape=outs + [like(room, inner), like(8, width), like(width, tile, dtype=bf16)],
-            in_specs=[VM] * 4,
-            out_specs=[VM] * 10,
-            scratch_shapes=scratch,
-            compiler_params=params(),
-            name="enter",
-        )(tok, halo, in_full, tail_full)
+        (ext, z, u, dt, y, gated, hist, proj, dsum, vec, gain, router, hid, moe_in, gate, sent) = pl.pallas_call(
+            partial(forward_kernel, dims, share, low_share, experts, capacity, room, seq),
+            out_shape=[ext_s, acts, acts, acts, acts, low_s, hist_s, proj_s, dsum_s, vec_s, gain_s, router_s,
+                       hid_s, moe_s, gate_s, rows_s],
+            in_specs=[VM] * 6 + [HBM] * 2,
+            out_specs=[HBM] * 7 + [VM] * 9,
+            scratch_shapes=[
+                vmem(in_full), vmem(out_full), vmem(ext_s), vmem(acts), vmem(acts), vmem(acts), vmem(acts), vmem(low_s),
+                vmem(state_s), vmem(state_s), normed, *leave_scratch, dma((2 * wide + 7,)),
+                *relay_scratch(seqs, states, inner),
+            ],
+            compiler_params=pltpu.CompilerParams(
+                collective_id=3, has_side_effects=True, vmem_limit_bytes=58 << 20),
+            name="forward",
+        )(tok, halo, tail_full, cot, routes, slot_index, in_full, out_full)
     else:
         vec = tail_full[:, tile : tile + room].T.astype(f32)
         router = tail_full[:, tile:].reshape(devices, share, tile)[:, :low_share].reshape(width, tile)
         gain = router[:, room + experts : room + experts + 2].T.astype(f32)
-        outs = pl.pallas_call(
+        ext, z, u, dt, proj, end, dsum = pl.pallas_call(
             partial(enter_kernel, dims),
-            out_shape=outs,
+            out_shape=[ext_s, acts, acts, acts, proj_s, state_s, dsum_s],
             in_specs=[VM] * 6,
             out_specs=[VM] * 7,
-            scratch_shapes=scratch,
+            scratch_shapes=[normed],
             compiler_params=params(),
             name="enter",
         )(tok, halo, in_full, tail_full[:, :tile], vec, gain)
-    ext, z, u, dt, proj, end, dsum = outs
-    before = relay_states(batch, seq, True, states, dsum, vec, end)
-    size = GROUP * states
-    total = experts * capacity
-    hist, y, hid, gated, moe_in, gate, sent = pl.pallas_call(
-        partial(leave_kernel, dims, capacity, room),
-        out_shape=[
-            like(seqs, (rows + 1) * states, inner, dtype=bf16),
-            like(count, inner),
-            like(count, width),
-            like(count, inner, dtype=bf16),
-            like(count, width, dtype=bf16),
-            like(count, 1),
-            like(total, 2 * width, dtype=bf16),
-        ],
-        in_specs=[VM] * 13,
-        out_specs=[HBM] + [VM] * 6,
-        scratch_shapes=[
-            pltpu.VMEM((2, size, inner), bf16),
-            pltpu.VMEM((seqs, states, inner), bf16),
-            pltpu.SemaphoreType.DMA((2,)),
-            pltpu.SemaphoreType.DMA((seqs,)),
-        ],
-        compiler_params=params(),
-        name="leave",
-    )(tok, cot, before, dt, u, z, proj, vec, out_full, gain, router, routes, slot_index)
+        rates = -jnp.exp(vec[:states])
+        before = chain_states(seq, True, dsum, rates, end)
+        hist, y, hid, gated, moe_in, gate, sent = pl.pallas_call(
+            partial(leave_kernel, dims, capacity, room),
+            out_shape=[hist_s, acts, hid_s, low_s, moe_s, gate_s, rows_s],
+            in_specs=[VM] * 13,
+            out_specs=[HBM] + [VM] * 6,
+            scratch_shapes=leave_scratch,
+            compiler_params=params(),
+            name="leave",
+        )(tok, cot, before, dt, u, z, proj, vec, out_full, gain, router, routes, slot_index)
 
     back, d_up, d_down, d_up2, d_down2 = moe_rows(
         batch, seq, sent.reshape(experts, capacity, 2 * width), up, down, up2, down2)
     back = back.reshape(total, 2 * width)
 
-    block_out, ghid, gy, gz, d_out, d_router, d_skip, d_moe, adj = pl.pallas_call(
-        partial(return_kernel, dims, capacity, room),
-        out_shape=[
-            like(count, width, dtype=bf16),
-            like(count, width),
-            like(count, inner),
-            like(count, inner, dtype=bf16),
-            like(inner, width, dtype=bf16),
-            like(width, tile),
-            like(1, inner),
-            like(1, width),
-            like(seqs, states, inner),
-        ],
-        in_specs=[VM] * 17,
-        out_specs=[VM] * 9,
-        compiler_params=params(),
-        name="back_experts",
-    )(back, cot, hid, moe_in, gate, gated, y, u, z, dt, proj, vec, out_full, gain, router, routes, slot_index)
-    later = relay_states(batch, seq, False, states, dsum, vec, adj)
-    d_tok, d_halo, d_in, d_small, d_vec, d_norm = pl.pallas_call(
-        partial(back_kernel, dims),
-        out_shape=[
-            like(count, width),
-            like(seqs * 8, width),
-            like(width, 2 * inner, dtype=bf16),
-            like(inner, tile, dtype=bf16),
-            like(room, inner),
-            like(1, width),
-        ],
-        in_specs=[VM] * 3 + [HBM] + [VM] * 11,
-        out_specs=[VM] * 6,
-        scratch_shapes=[
-            pltpu.VMEM((2, size + states, inner), bf16),
-            pltpu.VMEM((GROUP, states, tile), f32),
-            pltpu.VMEM((GROUP, states, tile), f32),
-            pltpu.VMEM((GROUP, states, tile), f32),
-            pltpu.VMEM((GROUP, states, tile), f32),
-            pltpu.VMEM((states, inner), f32),
-            pltpu.VMEM((count, inner), f32),
-            pltpu.VMEM((count, inner), f32),
-            pltpu.VMEM((count, tile), f32),
-            pltpu.VMEM((rows + 16, WIDE), f32),
-            pltpu.VMEM((count + seqs * 8, inner), bf16),
-            pltpu.VMEM((count + seqs * 8, width), bf16),
-            pltpu.VMEM((count, inner), bf16),
-            pltpu.SemaphoreType.DMA((2,)),
-        ],
-        compiler_params=params(),
-        name="back_mixer",
-    )(tok, halo, ext, hist, later, gy, gz, ghid, u, dt, proj, in_full, tail_full, vec, gain)
+    if fast:
+        (block_out, d_tok, d_halo, d_in, d_out, d_small, d_vec, d_norm, d_moe, d_router, d_skip) = pl.pallas_call(
+            partial(backward_kernel, dims, capacity, room, seq),
+            out_shape=[moe_s, tok_s, halo_s, din_s, dout_s, dsmall_s, vec_s, dgain_s, dgain_s, drouter_s, dskip_s],
+            in_specs=[VM] * 12 + [HBM] * 12,
+            out_specs=[VM] * 3 + [HBM] * 2 + [VM] * 6,
+            scratch_shapes=[
+                vmem(low_s), vmem(out_full), vmem(acts), vmem(acts), vmem(acts), vmem(acts), vmem(ext_s), vmem(in_full),
+                vmem(tail_full), vmem(tok), vmem(halo), vmem(acts), vmem(low_s), vmem(tok_s), vmem(din_s), vmem(dout_s),
+                vmem(state_s), vmem(state_s), *back_scratch, dma((2 * wide + 12,)),
+                *relay_scratch(seqs, states, inner),
+            ],
+            compiler_params=pltpu.CompilerParams(
+                collective_id=4, has_side_effects=True, vmem_limit_bytes=60 << 20),
+            name="backward",
+        )(back, cot, hid, moe_in, gate, vec, gain, router, routes, slot_index, dsum, proj,
+          gated, out_full, z, y, u, dt, ext, in_full, tail_full, tok, halo, hist)
+    else:
+        block_out, ghid, gy, gz, d_out, d_router, d_skip, d_moe, adj = pl.pallas_call(
+            partial(return_kernel, dims, capacity, room),
+            out_shape=[moe_s, tok_s, acts, low_s, dout_s, drouter_s, dskip_s, dgain_s, state_s],
+            in_specs=[VM] * 17,
+            out_specs=[VM] * 9,
+            compiler_params=params(),
+            name="back_experts",
+        )(back, cot, hid, moe_in, gate, gated, y, u, z, dt, proj, vec, out_full, gain, router, routes, slot_index)
+        later = chain_states(seq, False, dsum, rates, adj)
+        d_tok, d_halo, d_in, d_small, d_vec, d_norm = pl.pallas_call(
+            partial(back_kernel, dims),
+            out_shape=[tok_s, halo_s, din_s, dsmall_s, vec_s, dgain_s],
+            in_specs=[VM] * 3 + [HBM] + [VM] * 11,
+            out_specs=[VM] * 6,
+            scratch_shapes=back_scratch,
+            compiler_params=params(),
+            name="back_mixer",
+        )(tok, halo, ext, hist, later, gy, gz, ghid, u, dt, proj, in_full, tail_full, vec, gain)
 
     skip_row = states + taps + 2
     if fast:
@@ -1575,25 +1718,26 @@
         steps = 4
         slab = lambda a: pl.BlockSpec((a.shape[0] // steps, a.shape[1]), lambda i: (i, 0))
         whole = lambda *shape: pl.BlockSpec(shape, lambda i: (0,) * len(shape))
-        edge = pl.BlockSpec((seqs, 8, width), lambda i: (0, rows // 8 - 1, 0))
+        piece = pl.BlockSpec((seqs, rows // steps, width), lambda i: (0, i, 0))
         shapes = [
             s_in.shape, (taps, share), (1, share), (share, rank + 2 * states), (rank, share), (1, share),
-            (states, share), (1, share), s_out.shape, (1, low_share), (1, low_share), (low_share, experts),
+            (states, share), (1, share), s_out.shape, (1, low_share), (1, low_share), (experts, low_share),
         ]
-        d_tok, *sums, d_up, d_down = pl.pallas_call(
+        block_out, d_tok, *sums, d_up, d_down = pl.pallas_call(
             partial(finish_kernel, dims, low_share, experts),
-            out_shape=[like(*tokens.shape)] + [like(*a) for a in shapes] + [like(*d_up.shape), like(*d_down.shape)],
+            out_shape=[like(*tokens.shape, dtype=bf16), like(*tokens.shape)] + [like(*a) for a in shapes] + [like(*d_up.shape), like(*d_down.shape)],
             grid=(steps,),
-            in_specs=[whole(*s_in.shape), whole(*s_out.shape), whole(*s_tail.shape), whole(seqs, 8, width), edge]
+            in_specs=[whole(*s_in.shape), whole(*s_out.shape), whole(*s_tail.shape), whole(seqs, 8, width), piece, piece]
             + [slab(a) for a in (d_up, d_up2, d_down, d_down2)],
-            out_specs=[edge] + [whole(*a) for a in shapes] + [slab(d_up), slab(d_down)],
-            input_output_aliases={4: 0},
+            out_specs=[piece, piece] + [whole(*a) for a in shapes] + [slab(d_up), slab(d_down)],
             compiler_params=params(),
             name="finish",
-        )(s_in, s_out, s_tail, from_next.reshape(seqs, 8, width), d_tok.reshape(tokens.shape), d_up, d_up2, d_down, d_down2)
+        )(s_in, s_out, s_tail, from_next.reshape(seqs, 8, width), d_tok.reshape(tokens.shape),
+          block_out.reshape(tokens.shape), d_up, d_up2, d_down, d_down2)
         for i in (2, 5, 7, 9, 10):
             sums[i] = sums[i][0]
-        return (block_out.reshape(tokens.shape), d_tok, *sums, d_up[None], d_down[None])
+        sums[11] = sums[11].T
+        return (block_out, d_tok, *sums, d_up[None], d_down[None])
     d_model = d_router.at[:, room + experts : room + experts + 2].set(jnp.concatenate([d_norm, d_moe]).T)
     d_model = jnp.pad(
         d_model.reshape(devices, low_share, tile)[:, :, room:], ((0, 0), (0, share - low_share), (0, 0))

time: 314 us -> 292 us (0.930)
  Pallas kernels: 295 us -> 283 us
  waiting for transfers between devices: 7.39 us -> 0.01 us
    pallas_call x6 -> x2, Pallas kernels: 124 us -> 98.2 us  [the longest x1 63.4 us: body(): pl.pallas_call(partial(backward_kernel, dims, capacity, room, seq), out_s...]
    pallas_call x1, Pallas kernels: 54 us -> 65.9 us  [moe_rows(): pl.pallas_call(functools.partial(moe_kernel, seq), out_shape=[like(seq, c...]
    ppermute x4, waiting for transfers between devices: 7.39 us -> 0.01 us  [cross(): lax.ppermute(a, 'batch', [(i, (i + 2) % batch) for i in range(batch)])]
  transfers between devices with their start and end apart: 4 -> 4, of which waited for: 1 -> 0; matrix products, arithmetic and copies ran while one was open for 0% -> 0% of each run, Pallas kernels for 61% -> 57%
where the time goes in v1:
time: 292 us; the launch traced here: 291 us
  Pallas kernels  283 us (97%)
  starting transfers between devices  4.25 us (1%)
  local copies, waits for them, and re-layouts  3.52 us (1%)
    pallas_call x1, Pallas kernels, reduce_all(): pl.pallas_call(functools.partial(reduce_kernel, batch, seq, low_share, ex...  68 us
    pallas_call x1, Pallas kernels, moe_rows(): pl.pallas_call(functools.partial(moe_kernel, seq), out_shape=[like(seq, c...  65.9 us
    pallas_call x1, Pallas kernels, body(): pl.pallas_call(partial(backward_kernel, dims, capacity, room, seq), out_s...  63.4 us
    pallas_call x1, Pallas kernels, gather_all(): pl.pallas_call(functools.partial(gather_kernel, batch, seq), out_shape=[j...  43.6 us
    pallas_call x1, Pallas kernels, body(): pl.pallas_call(partial(forward_kernel, dims, share, low_share, experts, c...  34.8 us
    pallas_call x1, Pallas kernels, body(): pl.pallas_call(partial(finish_kernel, dims, low_share, experts), out_shap...  6.98 us
  transfers between devices with their start and end apart: 4, of which 0 were waited for; matrix products, arithmetic and copies ran while one was open for 0% of the time, Pallas kernels for 57%

profile of v1, /device:TPU:0, one launch (start us, length us, event | category | flops | bytes accessed | tf_op | source)
XLA Modules:
  0.0 291.4 jit_solution(11464844197276787074)
XLA Ops:
  0.7 43.6 %gather_weights.1 = (bf16[768,3072]{1,0:T(8,128)(2,1)}, bf16[1536,768]{1,0:T(8,128)(2,1)}, bf16[1536,256]{1,0:T(8,128)(2,1)}, bf16[2,8,768]{2,1,0:T(8,128)(2,1)}) custom-call(bf16[24,3072]{1,0:T(8,128)(2,1)} %refs_0_.1, bf16[48,768]{1,0:T(8,128)(2,1)} %refs_1_.1, bf16[2,128,768]{2,1,0:T(8,128)(2,1)} %refs_2_.1, bf16[48,80]{1,0:T(8,128)(2,1)} %refs_3_.1, ...), custom_call_target="tpu_custom_call" | custom-call | tf_op jit(solution)/shard_map/gather_weights/pallas_call | solution.py:230
  44.3 1.2 collective-permute-start
  45.5 1.0 slice.3
  46.5 0.9 collective-permute-start.1
  47.5 34.8 %forward.1 = (f32[2,136,1536]{2,1,0:T(8,128)}, f32[256,1536]{1,0:T(8,128)}, f32[256,1536]{1,0:T(8,128)}, f32[256,1536]{1,0:T(8,128)}, f32[256,1536]{1,0:T(8,128)...) custom-call(bf16[256,768]{1,0:T(8,128)(2,1)} %bitcast.24, ...), custom_call_target="tpu_custom_call" | custom-call | tf_op jit(solution)/shard_map/forward/pallas_call | solution.py:1632
  82.2 0.0 collective-permute-done.1.first_ref
  82.2 0.0 copy-start.3
  82.2 0.0 collective-permute-done.up2_ref
  82.3 0.0 copy-start.2
  82.3 0.7 copy-done.3
  83.0 0.4 copy-done.2
  83.4 65.9 %experts.1 = (bf16[8,40,1536]{2,1,0:T(8,128)(2,1)}, bf16[2,320,1536]{2,1,0:T(8,128)(2,1)}, f32[768,768]{1,0:T(8,128)}, f32[768,768]{1,0:T(8,128)}, bf16[768,768]{1,0:T(8,128)(2,1)}, /*index=5*/bf16[768,768]{1,0:T(8,128)(2,1)}) custom-call(bf16[8,40,1536]{2,1,0:T(8,128)(2,1)} %bitcast.32, bf16[768,768]{1,0:T(8,128)(2,1)} %bitcast.31, ...), custom_call_target="tpu_custom_call" | custom-call | tf_op jit(solution)/shard_map/experts/pallas_call | solution.py:1367
  149.3 1.2 collective-permute-start.2
  150.4 0.9 collective-permute-start.3
  151.4 63.4 %backward.1 = (bf16[256,768]{1,0:T(8,128)(2,1)}, f32[256,768]{1,0:T(8,128)}, f32[16,768]{1,0:T(8,128)}, bf16[768,3072]{1,0:T(8,128)(2,1)}, bf16[1536,768]{1,0:T(...) custom-call(bf16[320,1536]{1,0:T(8,128)(2,1)} %bitcast.33, ...), custom_call_target="tpu_custom_call" | custom-call | tf_op jit(solution)/shard_map/backward/pallas_call | solution.py:1677
  214.8 68.0 %reduce_grads.1 = (f32[24,3072]{1,0:T(8,128)}, f32[48,768]{1,0:T(8,128)}, f32[48,256]{1,0:T(8,128)}, f32[16,768]{1,0:T(8,128)}) custom-call(bf16[768,3072]{1,0:T(8,128)(2,1)} %get-tuple-element.99.refs_0_, bf16[1536,768]{1,0:T(8,128)(2,1)} %get-tuple-element.100.refs_1_, bf16[1536,128]{1,0:T(8,128)(2,1)} %get-tuple-element.101.refs_2_, ...), custom_call_target="tpu_custom_call" | custom-call | tf_op jit(solution)/shard_map/reduce_grads/pallas_call | solution.py:459
  282.8 0.0 collective-permute-done.2.up2_ref
  282.8 0.0 copy-start
  282.8 0.0 collective-permute-done.3.down2_ref
  282.8 0.0 copy-start.1
  282.8 1.0 copy-done
  283.8 0.4 copy-done.1
  284.2 7.0 %finish.1 = (bf16[2,128,768]{2,1,0:T(8,128)(2,1)}, f32[2,128,768]{2,1,0:T(8,128)}, f32[24,3072]{1,0:T(8,128)}, f32[4,48]{1,0:T(4,128)}, f32[1,48]{1,0:T(1,128)},...) custom-call(f32[24,3072]{1,0:T(8,128)} %get-tuple-element.108.in_ref, ...), custom_call_target="tpu_custom_call" | custom-call | tf_op jit(solution)/shard_map/finish/pallas_call | solution.py:1726
Async XLA Ops:
  44.3 38.0 %collective-permute-start = (bf16[768,768]{1,0:T(8,128)(2,1)}, bf16[768,768]{1,0:T(8,128)(2,1)S(1)}, u32[]{:S(2)}, u32[]{:S(2)}) collective-permute-start(bf16[768,768]{1,0:T(8,128)(2,1)} %bitcast.30), channel_id=1, source_target_pairs={{0,16},{8,24},{16,0},{24,8},{1,17},{9,25},{17,1},{25,9},{2,18},{10... | collective-permute-start | bytes 3538952 | tf_op jit(solution)/shard_map/ppermute | solution.py:1357
  46.5 35.7 %collective-permute-start.1 = (bf16[256,768]{1,0:T(8,128)(2,1)S(1)}, bf16[256,768]{1,0:T(8,128)(2,1)S(1)}, u32[]{:S(2)}, u32[]{:S(2)}) collective-permute-start(bf16[256,768]{1,0:T(8,128)(2,1)S(1)} %slice.3), channel_id=1, source_target_pairs={{0,16},{8,24},{16,0},{24,8},{1,17},{9,25},{17,1},{25,9},{2,18},{10... | collective-permute-start | bytes 1179656 | tf_op jit(solution)/shard_map/ppermute | solution.py:1357
  82.2 0.7 copy-start.3
  82.3 1.1 copy-start.2
  149.3 133.5 %collective-permute-start.2 = (bf16[768,768]{1,0:T(8,128)(2,1)}, bf16[768,768]{1,0:T(8,128)(2,1)S(1)}, u32[]{:S(2)}, u32[]{:S(2)}) collective-permute-start(bf16[768,768]{1,0:T(8,128)(2,1)} %get-tuple-element.115), channel_id=1, source_target_pairs={{0,16},{8,24},{16,0},{24,8},{1,17},{9,25},{17,1},{25,9},{2,18},{10... | collective-permute-start | bytes 3538952 | tf_op jit(solution)/shard_map/ppermute | solution.py:1357
  150.4 132.4 %collective-permute-start.3 = (bf16[768,768]{1,0:T(8,128)(2,1)}, bf16[768,768]{1,0:T(8,128)(2,1)S(1)}, u32[]{:S(2)}, u32[]{:S(2)}) collective-permute-start(bf16[768,768]{1,0:T(8,128)(2,1)} %get-tuple-element.117), channel_id=1, source_target_pairs={{0,16},{8,24},{16,0},{24,8},{1,17},{9,25},{17,1},{25,9},{2,18},{10... | collective-permute-start | bytes 3538952 | tf_op jit(solution)/shard_map/ppermute | solution.py:1357
  282.8 1.0 copy-start
  282.8 1.4 copy-start.1

commit v2 on v1

--- a/solution.py
+++ b/solution.py
@@ -249,110 +249,145 @@
     )(in_proj, out_proj, tokens, state, step, router, *lines, *gains)
 
 
-def reduce_kernel(batch, seq, low_share, experts, skip_row, *refs):
-    n = 3
-    din_ref, dout_ref, dsmall_ref, dvec_ref, dskip_ref, drouter_ref, dnorm_ref, dmoe_ref, dhalo_ref = refs[:9]
-    outs, halo_ref = refs[9:12], refs[12]
-    refs = refs[13:]
-    work, sib_buf, far_buf, near_buf, line_buf = (refs[i * n : (1 + i) * n] for i in range(5))
-    tail, zeros, load_sem, send_sem, sib_sem, far_sem, near_sem, line_sem, halo_sem = refs[5 * n :]
-    me = Place(batch, seq)
-    Z, z = me.Z, me.z
-    rows = [r.shape[0] for r in outs]
-    sib = me.at(c=1 - me.c)
-    up, down = me.at(z=z + 1), me.at(z=z - 1)
-    nx, ny = me.at(x=1 - me.x), me.at(y=1 - me.y)
-    first = me.c == 0
-    pick = lambda flag, a, b: jnp.where(flag, a, b)
-    near = tuple(pick(first, a, b) for a, b in zip(ny, nx))
-    far = tuple(pick(first, a, b) for a, b in zip(nx, ny))
-    b, part_of = me.at()
-    has_before, has_after = part_of > 0, part_of < seq - 1
-    before, after = (b, part_of - 1), (b, part_of + 1)
-    greet([(None, sib), (None, nx), (None, ny), (z < Z - 1, up), (z > 0, down), (has_before, before), (has_after, after)])
-
-    def groups(c):
-        f = c == 0
+class Reducer:
+    def __init__(self, batch, seq, items, sib_bufs, far_bufs, near_bufs, line_bufs, sems):
+        self.items, self.sib_bufs, self.far_bufs, self.near_bufs, self.line_bufs = (
+            items, sib_bufs, far_bufs, near_bufs, line_bufs)
+        (self.sib_send, self.sib_recv, self.far_send, self.far_recv, self.near_send, self.near_recv,
+         self.line_send, self.line_recv) = sems
+        self.me = me = Place(batch, seq)
+        self.Z, self.z = me.Z, me.z
+        self.sib = me.at(c=1 - me.c)
+        self.up, self.down = me.at(z=me.z + 1), me.at(z=me.z - 1)
+        self.nx, self.ny = me.at(x=1 - me.x), me.at(y=1 - me.y)
+        pick = lambda a, b: tuple(jnp.where(me.c == 0, p, q) for p, q in zip(a, b))
+        self.near, self.far = pick(self.ny, self.nx), pick(self.nx, self.ny)
+        self.mine, self.others = self.groups(me.c), self.groups(1 - me.c)
+
+    def peers(self):
+        return [(None, self.sib), (None, self.nx), (None, self.ny),
+                (self.z < self.Z - 1, self.up), (self.z > 0, self.down)]
+
+    def groups(self, c):
+        me = self.me
         ox, oy = 1 - me.x, 1 - me.y
-        return [
-            (ox, oy),
-            (pick(f, ox, me.x), pick(f, me.y, oy)),
-            (pick(f, me.x, ox), pick(f, oy, me.y)),
-            (me.x, me.y),
-        ]
-
-    def slot(xy, zz):
-        return (xy[0] * 2 + xy[1]) * Z + zz
-
-    def turn(k):
-        return (z + 1 + k) % Z
-
-    sends = []
-
-    def send(pred, srcs, dsts, recv, dev):
-        copies = [
-            pltpu.make_async_remote_copy(
-                src_ref=srcs[a], dst_ref=dsts[a], send_sem=send_sem.at[len(sends), a],
-                recv_sem=recv(a), device_id=dev, device_id_type=MESH)
-            for a in range(n)
-        ]
-
-        def go():
-            for cp in copies:
-                cp.start()
-        if pred is None:
-            go()
+        pick = lambda a, b: jnp.where(c == 0, a, b)
+        return [(ox, oy), (pick(ox, me.x), pick(me.y, oy)), (pick(me.x, ox), pick(oy, me.y)), (me.x, me.y)]
+
+    def slot(self, xy, zz):
+        return (xy[0] * 2 + xy[1]) * self.Z + zz
+
+    def turn(self, k):
+        above = self.Z - 1 - self.z
+        return jnp.where(k < above, self.Z - 1 - k, jnp.where(k < self.Z - 1, k - above, self.z))
+
+    def item(self, a, c, xy, zz):
+        return self.items[a].at[self.me.index((xy[0] * 2 + c, zz * self.me.Y + xy[1]))]
+
+    def copy(self, src, dst, send, recv, dev):
+        return pltpu.make_async_remote_copy(
+            src_ref=src, dst_ref=dst, send_sem=send, recv_sem=recv, device_id=dev, device_id_type=MESH)
+
+    def to_sib(self, a, xy, k):
+        t = self.turn(k)
+        s = self.slot(xy, t)
+        return self.copy(self.item(a, 1 - self.me.c, xy, t), self.sib_bufs[a].at[s],
+                         self.sib_send.at[a, s], self.sib_recv.at[a, s], self.sib)
+
+    def give(self, a, columns):
+        for k in range(self.Z):
+            for xy in columns:
+                self.to_sib(a, xy, k).start()
+
+    def to_far(self, a, g, k):
+        t = self.turn(k)
+        fs = g * self.Z + t
+        return self.copy(self.item(a, self.me.c, self.mine[g], t), self.far_bufs[a].at[fs],
+                         self.far_send.at[a, fs], self.far_recv.at[a, fs], self.far)
+
+    def to_near(self, a, k):
+        t = self.turn(k)
+        return self.copy(self.item(a, self.me.c, self.mine[2], t), self.near_bufs[a].at[t],
+                         self.near_send.at[a, t], self.near_recv.at[a, t], self.near)
+
+    def step(self, a, g, k):
+        t = self.turn(k)
+        s = self.slot(self.mine[g], t)
+        item = self.item(a, self.me.c, self.mine[g], t)
+        take = lambda ref, recv: self.copy(ref, ref, self.sib_send.at[a, 0], recv, self.sib).wait_recv()
+        parts = [self.sib_bufs[a].at[s]]
+        take(parts[0], self.sib_recv.at[a, s])
+        if g >= 2:
+            fs = (g - 2) * self.Z + t
+            parts.append(self.far_bufs[a].at[fs])
+            take(parts[-1], self.far_recv.at[a, fs])
+        if g == 3:
+            parts.append(self.near_bufs[a].at[t])
+            take(parts[-1], self.near_recv.at[a, t])
+        total = item[...].astype(f32)
+        for part in parts:
+            total = total + part[...].astype(f32)
+        item[...] = total.astype(bf16)
+        if g < 2:
+            self.to_far(a, g, k).start()
+        elif g == 2:
+            self.to_near(a, k).start()
+
+    def onward(self, a, k):
+        t = self.turn(k)
+        rising = t > self.z
+        side = jnp.where(rising, 0, 1)
+        dev = (self.me.at()[0], jnp.where(rising, self.up[1], self.down[1]))
+        return self.copy(self.item(a, self.me.c, self.mine[3], t), self.line_bufs[a].at[side, t],
+                         self.line_send.at[a, k], self.line_recv.at[a, side, t], dev)
+
+    def line(self, a, k, out_ref):
+        t = self.turn(k)
+        item = self.item(a, self.me.c, self.mine[3], t)
+
+        def take(side):
+            ref = self.line_bufs[a].at[side, t]
+            self.copy(ref, ref, self.sib_send.at[a, 0], self.line_recv.at[a, side, t], self.sib).wait_recv()
+            return ref[...].astype(f32)
+        if k < self.Z - 1:
+            rising = t > self.z
+
+            @pl.when(jnp.where(rising, self.z, self.Z - 1 - self.z) > 0)
+            def _():
+                item[...] = (item[...].astype(f32) + take(jnp.where(rising, 0, 1))).astype(bf16)
+            self.onward(a, k).start()
         else:
-            pl.when(pred)(go)
-        sends.append((pred, copies))
-
-    def take(bufs, recv):
-        for a in range(n):
-            pltpu.make_async_remote_copy(
-                src_ref=bufs[a], dst_ref=bufs[a], send_sem=send_sem.at[0, a],
-                recv_sem=recv(a), device_id=sib, device_id_type=MESH).wait_recv()
-
-    def source(a, c, xy, zz):
-        index = me.index((xy[0] * 2 + c, zz * me.Y + xy[1]))
-        if a == 2:
-            return tail.at[index]
-        return (din_ref, dout_ref)[a].at[pl.ds(pl.multiple_of(index * rows[a], 8), rows[a])]
-
-    halo = pltpu.make_async_remote_copy(
-        src_ref=dhalo_ref, dst_ref=halo_ref, send_sem=halo_sem.at[0], recv_sem=halo_sem.at[1],
-        device_id=before, device_id_type=MESH)
-    blank = pltpu.make_async_copy(zeros, halo_ref, halo_sem.at[2])
-    zeros[...] = jnp.zeros_like(zeros)
-    pl.when(has_before)(halo.start)
-    pl.when(jnp.logical_not(has_after))(blank.start)
-
-    other = 1 - me.c
-    mine = groups(me.c)
-    first_sends, loads = [], []
-    for xy in groups(other):
-        for k in range(Z):
-            s = slot(xy, turn(k))
-            copies = [
-                pltpu.make_async_remote_copy(
-                    src_ref=source(a, other, xy, turn(k)), dst_ref=sib_buf[a].at[s],
-                    send_sem=send_sem.at[len(sends), a], recv_sem=sib_sem.at[s, a],
-                    device_id=sib, device_id_type=MESH)
-                for a in range(n)
-            ]
-            sends.append((None, copies))
-            first_sends.append(copies)
-    for xy in mine:
-        for k in range(Z):
-            s = slot(xy, turn(k))
-            loads.append([
-                pltpu.make_async_copy(source(a, me.c, xy, turn(k)), work[a].at[s], load_sem.at[s, a]) for a in range(n)
-            ])
-    for copies in first_sends + loads:
-        for cp in copies[:2]:
-            cp.start()
-
-    room, share = dvec_ref.shape[0], tail.shape[1]
-    blocks, width = tail.shape[0], drouter_ref.shape[0]
+            out_ref[...] = item[...].astype(f32)
+            for side, pred in ((0, self.z > 0), (1, self.z < self.Z - 1)):
+                @pl.when(pred)
+                def _(side=side):
+                    out_ref[...] = out_ref[...] + take(side)
+
+    def settle(self, a):
+        def one(k, carry):
+            for xy in self.others:
+                self.to_sib(a, xy, k).wait_send()
+            for g in range(2):
+                self.to_far(a, g, k).wait_send()
+            self.to_near(a, k).wait_send()
+
+            @pl.when(k < self.Z - 1)
+            def _():
+                self.onward(a, k).wait_send()
+            return carry
+        lax.fori_loop(0, self.Z, one, 0)
+
+
+def reduce_scratch(count, Z, shapes):
+    half, n, dma = count // 2, len(shapes), pltpu.SemaphoreType.DMA
+    bufs = [pltpu.VMEM(lead + s, bf16) for lead in ((count,), (half,), (2 * Z,), (Z,), (2, Z)) for s in shapes]
+    return bufs + [dma((n, half)), dma((n, half)), dma((n, 2 * Z)), dma((n, 2 * Z)), dma((n, Z)), dma((n, Z)),
+                   dma((n, Z)), dma((n, 2, Z))]
+
+
+def pack_tail(tail, low_share, experts, skip_row, dsmall_ref, dvec_ref, dskip_ref, drouter_ref, dnorm_ref, dmoe_ref):
+    blocks, share = tail.shape[:2]
+    room, width = dvec_ref.shape[0], drouter_ref.shape[0]
     vec = jnp.where(subs(dvec_ref.shape) == skip_row, dskip_ref[...], dvec_ref[...])
     line = subs((8, width))
     gains = jnp.where(line == 0, dnorm_ref[...], jnp.where(line == 1, dmoe_ref[...], 0.0))
@@ -362,118 +397,14 @@
     right = dot_tn(vec.astype(bf16), spot(room, 0, TILE)).reshape(blocks, share, TILE) + model
     tail[:, :, 0:TILE] = dsmall_ref[...].reshape(blocks, share, TILE)
     tail[:, :, TILE:] = right.astype(bf16)
-    for copies in first_sends + loads:
-        copies[2].start()
-
-    def total(bufs):
-        t = bufs[0][...].astype(jnp.float32)
-        for b in bufs[1:]:
-            t = t + b[...].astype(jnp.float32)
-        return t
-
-    for g, xy in enumerate(mine):
-        for k in range(Z):
-            zz = turn(k)
-            s = slot(xy, zz)
-            for cp in loads[g * Z + k]:
-                cp.wait()
-            take([sib_buf[a].at[s] for a in range(n)], lambda a: sib_sem.at[s, a])
-            parts = [[work[a].at[s], sib_buf[a].at[s]] for a in range(n)]
-            if g >= 2:
-                fs = (g - 2) * Z + zz
-                take([far_buf[a].at[fs] for a in range(n)], lambda a: far_sem.at[fs, a])
-                for a in range(n):
-                    parts[a].append(far_buf[a].at[fs])
-            if g == 3:
-                take([near_buf[a].at[zz] for a in range(n)], lambda a: near_sem.at[zz, a])
-                for a in range(n):
-                    parts[a].append(near_buf[a].at[zz])
-            if g < 3:
-                for a in range(n):
-                    work[a][s] = total(parts[a]).astype(jnp.bfloat16)
-                srcs = [work[a].at[s] for a in range(n)]
-                if g < 2:
-                    fs = g * Z + zz
-                    send(None, srcs, [far_buf[a].at[fs] for a in range(n)],
-                         lambda a: far_sem.at[fs, a], far)
-                else:
-                    send(None, srcs, [near_buf[a].at[zz] for a in range(n)],
-                         lambda a: near_sem.at[zz, a], near)
-                continue
-            if k < Z - 1:
-                rising = zz > z
-                side = jnp.where(rising, 0, 1)
-                more = jnp.where(rising, z, Z - 1 - z) > 0
-                line = [line_buf[a].at[side, zz] for a in range(n)]
-                for a in range(n):
-                    work[a][s] = total(parts[a]).astype(jnp.bfloat16)
-
-                @pl.when(more)
-                def _():
-                    take(line, lambda a: line_sem.at[side, zz, a])
-                    for a in range(n):
-                        work[a][s] = total([work[a].at[s], line[a]]).astype(jnp.bfloat16)
-                dev = (me.at()[0], jnp.where(rising, up[1], down[1]))
-                send(None, [work[a].at[s] for a in range(n)], line,
-                     lambda a: line_sem.at[side, zz, a], dev)
-            else:
-                for a in range(n):
-                    outs[a][...] = total(parts[a])
-                for side, pred in ((0, z > 0), (1, z < Z - 1)):
-                    @pl.when(pred)
-                    def _(side=side):
-                        line = [line_buf[a].at[side, zz] for a in range(n)]
-                        take(line, lambda a: line_sem.at[side, zz, a])
-                        for a in range(n):
-                            outs[a][...] = outs[a][...] + line[a][...].astype(jnp.float32)
-    pl.when(has_after)(halo.wait_recv)
-    pl.when(has_before)(halo.wait_send)
-    pl.when(jnp.logical_not(has_after))(blank.wait)
-    for pred, copies in sends:
-        for cp in copies:
-            cp.wait_send()
-
-
-def reduce_all(batch, seq, low_share, experts, skip_row, d_in, d_out, *rest):
-    count, Z, n = batch * seq, seq // 2, 3
-    wide = 2 * TILE
-    share = d_out.shape[0] // count
-    shapes = [(a.shape[0] // count,) + a.shape[1:] for a in (d_in, d_out)] + [(share, wide)]
-    edge = rest[-1].shape
-    half = count // 2
-    scratch = []
-    for lead in ((half,), (half,), (2 * Z,), (Z,), (2, Z)):
-        scratch += [pltpu.VMEM(lead + s, bf16) for s in shapes]
-    dma = pltpu.SemaphoreType.DMA
-    scratch += [
-        pltpu.VMEM((count, share, wide), bf16),
-        pltpu.VMEM(edge, f32),
-        dma((half, n)),
-        dma((half + 4 * Z, n)),
-        dma((half, n)),
-        dma((2 * Z, n)),
-        dma((Z, n)),
-        dma((2, Z, n)),
-        dma((3,)),
-    ]
-    return pl.pallas_call(
-        functools.partial(reduce_kernel, batch, seq, low_share, experts, skip_row),
-        out_shape=[jax.ShapeDtypeStruct(s, f32) for s in shapes] + [jax.ShapeDtypeStruct(edge, f32)],
-        in_specs=[HBM] * 2 + [VM] * 7,
-        out_specs=[VM] * 3 + [HBM],
-        scratch_shapes=scratch,
-        compiler_params=pltpu.CompilerParams(
-            collective_id=1, has_side_effects=True, vmem_limit_bytes=58 << 20),
-        name="reduce_grads",
-    )(d_in, d_out, *rest)
-
-
-def finish_kernel(dims, low_share, experts, in_ref, out_ref, tail_ref, halo_ref, tok_ref, block_ref, up_ref, up2_ref,
-                  down_ref, down2_ref, block_out, tok_out, din, dconv, dbias, dstate, dstep, dstep_bias, ddecay, dskip, dout, dnorm, dmoe,
+
+
+def finish_kernel(dims, low_share, experts, in_ref, out_ref, tail_ref, halo_ref, tok_ref, block_ref, up_ref,
+                  down_ref, block_out, tok_out, din, dconv, dbias, dstate, dstep, dstep_bias, ddecay, dskip, dout, dnorm, dmoe,
                   drouter, dup, ddown):
     seqs, rows, inner, states, rank, taps = dims
-    dup[...] = up_ref[...] + up2_ref[...].astype(f32)
-    ddown[...] = down_ref[...] + down2_ref[...].astype(f32)
+    dup[...] = up_ref[...]
+    ddown[...] = down_ref[...]
     block_out[...] = block_ref[...]
     tok_out[...] = tok_ref[...]
 
@@ -712,7 +643,6 @@
 WIDE = 256
 GROUP = 16
 LOG2E = math.log2(math.e)
-AHEAD = 256
 
 
 def conv_sum(ext_ref, s, cols, vec_ref, states, taps, rows):
@@ -948,7 +878,7 @@
 def return_kernel(dims, capacity, room, ret_ref, cot_ref, hid_ref, moe_ref, gate_ref, gated_ref, y_ref, u_ref, z_ref, dt_ref,
                   proj_ref, vec_ref, out_ref, gain_ref, router_ref, route_ref, slot_ref,
                   block_ref, ghid_ref, gy_ref, gz_ref, dout_ref, drouter_ref, dskip_ref, dgain_ref, adj_ref,
-                  hooks=QUIET):
+                  hooks=QUIET, out_grads=None):
     seqs, rows, inner, states, rank, taps = dims
     count = seqs * rows
     total, width = ret_ref.shape[0], hid_ref.shape[1]
@@ -971,9 +901,12 @@
     ghid_ref[...] = grad_hid
     branch = grad_hid.astype(jnp.bfloat16)
     hooks.activations()
+    if out_grads is not None:
+        out_grads(branch)
     for j in range(inner // WIDE):
         cols = slice(j * WIDE, (j + 1) * WIDE)
-        dout_ref[cols, :] = dot_tn(gated_ref[:, cols], branch).astype(jnp.bfloat16)
+        if out_grads is None:
+            dout_ref[cols, :] = dot_tn(gated_ref[:, cols], branch).astype(jnp.bfloat16)
         grad = dot_nt(branch, out_ref[cols, :])
         z = z_ref[:, cols]
         sig = sigmoid(z)
@@ -1006,7 +939,7 @@
 def back_kernel(dims, tok_ref, halo_ref, ext_ref, hist_ref, later_ref, gy_ref, gz_ref, ghid_ref, u_ref, dt_ref,
                 proj_ref, win_ref, small_ref, vec_ref, gain_ref,
                 dtok_ref, dhalo_ref, din_ref, dsmall_ref, dvec_ref, dgain_ref,
-                hbuf, ccol, bcol, gbsum, gcsum, adj, gdt, gu, gproj, gpad, gm, xn, gpre, sem, hooks=QUIET):
+                hbuf, ccol, bcol, gbsum, gcsum, adj, gdt, gu, gproj, gpad, gm, xn, gpre, sem, hooks=QUIET, in_grads=None):
     small_ref = small_ref.at[:, 0:TILE]
     seqs, rows, inner, states, rank, taps = dims
     count = seqs * rows
@@ -1042,6 +975,7 @@
             gbsum[t] = jnp.zeros((states, 128), f32)
             gcsum[t] = jnp.zeros((states, 128), f32)
         fetch(i, slot).wait()
+        hooks.group(i)
         for c0 in range(0, inner, strip):
             sls = [slice(c0 + k, c0 + k + 128) for k in range(0, strip, 128)]
             rates = [-jnp.exp(vec_ref[0:states, sl]) for sl in sls]
@@ -1138,10 +1072,15 @@
         dvec_ref[row : row + 1, cols] = bias_sum
         for k in range(taps):
             dvec_ref[states + k : states + k + 1, cols] = taps_sum[k]
-        zcols = slice(inner + j * WIDE, inner + (j + 1) * WIDE)
-        din_ref[:, cols] = dot_tn(xn[...], gm[:, cols]).astype(jnp.bfloat16)
-        din_ref[:, zcols] = dot_tn(xn[:count], gz_ref[:, cols]).astype(jnp.bfloat16)
-        hooks.columns(j)
+    if in_grads is None:
+        for j in range(inner // WIDE):
+            cols, zcols = (slice(at + j * WIDE, at + (j + 1) * WIDE) for at in (0, inner))
+            din_ref[:, cols] = dot_tn(xn[...], gm[:, cols]).astype(jnp.bfloat16)
+            din_ref[:, zcols] = dot_tn(xn[:count], gz_ref[:, cols]).astype(jnp.bfloat16)
+    else:
+        in_grads()
+    for j in range(inner // WIDE):
+        cols, zcols = (slice(at + j * WIDE, at + (j + 1) * WIDE) for at in (0, inner))
         gz = jnp.concatenate([gz_ref[:, cols], jnp.zeros((gm.shape[0] - count, WIDE), jnp.bfloat16)])
         grad_normed = grad_normed + dot_nt(gm[:, cols], win_ref[:, cols]) + dot_nt(gz, win_ref[:, zcols])
     gain_sum = 0.0
@@ -1164,63 +1103,62 @@
     return pltpu.CompilerParams(vmem_limit_bytes=mib << 20)
 
 
-def moe_kernel(seq, rows_ref, up_ref, down_ref, up2_ref, first_ref,
-               back_ref, land_ref, dup_ref, ddown_ref, dup2_ref, ddown2_ref,
-               xbuf, part, act, ghid, hid, gact, sib_buf, own_sum,
-               local_sem, disp_sem, pass_sem, recv_sem, load_sem, sib_send, sib_recv,
-               final_send, final_recv, final_local, down2_ref, cross_sem):
+def moe_kernel(seq, rows_ref, up_ref, down_ref,
+               back_ref, land_ref, dup_ref, ddown_ref,
+               xbuf, part, act, ghid, hid, gact, far_buf, own_sum, up2_ref, down2_ref, dup2, ddown2, dup3, ddown3,
+               local_sem, disp_sem, pass_sem, recv_sem, load_sem, far_send, far_recv,
+               final_send, final_recv, final_local, swap_send, swap_recv):
     me = Place(4, seq)
     b, s = me.at()
-    y, z, Z, c = me.y, me.z, me.Z, me.c
+    y, z, Z, x = me.y, me.z, me.Z, me.x
     cap, wide = rows_ref.shape[1], rows_ref.shape[2]
     width = wide // 2
     share = up_ref.shape[1]
     two = 2 * cap
     block = 2 * two
-    sib, nx = me.at(c=1 - c), me.at(x=1 - me.x)
+    sib, nx = me.at(c=1 - me.c), me.at(x=1 - x)
     greet([(None, sib), (None, nx)] + [(None, (b, (s + k) % seq)) for k in range(1, seq)])
 
     def remote(src, dst, send, recv, dev):
         return pltpu.make_async_remote_copy(
             src_ref=src, dst_ref=dst, send_sem=send, recv_sem=recv, device_id=dev, device_id_type=MESH)
 
-    def slab(cc, ss):
-        return land_ref.at[cc, pl.ds(pl.multiple_of(ss * cap, 8), cap)]
+    def slab(xx, ss):
+        return land_ref.at[xx, pl.ds(pl.multiple_of(ss * cap, 8), cap)]
 
     def there(k, j):
         return ((z + k) % Z) * 2 + j
 
-    def arrived(cc, ss):
-        remote(slab(cc, ss), slab(cc, ss), disp_sem.at[0], recv_sem.at[cc, ss], sib).wait_recv()
+    def arrived(xx, ss):
+        remote(slab(xx, ss), slab(xx, ss), disp_sem.at[0], recv_sem.at[xx, ss], nx).wait_recv()
 
     def hand(ss):
-        return remote(slab(c, ss), slab(c, ss), pass_sem.at[ss], recv_sem.at[c, ss], sib)
-
-    def load(k, cc):
+        return remote(slab(x, ss), slab(x, ss), pass_sem.at[ss], recv_sem.at[x, ss], nx)
+
+    def load(k, xx):
         zz = (z + k) % Z
         return pltpu.make_async_copy(
-            land_ref.at[cc, pl.ds(pl.multiple_of(zz * two, 8), two)],
-            xbuf.at[k, pl.ds(pl.multiple_of(cc * two, 16), two)], load_sem.at[k, cc])
+            land_ref.at[xx, pl.ds(pl.multiple_of(zz * two, 8), two)],
+            xbuf.at[k, pl.ds(pl.multiple_of(xx * two, 16), two)], load_sem.at[k, xx])
 
     def dispatch(k, j):
         to = ((z + Z - k) % Z) * 2 + j
-        return remote(rows_ref.at[to], slab(c, s), disp_sem.at[2 * k + j], recv_sem.at[c, s], (b, to))
+        return remote(rows_ref.at[to], slab(x, s), disp_sem.at[2 * k + j], recv_sem.at[x, s], (b, to))
 
     dispatch(0, 1 - y).start()
-    own = remote(rows_ref.at[s], slab(c, s), pass_sem.at[s], recv_sem.at[c, s], sib)
+    own = remote(rows_ref.at[s], slab(x, s), pass_sem.at[s], recv_sem.at[x, s], nx)
     own.start()
-    local = pltpu.make_async_copy(rows_ref.at[s], slab(c, s), local_sem)
+    local = pltpu.make_async_copy(rows_ref.at[s], slab(x, s), local_sem)
     local.start()
     for j in range(2):
         dispatch(1, j).start()
 
-    head = first_ref.shape[0]
-    if head < share:
-        rest = remote(down_ref.at[head:], down2_ref.at[head:], cross_sem.at[0], cross_sem.at[1], nx)
-        rest.start()
-    if head:
-        front = pltpu.make_async_copy(first_ref, down2_ref.at[0:head], cross_sem.at[2])
-        front.start()
+    def swap(i, src, dst):
+        return remote(src, dst, swap_send.at[i], swap_recv.at[i], sib)
+
+    weights = [swap(0, up_ref, up2_ref), swap(1, down_ref, down2_ref)]
+    for cp in weights:
+        cp.start()
     ups, downs = (up_ref, up2_ref), (down_ref, down2_ref)
 
     def compute(k):
@@ -1250,11 +1188,11 @@
                 dot_nt(ghid[mine, :share], up_ref[cols, :]) + dot_nt(ghid[mine, share:], up2_ref[cols, :])
             ).astype(bf16)
 
-    def of_core(k, cc):
-        return part.at[k, pl.ds(pl.multiple_of(cc * two, 16), two)]
-
-    def to_sib(k):
-        return remote(of_core(k, 1 - c), sib_buf.at[k], sib_send.at[k], sib_recv.at[k], sib)
+    def of_chip(k, xx):
+        return part.at[k, pl.ds(pl.multiple_of(xx * two, 16), two)]
+
+    def to_far(k):
+        return remote(of_chip(k, 1 - x), far_buf.at[k], far_send.at[k], far_recv.at[k], nx)
 
     def to_home(k, j):
         return remote(own_sum.at[k, j], back_ref.at[s], final_send.at[k, j], final_recv.at[s], (b, there(k, j)))
@@ -1265,41 +1203,39 @@
     def own_stage(k):
         @pl.when(k == 0)
         def _():
-            arrived(c, z * 2 + 1 - y)
+            arrived(x, z * 2 + 1 - y)
             hand(z * 2 + 1 - y).start()
             local.wait()
 
         @pl.when(k > 0)
         def _():
             for j in range(2):
-                arrived(c, there(k, j))
+                arrived(x, there(k, j))
                 hand(there(k, j)).start()
 
         @pl.when(k < Z - 2)
         def _():
             for j in range(2):
                 dispatch(k + 2, j).start()
-        load(k, c).start()
+        load(k, x).start()
 
     def compute_stage(k):
         for j in range(2):
-            arrived(1 - c, there(k, j))
-        load(k, 1 - c).start()
-        for cc in range(2):
-            load(k, cc).wait()
+            arrived(1 - x, there(k, j))
+        load(k, 1 - x).start()
+        for xx in range(2):
+            load(k, xx).wait()
 
         @pl.when(k == 0)
         def _():
-            if head < share:
-                rest.wait_recv()
-            if head:
-                front.wait()
+            for cp in weights:
+                cp.wait_recv()
         compute(k)
-        to_sib(k).start()
+        to_far(k).start()
 
     def home_stage(k):
-        to_sib(k).wait_recv()
-        total = of_core(k, c)[...].astype(f32) + sib_buf[k].astype(f32)
+        to_far(k).wait_recv()
+        total = of_chip(k, x)[...].astype(f32) + far_buf[k].astype(f32)
         for j in range(2):
             own_sum[k, j] = total[j * cap : (j + 1) * cap].astype(bf16)
 
@@ -1322,26 +1258,36 @@
             pl.when(jnp.logical_and(k >= 0, k < Z))(functools.partial(stage, k))
         return carry
     lax.fori_loop(0, Z + 2, step, 0)
-    for i, (dup, ddown) in enumerate(((dup2_ref, ddown2_ref), (dup_ref, ddown_ref))):
-        for n in range(0, share, WIDE):
-            at = (1 - i) * share + n
-            x, g = xbuf[:, :, :width].reshape(everything), xbuf[:, :, width:].reshape(everything)
-            ddown[n : n + WIDE, :] = dot_tn(act[:, at : at + WIDE], g).astype(ddown.dtype)
-            dup[:, n : n + WIDE] = dot_tn(x, ghid[:, at : at + WIDE]).astype(dup.dtype)
+    x_all = lambda: xbuf[:, :, :width].reshape(everything)
+    g_all = lambda: xbuf[:, :, width:].reshape(everything)
+    grads = [swap(2, dup2, dup3), swap(3, ddown2, ddown3)]
+    for n in range(0, share, WIDE):
+        dup2[:, n : n + WIDE] = dot_tn(x_all(), ghid[:, share + n : share + n + WIDE]).astype(bf16)
+    grads[0].start()
+    for n in range(0, share, WIDE):
+        ddown2[n : n + WIDE, :] = dot_tn(act[:, share + n : share + n + WIDE], g_all()).astype(bf16)
+    grads[1].start()
+    for n in range(0, share, WIDE):
+        dup_ref[:, n : n + WIDE] = dot_tn(x_all(), ghid[:, n : n + WIDE])
+        ddown_ref[n : n + WIDE, :] = dot_tn(act[:, n : n + WIDE], g_all())
+    grads[0].wait_recv()
+    dup_ref[...] += dup3[...].astype(f32)
+    grads[1].wait_recv()
+    ddown_ref[...] += ddown3[...].astype(f32)
+    for cp in weights + grads:
+        cp.wait_send()
 
     for k in range(1, seq):
         e = (s + k) % seq
         remote(back_ref.at[e], back_ref.at[e], disp_sem.at[0], final_recv.at[e], sib).wait_recv()
     keep_home().wait()
-    if head < share:
-        rest.wait_send()
     dispatch(0, 1 - y).wait_send()
     own.wait_send()
     hand(z * 2 + 1 - y).wait_send()
     to_home(0, 1 - y).wait_send()
 
     def settle(k, carry):
-        to_sib(k).wait_send()
+        to_far(k).wait_send()
 
         @pl.when(k > 0)
         def _():
@@ -1353,17 +1299,14 @@
     lax.fori_loop(0, Z, settle, 0)
 
 
-def cross(batch, *arrays):
-    return [lax.ppermute(a, "batch", [(i, (i + 2) % batch) for i in range(batch)]) for a in arrays]
-
-
-def moe_rows(batch, seq, sent, up, down, up2, down2):
+def moe_rows(batch, seq, sent, up, down):
     width, hidden_share = up.shape
     capacity, wide = sent.shape[1:]
     block = seq * capacity
     if tuned(batch, seq):
         Z, block = seq // 2, 4 * capacity
         dma = pltpu.SemaphoreType.DMA
+        quarter = [pltpu.VMEM((width, hidden_share), bf16), pltpu.VMEM((hidden_share, width), bf16)]
         out = pl.pallas_call(
             functools.partial(moe_kernel, seq),
             out_shape=[
@@ -1371,11 +1314,9 @@
                 like(2, seq * capacity, wide, dtype=bf16),
                 like(width, hidden_share),
                 like(hidden_share, width),
-                like(width, hidden_share, dtype=bf16),
-                like(hidden_share, width, dtype=bf16),
             ],
-            in_specs=[HBM] + [VM] * 4,
-            out_specs=[HBM, HBM] + [VM] * 4,
+            in_specs=[HBM] + [VM] * 2,
+            out_specs=[HBM, HBM] + [VM] * 2,
             scratch_shapes=[
                 pltpu.VMEM((Z, block, wide), bf16),
                 pltpu.VMEM((Z, block, wide), bf16),
@@ -1385,6 +1326,9 @@
                 pltpu.VMEM((block, 2 * hidden_share), f32),
                 pltpu.VMEM((Z, 2 * capacity, wide), bf16),
                 pltpu.VMEM((Z, 2, capacity, wide), bf16),
+                *quarter,
+                *quarter,
+                *quarter,
                 dma,
                 dma((2 * Z,)),
                 dma((seq,)),
@@ -1395,16 +1339,14 @@
                 dma((Z, 2)),
                 dma((seq,)),
                 dma,
-                pltpu.VMEM((hidden_share, width), bf16),
-                dma((3,)),
+                dma((4,)),
+                dma((4,)),
             ],
             compiler_params=pltpu.CompilerParams(
                 collective_id=2, has_side_effects=True, vmem_limit_bytes=56 << 20),
             name="experts",
-        )(sent, up, down, up2, down2)
-        back, _, d_up, d_down, d_up2, d_down2 = out
-        d_up2, d_down2 = cross(batch, d_up2, d_down2)
-        return back, d_up, d_down, d_up2, d_down2
+        )(sent, up, down)
+        return out[0], out[2], out[3]
     mine = lax.all_to_all(sent, "seq", split_axis=0, concat_axis=0, tiled=True)
     rows = lax.all_gather(mine, "batch", axis=0).reshape(batch * block, wide)
     part, d_up, d_down = pl.pallas_call(
@@ -1430,7 +1372,7 @@
     )(rows, up, down)
     part = part.reshape((batch,) + sent.shape)
     mine = lax.psum_scatter(part, "batch", scatter_dimension=0, tiled=False)
-    return lax.all_to_all(mine, "seq", split_axis=0, concat_axis=0, tiled=True), d_up, d_down, None, None
+    return lax.all_to_all(mine, "seq", split_axis=0, concat_axis=0, tiled=True), d_up, d_down
 
 
 class Moves:
@@ -1488,15 +1430,18 @@
     moves.wait_all()
 
 
-def backward_kernel(dims, capacity, room, seq,
+def backward_kernel(dims, share, low_share, experts, capacity, room, batch, seq,
                     ret_ref, cot_ref, hid_ref, moe_ref, gate_ref, vec_ref, gain_ref, router_ref, route_ref, slot_ref,
                     dsum_ref, proj_ref, gated_hbm, out_hbm, z_hbm, y_hbm, u_hbm, dt_hbm, ext_hbm, win_hbm, tail_hbm,
                     tok_hbm, halo_hbm, hist_ref,
-                    block_ref, dtok_ref, dhalo_ref, din_hbm, dout_hbm, dsmall_ref, dvec_ref, dnorm_ref, dmoe_ref,
-                    drouter_ref, dskip_ref,
-                    gated, out, z, y, u, dt, ext, win, tail, tok, halo, gy, gz, ghid, din, dout, adj, later,
-                    hbuf, ccol, bcol, gbsum, gcsum, carry, gdt, gu, gproj, gpad, gm, xn, gpre, sem, sems, *relay_refs):
-    inner = dims[2]
+                    block_ref, dtok_ref, next_ref, in_out, out_out, tail_out,
+                    gated, out, z, y, u, dt, ext, win, tail, tok, halo, gy, gz, ghid, adj, later,
+                    dhalo, dsmall, dvec, dnorm, dmoe, drouter, dskip, blank,
+                    hbuf, ccol, bcol, gbsum, gcsum, carry, gdt, gu, gproj, gpad, gm, xn, gpre, sem, sems, edge_sem,
+                    *more):
+    seqs, rows, inner, states, rank, taps = dims
+    count, devices = seqs * rows, batch * seq
+    relay_refs, more = more[:9], more[9:]
     moves = Moves(sems)
     for name, src, dst in (
         ("gated", gated_hbm, gated), ("out", out_hbm, out), ("z", z_hbm, z), ("y", y_hbm, y), ("u", u_hbm, u),
@@ -1504,32 +1449,76 @@
         ("tok", tok_hbm, tok), ("halo", halo_hbm, halo),
     ):
         moves.start(name, src, dst)
-    relay = Relay(seq, False, dims[3], dsum_ref, vec_ref, adj, later, *relay_refs)
-    greet(relay.peers())
-
-    def gradients():
-        moves.start("dout", dout, dout_hbm)
-        moves.wait("dt")
+    relay = Relay(seq, False, states, dsum_ref, vec_ref, adj, later, *relay_refs)
+    reducer = Reducer(batch, seq, *(more[3 * i : 3 * i + 3] for i in range(5)), more[15:])
+    OUT, IN, REST = range(3)
+    b, s = reducer.me.at()
+    has_before, has_after = s > 0, s < seq - 1
+    greet(reducer.peers() + [(has_before, (b, s - 1)), (has_after, (b, s + 1))])
+
+    def out_grads(branch):
+        cut = 8 * share
+        for q in range(devices // 8):
+            part = dot_tn(gated[:, q * cut : (q + 1) * cut], branch)
+            reducer.items[OUT][q * 8 : (q + 1) * 8] = part.astype(bf16).reshape(8, share, part.shape[1])
+        reducer.give(OUT, reducer.others)
 
     return_kernel(dims, capacity, room, ret_ref, cot_ref, hid_ref, moe_ref, gate_ref, gated, y, u, z, dt, proj_ref,
                   vec_ref, out, gain_ref, router_ref, route_ref, slot_ref,
-                  block_ref, ghid, gy, gz, dout, drouter_ref, dskip_ref, dmoe_ref, adj,
-                  hooks=Hooks(activations=lambda: moves.wait("gated", "out", "z", "y", "u"), gradients=gradients,
-                              scanned=relay.start))
+                  block_ref, ghid, gy, gz, None, drouter, dskip, dmoe, adj,
+                  hooks=Hooks(activations=lambda: moves.wait("gated", "out", "z", "y", "u"),
+                              gradients=lambda: moves.wait("dt"), scanned=relay.start),
+                  out_grads=out_grads)
     for i in range(relay.count):
         relay.finish(i)
 
-    def columns(j):
-        for base in (0, inner):
-            cols = pl.ds(base + j * WIDE, WIDE)
-            moves.start("din", din.at[:, cols], din_hbm.at[:, cols])
+    def group(i):
+        for g in range(4):
+            pl.when(i // reducer.Z == g)(functools.partial(reducer.step, OUT, g, i % reducer.Z))
+
+    def in_grads():
+        half, cut = devices // 2, low_share * devices // 2
+        wide = 2 * WIDE
+
+        def fill(xx):
+            at = pl.ds(pl.multiple_of(xx * cut, 128), cut)
+            items = pl.ds(xx * half, half)
+            for base, grads, n in ((0, gm, count + 8 * seqs), (inner, gz, count)):
+                for c0 in range(0, inner, wide):
+                    part = dot_tn(xn[0:n, at], grads[:, c0 : c0 + wide]).reshape(half, low_share, wide)
+                    reducer.items[IN][items, :, base + c0 : base + c0 + wide] = part.astype(bf16)
+
+        me = reducer.me
+        for xx in (1 - me.x, me.x):
+            fill(xx)
+            reducer.give(IN, [(xx, 1 - me.y), (xx, me.y)])
 
     back_kernel(dims, tok, halo, ext, hist_ref, later, gy, gz, ghid, u, dt, proj_ref, win, tail, vec_ref, gain_ref,
-                dtok_ref, dhalo_ref, din, dsmall_ref, dvec_ref, dnorm_ref,
+                dtok_ref, dhalo, None, dsmall, dvec, dnorm,
                 hbuf, ccol, bcol, gbsum, gcsum, carry, gdt, gu, gproj, gpad, gm, xn, gpre, sem,
-                hooks=Hooks(rest=lambda: moves.wait("ext", "win", "tail", "tok", "halo"), columns=columns))
+                hooks=Hooks(rest=lambda: moves.wait("ext", "win", "tail", "tok", "halo"), group=group),
+                in_grads=in_grads)
+    edge = reducer.copy(dhalo, next_ref, edge_sem.at[0], edge_sem.at[1], (b, s - 1))
+    none = pltpu.make_async_copy(blank, next_ref, edge_sem.at[2])
+    blank[...] = jnp.zeros_like(blank)
+    pl.when(has_before)(edge.start)
+    pl.when(jnp.logical_not(has_after))(none.start)
+    pack_tail(reducer.items[REST], low_share, experts, states + taps + 2, dsmall, dvec, dskip, drouter, dnorm, dmoe)
+    reducer.give(REST, reducer.others)
+    for t in range(reducer.Z + 2):
+        for g, k in ((0, t), (1, t), (2, t - 1), (3, t - 2)):
+            if 0 <= k < reducer.Z:
+                for a in (IN, REST):
+                    reducer.step(a, g, k)
+                if g == 3:
+                    for a, ref in ((IN, in_out), (REST, tail_out), (OUT, out_out)):
+                        reducer.line(a, k, ref)
     relay.settle()
-    moves.wait_all()
+    for a in (OUT, IN, REST):
+        reducer.settle(a)
+    pl.when(has_after)(edge.wait_recv)
+    pl.when(has_before)(edge.wait_send)
+    pl.when(jnp.logical_not(has_after))(none.wait)
 
 
 def body(
@@ -1591,8 +1580,6 @@
         in_full, out_full, tail_full = (
             lax.all_gather(a, both, axis=0, tiled=True) for a in (in_proj, out_proj, tail)
         )
-    up, down, tail_full = lax.optimization_barrier((expert_up[0], expert_down[0], tail_full))
-    up2, down2 = cross(batch, up, down[:AHEAD]) if fast else (None, None)
     tok, cot = tokens.reshape(count, width), cotangent.reshape(count, width)
     size = GROUP * states
     total = experts * capacity
@@ -1669,24 +1656,26 @@
             name="leave",
         )(tok, cot, before, dt, u, z, proj, vec, out_full, gain, router, routes, slot_index)
 
-    back, d_up, d_down, d_up2, d_down2 = moe_rows(
-        batch, seq, sent.reshape(experts, capacity, 2 * width), up, down, up2, down2)
+    back, d_up, d_down = moe_rows(
+        batch, seq, sent.reshape(experts, capacity, 2 * width), expert_up[0], expert_down[0])
     back = back.reshape(total, 2 * width)
 
     if fast:
-        (block_out, d_tok, d_halo, d_in, d_out, d_small, d_vec, d_norm, d_moe, d_router, d_skip) = pl.pallas_call(
-            partial(backward_kernel, dims, capacity, room, seq),
-            out_shape=[moe_s, tok_s, halo_s, din_s, dout_s, dsmall_s, vec_s, dgain_s, dgain_s, drouter_s, dskip_s],
+        own = [(share, width), (low_share, 2 * inner), (share, 2 * tile)]
+        block_out, d_tok, from_next, s_in, s_out, s_tail = pl.pallas_call(
+            partial(backward_kernel, dims, share, low_share, experts, capacity, room, batch, seq),
+            out_shape=[moe_s, tok_s, halo_s, like(*own[1]), like(*own[0]), like(*own[2])],
             in_specs=[VM] * 12 + [HBM] * 12,
-            out_specs=[VM] * 3 + [HBM] * 2 + [VM] * 6,
+            out_specs=[VM] * 2 + [HBM] + [VM] * 3,
             scratch_shapes=[
                 vmem(low_s), vmem(out_full), vmem(acts), vmem(acts), vmem(acts), vmem(acts), vmem(ext_s), vmem(in_full),
-                vmem(tail_full), vmem(tok), vmem(halo), vmem(acts), vmem(low_s), vmem(tok_s), vmem(din_s), vmem(dout_s),
-                vmem(state_s), vmem(state_s), *back_scratch, dma((2 * wide + 12,)),
-                *relay_scratch(seqs, states, inner),
+                vmem(tail_full), vmem(tok), vmem(halo), vmem(acts), vmem(low_s), vmem(tok_s), vmem(state_s),
+                vmem(state_s), vmem(halo_s), vmem(dsmall_s), vmem(vec_s), vmem(dgain_s), vmem(dgain_s),
+                vmem(drouter_s), vmem(dskip_s), vmem(halo_s), *back_scratch, dma((12,)), dma((3,)),
+                *relay_scratch(seqs, states, inner), *reduce_scratch(devices, seq // 2, own),
             ],
             compiler_params=pltpu.CompilerParams(
-                collective_id=4, has_side_effects=True, vmem_limit_bytes=60 << 20),
+                collective_id=4, has_side_effects=True, vmem_limit_bytes=62 << 20),
             name="backward",
         )(back, cot, hid, moe_in, gate, vec, gain, router, routes, slot_index, dsum, proj,
           gated, out_full, z, y, u, dt, ext, in_full, tail_full, tok, halo, hist)
@@ -1712,9 +1701,6 @@
 
     skip_row = states + taps + 2
     if fast:
-        s_in, s_out, s_tail, from_next = reduce_all(
-            batch, seq, low_share, experts, skip_row, d_in, d_out, d_small, d_vec, d_skip, d_router, d_norm, d_moe,
-            d_halo)
         steps = 4
         slab = lambda a: pl.BlockSpec((a.shape[0] // steps, a.shape[1]), lambda i: (i, 0))
         whole = lambda *shape: pl.BlockSpec(shape, lambda i: (0,) * len(shape))
@@ -1728,12 +1714,12 @@
             out_shape=[like(*tokens.shape, dtype=bf16), like(*tokens.shape)] + [like(*a) for a in shapes] + [like(*d_up.shape), like(*d_down.shape)],
             grid=(steps,),
             in_specs=[whole(*s_in.shape), whole(*s_out.shape), whole(*s_tail.shape), whole(seqs, 8, width), piece, piece]
-            + [slab(a) for a in (d_up, d_up2, d_down, d_down2)],
+            + [slab(a) for a in (d_up, d_down)],
             out_specs=[piece, piece] + [whole(*a) for a in shapes] + [slab(d_up), slab(d_down)],
             compiler_params=params(),
             name="finish",
         )(s_in, s_out, s_tail, from_next.reshape(seqs, 8, width), d_tok.reshape(tokens.shape),
-          block_out.reshape(tokens.shape), d_up, d_up2, d_down, d_down2)
+          block_out.reshape(tokens.shape), d_up, d_down)
         for i in (2, 5, 7, 9, 10):
             sums[i] = sums[i][0]
         sums[11] = sums[11].T

time: 292 us -> 264 us (0.904)
  Pallas kernels: 283 us -> 263 us
  starting transfers between devices: 4.25 us -> 0 us
  local copies, waits for them, and re-layouts: 3.52 us -> 0 us
    pallas_call x2 -> x1, Pallas kernels: 131 us -> 97.8 us  [body(): pl.pallas_call(partial(backward_kernel, dims, share, low_share, experts,...]
    pallas_call x1, Pallas kernels: 65.9 us -> 79.8 us  [moe_rows(): pl.pallas_call(functools.partial(moe_kernel, seq), out_shape=[like(seq, c...]
    ppermute x4 -> x0, starting transfers between devices: 4.25 us -> none  [cross(): lax.ppermute(a, 'batch', [(i, (i + 2) % batch) for i in range(batch)])]
  transfers between devices with their start and end apart: 4 -> 0, of which waited for: 0 -> 0; matrix products, arithmetic and copies ran while one was open for 0% -> 0% of each run, Pallas kernels for 57% -> 0%
where the time goes in v2:
time: 264 us
  Pallas kernels  263 us (100%)
    pallas_call x1, Pallas kernels, body(): pl.pallas_call(partial(backward_kernel, dims, share, low_share, experts,...  97.8 us
    pallas_call x1, Pallas kernels, moe_rows(): pl.pallas_call(functools.partial(moe_kernel, seq), out_shape=[like(seq, c...  79.8 us
    pallas_call x1, Pallas kernels, gather_all(): pl.pallas_call(functools.partial(gather_kernel, batch, seq), out_shape=[j...  43.6 us
    pallas_call x1, Pallas kernels, body(): pl.pallas_call(partial(forward_kernel, dims, share, low_share, experts, c...  35.1 us
    pallas_call x1, Pallas kernels, body(): pl.pallas_call(partial(finish_kernel, dims, low_share, experts), out_shap...  6.44 us

profile of v2, /device:TPU:0, one launch (start us, length us, event | category | flops | bytes accessed | tf_op | source)
XLA Modules:
  0.0 263.6 jit_solution(12452341965511995071)
XLA Ops:
  0.7 43.6 %gather_weights.1 = (bf16[768,3072]{1,0:T(8,128)(2,1)}, bf16[1536,768]{1,0:T(8,128)(2,1)}, bf16[1536,256]{1,0:T(8,128)(2,1)}, bf16[2,8,768]{2,1,0:T(8,128)(2,1)}) custom-call(bf16[24,3072]{1,0:T(8,128)(2,1)} %refs_0_.1, bf16[48,768]{1,0:T(8,128)(2,1)} %refs_1_.1, bf16[2,128,768]{2,1,0:T(8,128)(2,1)} %refs_2_.1, bf16[48,80]{1,0:T(8,128)(2,1)} %refs_3_.1, ...), custom_call_target="tpu_custom_call" | custom-call | tf_op jit(solution)/shard_map/gather_weights/pallas_call | solution.py:230
  44.3 35.1 %forward.1 = (f32[2,136,1536]{2,1,0:T(8,128)}, f32[256,1536]{1,0:T(8,128)}, f32[256,1536]{1,0:T(8,128)}, f32[256,1536]{1,0:T(8,128)}, f32[256,1536]{1,0:T(8,128)...) custom-call(bf16[256,768]{1,0:T(8,128)(2,1)} %bitcast.24, ...), custom_call_target="tpu_custom_call" | custom-call | tf_op jit(solution)/shard_map/forward/pallas_call | solution.py:1619
  79.3 79.8 %experts.1 = (bf16[8,40,1536]{2,1,0:T(8,128)(2,1)}, bf16[2,320,1536]{2,1,0:T(8,128)(2,1)}, f32[768,768]{1,0:T(8,128)}, f32[768,768]{1,0:T(8,128)}) custom-call(bf16[8,40,1536]{2,1,0:T(8,128)(2,1)} %bitcast.31, bf16[768,768]{1,0:T(8,128)(2,1)} %bitcast.28, bf16[768,768]{1,0:T(8,128)(2,1)} %bitcast.29), custom_call_target="tpu_custom_call" | custom-call | tf_op jit(solution)/shard_map/experts/pallas_call | solution.py:1310
  159.2 97.8 %backward.1 = (bf16[256,768]{1,0:T(8,128)(2,1)}, f32[256,768]{1,0:T(8,128)}, f32[16,768]{1,0:T(8,128)}, f32[24,3072]{1,0:T(8,128)}, f32[48,768]{1,0:T(8,128)}, /*index=5*/f32[48,256]{1,0:T(8,128)}) custom-call(bf16[320,1536]{1,0:T(8,128)(2,1)} %bitcast.30, bf16[256,768]{1,0:T(8,128)(2,1)} %bitcast.27, f32[256,768]{1,0:T(8,128)} %get-tuple-element.67.hid_ref, ...), custom_call_target="tpu_custom_call" | custom-call | tf_op jit(solution)/shard_map/backward/pallas_call | solution.py:1665
  256.9 6.4 %finish.1 = (bf16[2,128,768]{2,1,0:T(8,128)(2,1)}, f32[2,128,768]{2,1,0:T(8,128)}, f32[24,3072]{1,0:T(8,128)}, f32[4,48]{1,0:T(4,128)}, f32[1,48]{1,0:T(1,128)},...) custom-call(f32[24,3072]{1,0:T(8,128)} %get-tuple-element.82.in_ref,, ...), custom_call_target="tpu_custom_call" | custom-call | tf_op jit(solution)/shard_map/finish/pallas_call | solution.py:1712

commit v3 on v2

--- a/solution.py
+++ b/solution.py
@@ -55,95 +55,105 @@
     return (lanes((rows, width)) == subs((rows, width)) + at).astype(bf16)
 
 
-def gather_kernel(batch, seq, *refs):
-    n_arrays = 3
-    in_ref, out_ref, tok_ref, state_ref, step_ref, router_ref = refs[:6]
-    lines, gains = refs[6:11], refs[11:13]
-    outs, halo_ref = refs[13:16], refs[16]
-    tail, vecs, feats, zeros, local_sem, send_sem, recv_sem, halo_sem = refs[17:]
-    ins = [in_ref, out_ref, tail]
-    me = Place(batch, seq)
-    Z, z = me.Z, me.z
-    rows = [r.shape[0] for r in ins]
-    sib = me.at(c=1 - me.c)
-    up_ok, down_ok = z < Z - 1, z > 0
-    up, down = me.at(z=z + 1), me.at(z=z - 1)
-    nx, ny = me.at(x=1 - me.x), me.at(y=1 - me.y)
-    first = me.c == 0
-    nb2 = tuple(jnp.where(first, a, b) for a, b in zip(ny, nx))
-    nb3 = tuple(jnp.where(first, a, b) for a, b in zip(nx, ny))
-    x2, y2 = jnp.where(first, me.x, 1 - me.x), jnp.where(first, 1 - me.y, me.y)
-    x3, y3 = jnp.where(first, 1 - me.x, me.x), jnp.where(first, me.y, 1 - me.y)
-    b, part_of = me.at()
-    has_before, has_after = part_of > 0, part_of < seq - 1
-    before, after = (b, part_of - 1), (b, part_of + 1)
-    greet([(None, sib), (None, nx), (None, ny), (up_ok, up), (down_ok, down), (has_before, before), (has_after, after)])
-    own = me.index(me.at())
-
-    def part(a, index):
-        return outs[a].at[pl.ds(pl.multiple_of(index * rows[a], 8), rows[a])]
-
-    sends = []
-
-    def send(pred, index, dev, mine=False):
-        slot = len(sends)
-        copies = []
-        for a in range(n_arrays):
-            copies.append(
-                pltpu.make_async_remote_copy(
-                    src_ref=ins[a] if mine else part(a, index),
-                    dst_ref=part(a, index),
-                    send_sem=send_sem.at[slot, a],
-                    recv_sem=recv_sem.at[index, a],
-                    device_id=dev,
-                    device_id_type=MESH,
-                )
-            )
-
-        def go(copies):
-            def start():
-                for cp in copies:
-                    cp.start()
-            if pred is None:
-                start()
-            else:
-                pl.when(pred)(start)
-        if mine:
-            go(copies[:2])
-            later.append(lambda: go(copies[2:]))
+class Gatherer:
+    def __init__(self, batch, seq, ins, outs, send_sem, recv_sem):
+        self.ins, self.outs, self.send_sem, self.recv_sem = ins, outs, send_sem, recv_sem
+        self.me = me = Place(batch, seq)
+        self.Z, self.z = me.Z, me.z
+        self.sib = me.at(c=1 - me.c)
+        self.up_ok, self.down_ok = me.z < me.Z - 1, me.z > 0
+        self.up, self.down = me.at(z=me.z + 1), me.at(z=me.z - 1)
+        self.nx, self.ny = me.at(x=1 - me.x), me.at(y=1 - me.y)
+        first = me.c == 0
+        pick = lambda a, b: tuple(jnp.where(first, p, q) for p, q in zip(a, b))
+        self.second_dev, self.third_dev = pick(self.ny, self.nx), pick(self.nx, self.ny)
+        ox, oy = 1 - me.x, 1 - me.y
+        self.second_at = (jnp.where(first, me.x, ox), jnp.where(first, oy, me.y))
+        self.third_at = (jnp.where(first, ox, me.x), jnp.where(first, me.y, oy))
+        self.across_at = (ox, oy)
+        self.own = me.index(me.at())
+        self.sends = [[] for _ in ins]
+
+    def peers(self):
+        return [(None, self.sib), (None, self.nx), (None, self.ny), (self.up_ok, self.up), (self.down_ok, self.down)]
+
+    def part(self, a, index):
+        rows = self.ins[a].shape[0]
+        return self.outs[a].at[pl.ds(pl.multiple_of(index * rows, 8), rows)]
+
+    def send(self, a, pred, src, index, dev):
+        copy = pltpu.make_async_remote_copy(
+            src_ref=src, dst_ref=self.part(a, index), send_sem=self.send_sem.at[a, len(self.sends[a])],
+            recv_sem=self.recv_sem.at[a, index], device_id=dev, device_id_type=MESH)
+        self.sends[a].append((pred, copy))
+        if pred is None:
+            copy.start()
         else:
-            go(copies)
-        sends.append((pred, copies))
-
-    def arrive(pred, index, targets):
-        def wait():
-            for a in range(n_arrays):
-                pltpu.make_async_remote_copy(
-                    src_ref=part(a, index), dst_ref=part(a, index),
-                    send_sem=send_sem.at[0, a], recv_sem=recv_sem.at[index, a],
-                    device_id=sib, device_id_type=MESH,
-                ).wait_recv()
+            pl.when(pred)(copy.start)
+
+    def give(self, a):
+        for pred, dev in self.targets():
+            self.send(a, pred, self.ins[a], self.own, dev)
+
+    def targets(self):
+        return [(self.up_ok, self.up), (self.down_ok, self.down), (None, self.second_dev), (None, self.third_dev),
+                (None, self.sib)]
+
+    def arrive(self, a, pred, index, targets):
+        part = self.part(a, index)
+        copy = pltpu.make_async_remote_copy(
+            src_ref=part, dst_ref=part, send_sem=self.send_sem.at[a, 0], recv_sem=self.recv_sem.at[a, index],
+            device_id=self.sib, device_id_type=MESH)
         if pred is None:
-            wait()
+            copy.wait_recv()
         else:
-            pl.when(pred)(wait)
+            pl.when(pred)(copy.wait_recv)
         for extra, dev in targets:
             p = pred if extra is None else (extra if pred is None else jnp.logical_and(pred, extra))
-            send(p, index, dev)
-
-    later = []
-    for dev, pred in ((up, up_ok), (down, down_ok), (nb2, None), (nb3, None), (sib, None)):
-        send(pred, own, dev, mine=True)
-    seqs, rows_here = tok_ref.shape[:2]
-    edge = pl.ds(rows_here - 8, 8)
-    halo = pltpu.make_async_remote_copy(
-        src_ref=tok_ref.at[:, edge], dst_ref=halo_ref, send_sem=halo_sem.at[0], recv_sem=halo_sem.at[1],
-        device_id=after, device_id_type=MESH)
-    blank = pltpu.make_async_copy(zeros, halo_ref, halo_sem.at[2])
-    zeros[...] = jnp.zeros_like(zeros)
-    pl.when(has_after)(halo.start)
-    pl.when(jnp.logical_not(has_before))(blank.start)
-
+            self.send(a, p, part, index, dev)
+
+    def offsets(self, k):
+        return [(None, 0)] if k == 0 else [(self.z >= k, -k), (self.z + k < self.Z, k)]
+
+    def hop(self, arrays, h):
+        me, z = self.me, self.z
+        to_second, to_third, to_sib = (None, self.second_dev), (None, self.third_dev), (None, self.sib)
+        for k, at, targets in (
+            (h, (me.x, me.y), None), (h - 1, self.second_at, [to_third, to_sib]), (h - 2, self.third_at, [to_sib]),
+            (h - 3, self.across_at, [to_sib]),
+        ):
+            if not 0 <= k < self.Z or (targets is None and k == 0):
+                continue
+            for pred, off in self.offsets(k):
+                onward = targets
+                if targets is None:
+                    onward = [(self.up_ok, self.up) if off < 0 else (self.down_ok, self.down), to_second, to_third, to_sib]
+                for a in arrays:
+                    self.arrive(a, pred, me.index(me.at(x=at[0], y=at[1], z=z + off)), onward)
+
+    def rest(self, arrays):
+        me = self.me
+        for h in range(self.Z):
+            for xx in (0, 1):
+                for yy in (0, 1):
+                    for pred, off in self.offsets(h):
+                        for a in arrays:
+                            self.arrive(a, pred, me.index(me.at(x=xx, y=yy, c=1 - me.c, z=self.z + off)), [])
+
+    def settle(self):
+        for sends in self.sends:
+            for pred, copy in sends:
+                if pred is None:
+                    copy.wait_send()
+                else:
+                    pl.when(pred)(copy.wait_send)
+
+
+def n_sends(Z):
+    return 5 + (Z - 1) * 8 + (2 * Z - 1) * 2 + (2 * Z - 1) * 2
+
+
+def pack_weights(tail, vecs, feats, state_ref, step_ref, router_ref, lines, gains):
     share, low_share, experts = state_ref.shape[0], router_ref.shape[1], router_ref.shape[0]
     rank, room, wide = step_ref.shape[0], vecs.shape[0], tail.shape[1]
     vecs[...] = jnp.zeros_like(vecs)
@@ -163,90 +173,6 @@
         feats[...].astype(bf16), spot(feats.shape[0], TILE + room + experts, wide))
     by_feature = jnp.concatenate([by_feature, jnp.zeros((share - low_share, wide), f32)])
     tail[...] = (by_channel + by_feature).astype(bf16)
-    for start in later:
-        start()
-    local = [pltpu.make_async_copy(ins[a], part(a, own), local_sem.at[a]) for a in range(n_arrays)]
-    for cp in local:
-        cp.start()
-
-    def offsets(k):
-        return [(None, 0)] if k == 0 else [(z >= k, -k), (z + k < Z, k)]
-
-    def col(k):
-        for pred, off in offsets(k):
-            fwd = (up_ok, up) if off < 0 else (down_ok, down)
-            arrive(pred, me.index(me.at(z=z + off)), [fwd, (None, nb2), (None, nb3), (None, sib)])
-
-    def second(k):
-        for pred, off in offsets(k):
-            arrive(pred, me.index(me.at(x=x2, y=y2, z=z + off)), [(None, nb3), (None, sib)])
-
-    def third(k):
-        for pred, off in offsets(k):
-            arrive(pred, me.index(me.at(x=x3, y=y3, z=z + off)), [(None, sib)])
-
-    def fourth(k):
-        for pred, off in offsets(k):
-            arrive(pred, me.index(me.at(x=1 - me.x, y=1 - me.y, z=z + off)), [(None, sib)])
-
-    for h in range(1, Z + 3):
-        if h < Z:
-            col(h)
-        if 0 <= h - 1 < Z:
-            second(h - 1)
-        if 0 <= h - 2 < Z:
-            third(h - 2)
-        if 0 <= h - 3 < Z:
-            fourth(h - 3)
-    for h in range(Z):
-        for xx in (0, 1):
-            for yy in (0, 1):
-                for pred, off in offsets(h):
-                    arrive(pred, me.index(me.at(x=xx, y=yy, c=1 - me.c, z=z + off)), [])
-    for cp in local:
-        cp.wait()
-    pl.when(has_before)(halo.wait_recv)
-    pl.when(has_after)(halo.wait_send)
-    pl.when(jnp.logical_not(has_before))(blank.wait)
-    for pred, copies in sends:
-        def done(copies=copies):
-            for cp in copies:
-                cp.wait_send()
-        if pred is None:
-            done()
-        else:
-            pl.when(pred)(done)
-
-
-def n_sends(Z):
-    return 5 + (Z - 1) * 8 + (2 * Z - 1) * 2 + (2 * Z - 1) * 2
-
-
-def gather_all(batch, seq, room, in_proj, out_proj, tokens, state, step, router, lines, gains):
-    count, share = batch * seq, out_proj.shape[0]
-    seqs, _, width = tokens.shape
-    wide = 2 * TILE
-    edge = (seqs, 8, width)
-    return pl.pallas_call(
-        functools.partial(gather_kernel, batch, seq),
-        out_shape=[
-            jax.ShapeDtypeStruct((count * a.shape[0],) + a.shape[1:], bf16) for a in (in_proj, out_proj)
-        ] + [jax.ShapeDtypeStruct((count * share, wide), bf16), jax.ShapeDtypeStruct(edge, bf16)],
-        in_specs=[HBM] * 3 + [VM] * (3 + len(lines) + len(gains)),
-        out_specs=[HBM] * 4,
-        scratch_shapes=[
-            pltpu.VMEM((share, wide), bf16),
-            pltpu.VMEM((room, share), f32),
-            pltpu.VMEM((8, router.shape[1]), f32),
-            pltpu.VMEM(edge, bf16),
-            pltpu.SemaphoreType.DMA((3,)),
-            pltpu.SemaphoreType.DMA((n_sends(seq // 2), 3)),
-            pltpu.SemaphoreType.DMA((count, 3)),
-            pltpu.SemaphoreType.DMA((3,)),
-        ],
-        compiler_params=pltpu.CompilerParams(collective_id=0, has_side_effects=True),
-        name="gather_weights",
-    )(in_proj, out_proj, tokens, state, step, router, *lines, *gains)
 
 
 class Reducer:
@@ -399,41 +325,47 @@
     tail[:, :, TILE:] = right.astype(bf16)
 
 
-def finish_kernel(dims, low_share, experts, in_ref, out_ref, tail_ref, halo_ref, tok_ref, block_ref, up_ref,
-                  down_ref, block_out, tok_out, din, dconv, dbias, dstate, dstep, dstep_bias, ddecay, dskip, dout, dnorm, dmoe,
-                  drouter, dup, ddown):
+def finish_kernel(dims, low_share, experts, tail_ref, halo_ref, in_ref, out_ref, block_hbm, tok_hbm, up_hbm, down_hbm,
+                  block_out, tok_out, din, dconv, dbias, dstate, dstep, dstep_bias, ddecay, dskip, dout, dnorm, dmoe,
+                  drouter, dup, ddown, block, tok, up, down, sems):
     seqs, rows, inner, states, rank, taps = dims
-    dup[...] = up_ref[...]
-    ddown[...] = down_ref[...]
-    block_out[...] = block_ref[...]
-    tok_out[...] = tok_ref[...]
-
-    @pl.when(pl.program_id(0) == pl.num_programs(0) - 1)
-    def _():
-        tok_out[:, tok_ref.shape[1] - 8 :] = tok_ref[:, tok_ref.shape[1] - 8 :] + halo_ref[...]
-
-    @pl.when(pl.program_id(0) == 0)
-    def _():
-        din[...] = in_ref[...]
-        dout[...] = out_ref[...]
-        tail = tail_ref[...]
-        share, wide = tail.shape
-        eye = (lanes((wide, wide)) == subs((wide, wide))).astype(f32)
-        turned = lax.dot_general(
-            eye, tail, (((1,), (1,)), ((), ())), precision=lax.Precision.HIGHEST, preferred_element_type=f32)
-        dstate[...] = tail[:, : rank + 2 * states]
-        dstep[...] = turned[TILE - rank : TILE]
-        ddecay[...] = turned[TILE : TILE + states]
-        dconv[...] = turned[TILE + states : TILE + states + taps]
-        at = TILE + states + taps
-        dbias[...] = turned[at : at + 1]
-        dstep_bias[...] = turned[at + 1 : at + 2]
-        dskip[...] = turned[at + 2 : at + 3]
-        at = TILE + -(-(states + taps + 3) // 8) * 8
-        drouter[...] = turned[at : at + experts, :low_share]
-        at += experts
-        dnorm[...] = turned[at : at + 1, :low_share]
-        dmoe[...] = turned[at + 1 : at + 2, :low_share]
+    moves = Moves(sems)
+    routes = []
+    for i in range(4):
+        for src, at, dst in ((up_hbm, up, dup), (down_hbm, down, ddown)):
+            n = src.shape[0] // 4
+            piece = pl.ds(i * n, n)
+            routes.append((len(routes), src.at[piece], at.at[piece], dst.at[piece]))
+    routes.append(("tok", tok_hbm, tok, tok_out))
+    routes.append(("block", block_hbm, block, block_out))
+    for name, src, at, _ in routes:
+        moves.start(name, src, at)
+    din[...] = in_ref[...]
+    dout[...] = out_ref[...]
+    tail = tail_ref[...]
+    wide = tail.shape[1]
+    eye = (lanes((wide, wide)) == subs((wide, wide))).astype(bf16)
+    high = tail.astype(bf16)
+    turned = dot_nt(eye, high) + dot_nt(eye, (tail - high.astype(f32)).astype(bf16))
+    dstate[...] = tail[:, : rank + 2 * states]
+    dstep[...] = turned[TILE - rank : TILE]
+    ddecay[...] = turned[TILE : TILE + states]
+    dconv[...] = turned[TILE + states : TILE + states + taps]
+    at = TILE + states + taps
+    dbias[...] = turned[at : at + 1]
+    dstep_bias[...] = turned[at + 1 : at + 2]
+    dskip[...] = turned[at + 2 : at + 3]
+    at = TILE + -(-(states + taps + 3) // 8) * 8
+    drouter[...] = turned[at : at + experts, :low_share]
+    at += experts
+    dnorm[...] = turned[at : at + 1, :low_share]
+    dmoe[...] = turned[at + 1 : at + 2, :low_share]
+    for name, _, at, dst in routes:
+        moves.wait(name)
+        if name == "tok":
+            tok[:, rows - 8 :] = tok[:, rows - 8 :] + halo_ref[...]
+        moves.start("out", at, dst)
+    moves.wait_all()
 
 
 def tuned(batch, seq):
@@ -802,6 +734,7 @@
             return tuple(hs)
         hs = tuple(h0_ref[s, :, k * 128 : (k + 1) * 128] for k in range(blocks))
         lax.fori_loop(0, groups, group, hs)
+        hooks.half(s)
         for g in (groups - 2, groups - 1):
             out_copy(s, g, g % 2).wait()
     for cp in firsts:
@@ -878,7 +811,7 @@
 def return_kernel(dims, capacity, room, ret_ref, cot_ref, hid_ref, moe_ref, gate_ref, gated_ref, y_ref, u_ref, z_ref, dt_ref,
                   proj_ref, vec_ref, out_ref, gain_ref, router_ref, route_ref, slot_ref,
                   block_ref, ghid_ref, gy_ref, gz_ref, dout_ref, drouter_ref, dskip_ref, dgain_ref, adj_ref,
-                  hooks=QUIET, out_grads=None):
+                  hooks=QUIET):
     seqs, rows, inner, states, rank, taps = dims
     count = seqs * rows
     total, width = ret_ref.shape[0], hid_ref.shape[1]
@@ -901,11 +834,9 @@
     ghid_ref[...] = grad_hid
     branch = grad_hid.astype(jnp.bfloat16)
     hooks.activations()
-    if out_grads is not None:
-        out_grads(branch)
     for j in range(inner // WIDE):
         cols = slice(j * WIDE, (j + 1) * WIDE)
-        if out_grads is None:
+        if dout_ref is not None:
             dout_ref[cols, :] = dot_tn(gated_ref[:, cols], branch).astype(jnp.bfloat16)
         grad = dot_nt(branch, out_ref[cols, :])
         z = z_ref[:, cols]
@@ -978,9 +909,10 @@
         hooks.group(i)
         for c0 in range(0, inner, strip):
             sls = [slice(c0 + k, c0 + k + 128) for k in range(0, strip, 128)]
-            rates = [-jnp.exp(vec_ref[0:states, sl]) for sl in sls]
+            scaled = [-jnp.exp(vec_ref[0:states, sl]) * LOG2E for sl in sls]
             m = [adj[:, sl] for sl in sls]
             dd = [dvec_ref[0:states, sl] for sl in sls]
+            now = [hbuf[slot, GROUP * states : (GROUP + 1) * states, sl].astype(f32) for sl in sls]
             for half in reversed(range(GROUP // 8)):
                 a8 = pl.multiple_of(at + half * 8, 8)
                 d8 = [dt_ref[pl.ds(a8, 8), sl] for sl in sls]
@@ -994,17 +926,18 @@
                     for k, sl in enumerate(sls):
                         d, gy = d8[k][j : j + 1], g8[k][j : j + 1]
                         a = m[k] + ccol[t] * gy
-                        m[k] = jnp.exp2(d * (rates[k] * LOG2E)) * a
-                        p = m[k] * hbuf[slot, t * states : (t + 1) * states, sl].astype(f32) * rates[k]
+                        m[k] = jnp.exp2(d * scaled[k]) * a
+                        gb = gb + a * w8[k][j : j + 1]
+                        gc = gc + gy * now[k]
+                        now[k] = hbuf[slot, t * states : (t + 1) * states, sl].astype(f32)
+                        p = m[k] * now[k] * scaled[k]
                         dd[k] = dd[k] + p * d
-                        gb = gb + a * w8[k][j : j + 1]
-                        gc = gc + gy * hbuf[slot, (t + 1) * states : (t + 2) * states, sl].astype(f32)
                         r1[k][j], r2[k][j] = fold(p), fold(a * bcol[t])
                     gbsum[t] += gb
                     gcsum[t] += gc
                 for k, sl in enumerate(sls):
                     w1, w2 = row_sums(r1[k]), row_sums(r2[k])
-                    gdt[pl.ds(a8, 8), sl] = w1 + u8[k] * w2
+                    gdt[pl.ds(a8, 8), sl] = w1 * (1.0 / LOG2E) + u8[k] * w2
                     gu[pl.ds(a8, 8), sl] = d8[k] * w2
             for k, sl in enumerate(sls):
                 adj[:, sl] = m[k]
@@ -1021,6 +954,7 @@
         gproj[pl.ds(at, GROUP), :] = out
         return carry
     lax.fori_loop(0, steps, group, 0)
+    dvec_ref[0:states] = dvec_ref[0:states] * (1.0 / LOG2E)
     hooks.rest()
 
     low = rank_lanes(proj_ref[...], rank, states)
@@ -1315,7 +1249,7 @@
                 like(width, hidden_share),
                 like(hidden_share, width),
             ],
-            in_specs=[HBM] + [VM] * 2,
+            in_specs=[VM] * 3,
             out_specs=[HBM, HBM] + [VM] * 2,
             scratch_shapes=[
                 pltpu.VMEM((Z, block, wide), bf16),
@@ -1394,30 +1328,90 @@
         self.wait(*list(self.named))
 
 
-def forward_kernel(dims, share, low_share, experts, capacity, room, seq,
-                   tok_ref, halo_ref, tail_ref, cot_ref, route_ref, slot_ref, win_hbm, out_hbm,
-                   ext_hbm, z_hbm, u_hbm, dt_hbm, y_hbm, gated_hbm, hist_ref, proj_ref, dsum_ref, vec_ref, gain_ref,
-                   router_ref, hid_ref, moe_ref, gate_ref, rows_ref,
-                   win, out, ext, z, u, dt, y, gated, end, start, xn, hbuf, hcur, sem, sem0, sems, *relay_refs):
-    inner = dims[2]
+def forward_kernel(dims, share, low_share, experts, capacity, room, batch, seq,
+                   tok_ref, cot_ref, route_ref, slot_ref, state_ref, step_ref, router_in, *refs):
+    seqs, rows, inner = dims[:3]
+    lines, gains, refs = refs[:5], refs[5:7], refs[7:]
+    (win_in, out_in, tok_hbm,
+     win_hbm, out_hbm, tail_hbm, halo_hbm, ext_hbm, z_hbm, u_hbm, dt_hbm, y_hbm, gated_hbm, hist_ref,
+     proj_ref, dsum_ref, vec_ref, gain_ref, router_ref, hid_ref, moe_ref, gate_ref, rows_ref,
+     win, out, tail_all, halo, ext, z, u, dt, y, gated, end, start, xn, hbuf, hcur, sem, sem0,
+     tail, vecs, feats, zeros, send_sem, recv_sem, edge_sem, sems) = refs[:48]
+    relay_refs = refs[48:]
     moves = Moves(sems)
+    gather = Gatherer(batch, seq, (win_in, tail, out_in), (win_hbm, tail_hbm, out_hbm), send_sem, recv_sem)
+    WIN, TAIL, OUT = range(3)
+    relay = Relay(seq, True, dims[3], dsum_ref, vec_ref, end, start, *relay_refs)
+    b, s = gather.me.at()
+    has_before, has_after = s > 0, s < seq - 1
+    greet(gather.peers() + [(has_before, (b, s - 1)), (has_after, (b, s + 1))])
+
+    gather.give(WIN)
+    edges = [
+        pltpu.make_async_remote_copy(
+            src_ref=tok_hbm.at[i, pl.ds(rows - 8, 8)], dst_ref=halo_hbm.at[pl.ds(8 * i, 8)],
+            send_sem=edge_sem.at[0, i], recv_sem=edge_sem.at[1, i], device_id=(b, s + 1), device_id_type=MESH)
+        for i in range(seqs)
+    ]
+    none = pltpu.make_async_copy(zeros, halo_hbm, edge_sem.at[2, 0])
+    zeros[...] = jnp.zeros_like(zeros)
+
+    @pl.when(has_after)
+    def _():
+        for cp in edges:
+            cp.start()
+    pl.when(jnp.logical_not(has_before))(none.start)
+    pack_weights(tail, vecs, feats, state_ref, step_ref, router_in, lines, gains)
+    gather.give(TAIL)
+    moves.start("own", win_in, gather.part(WIN, gather.own))
+    moves.start("own", tail, gather.part(TAIL, gather.own))
+    moves.start("own out", out_in, gather.part(OUT, gather.own))
+    for h in range(1, gather.Z + 3):
+        gather.hop((WIN, TAIL), h)
+    gather.give(OUT)
+    gather.rest((WIN, TAIL))
+
+    @pl.when(has_before)
+    def _():
+        for cp in edges:
+            cp.wait_recv()
+    pl.when(jnp.logical_not(has_before))(none.wait)
+    moves.wait("own")
+    moves.start("head", halo_hbm, halo)
+    moves.start("head", tail_hbm, tail_all)
     for j in range(inner // WIDE):
         for base in (0, inner):
             cols = pl.ds(base + j * WIDE, WIDE)
             moves.start(("win", j), win_hbm.at[:, cols], win.at[:, cols])
-    moves.start("out", out_hbm, out)
-    relay = Relay(seq, True, dims[3], dsum_ref, vec_ref, end, start, *relay_refs)
-    greet(relay.peers())
+    moves.wait("head")
+
+    def weights(j):
+        moves.wait(("win", j))
+        if j == 4:
+            gather.hop((OUT,), 1)
 
     def projected():
         for name, src, dst in (("ext", ext, ext_hbm), ("z", z, z_hbm), ("u", u, u_hbm), ("dt", dt, dt_hbm)):
             moves.start(name, src, dst)
-
-    enter_packed(dims, share, low_share, experts, tok_ref, halo_ref, win, tail_ref, ext, z, u, dt, proj_ref, end,
+        gather.hop((OUT,), 2)
+
+    def scanned(i):
+        relay.start(i)
+        gather.hop((OUT,), 3 + i)
+
+    enter_packed(dims, share, low_share, experts, tok_ref, halo, win, tail_all, ext, z, u, dt, proj_ref, end,
                  dsum_ref, vec_ref, gain_ref, router_ref, xn,
-                 hooks=Hooks(weights=lambda j: moves.wait(("win", j)), projected=projected, scanned=relay.start))
+                 hooks=Hooks(weights=weights, projected=projected, scanned=scanned))
     for i in range(relay.count):
         relay.finish(i)
+    for h in range(3 + relay.count, gather.Z + 3):
+        gather.hop((OUT,), h)
+
+    def half(i):
+        if i == 0:
+            gather.rest((OUT,))
+            moves.wait("own out")
+            moves.start("out", out_hbm, out)
 
     def mixed():
         moves.start("y", y, y_hbm)
@@ -1425,8 +1419,14 @@
 
     leave_kernel(dims, capacity, room, tok_ref, cot_ref, start, dt, u, z, proj_ref, vec_ref, out, gain_ref, router_ref,
                  route_ref, slot_ref, hist_ref, y, hid_ref, gated, moe_ref, gate_ref, rows_ref, hbuf, hcur, sem, sem0,
-                 hooks=Hooks(out_proj=lambda: moves.wait("out"), mixed=mixed))
+                 hooks=Hooks(out_proj=lambda: moves.wait("out"), mixed=mixed, half=half))
     relay.settle()
+    gather.settle()
+
+    @pl.when(has_after)
+    def _():
+        for cp in edges:
+            cp.wait_send()
     moves.wait_all()
 
 
@@ -1450,54 +1450,58 @@
     ):
         moves.start(name, src, dst)
     relay = Relay(seq, False, states, dsum_ref, vec_ref, adj, later, *relay_refs)
-    reducer = Reducer(batch, seq, *(more[3 * i : 3 * i + 3] for i in range(5)), more[15:])
-    OUT, IN, REST = range(3)
+    reducer = Reducer(batch, seq, *(more[4 * i : 4 * i + 4] for i in range(5)), more[20:])
+    OUT, GATE, IN, REST = range(4)
     b, s = reducer.me.at()
     has_before, has_after = s > 0, s < seq - 1
     greet(reducer.peers() + [(has_before, (b, s - 1)), (has_after, (b, s + 1))])
-
-    def out_grads(branch):
-        cut = 8 * share
-        for q in range(devices // 8):
-            part = dot_tn(gated[:, q * cut : (q + 1) * cut], branch)
-            reducer.items[OUT][q * 8 : (q + 1) * 8] = part.astype(bf16).reshape(8, share, part.shape[1])
-        reducer.give(OUT, reducer.others)
+    me = reducer.me
 
     return_kernel(dims, capacity, room, ret_ref, cot_ref, hid_ref, moe_ref, gate_ref, gated, y, u, z, dt, proj_ref,
                   vec_ref, out, gain_ref, router_ref, route_ref, slot_ref,
                   block_ref, ghid, gy, gz, None, drouter, dskip, dmoe, adj,
                   hooks=Hooks(activations=lambda: moves.wait("gated", "out", "z", "y", "u"),
-                              gradients=lambda: moves.wait("dt"), scanned=relay.start),
-                  out_grads=out_grads)
-    for i in range(relay.count):
+                              gradients=lambda: moves.wait("dt"), scanned=relay.start))
+
+    def in_grads(a, grads, n, xx):
+        half, cut, wide = devices // 2, low_share * devices // 2, 2 * WIDE
+        at = pl.ds(pl.multiple_of(xx * cut, 128), cut)
+        for c0 in range(0, inner, wide):
+            part = dot_tn(xn[0:n, at], grads[:, c0 : c0 + wide]).reshape(half, low_share, wide)
+            reducer.items[a][pl.ds(xx * half, half), :, c0 : c0 + wide] = part.astype(bf16)
+        reducer.give(a, [(xx, 1 - me.y), (xx, me.y)])
+
+    branch = ghid[...].astype(bf16)
+    cut = 8 * share
+    for q in range(devices // 8):
+        part = dot_tn(gated[:, q * cut : (q + 1) * cut], branch)
+        reducer.items[OUT][q * 8 : (q + 1) * 8] = part.astype(bf16).reshape(8, share, part.shape[1])
+    reducer.give(OUT, reducer.others)
+    relay.finish(0)
+    moves.wait("tok")
+    x = tok[...].astype(f32)
+    xn[0:count] = (x * normalize(x) * gain_ref[0:1]).astype(bf16)
+    for xx in (1 - me.x, me.x):
+        in_grads(GATE, gz, count, xx)
+    for i in range(1, relay.count):
         relay.finish(i)
 
     def group(i):
         for g in range(4):
-            pl.when(i // reducer.Z == g)(functools.partial(reducer.step, OUT, g, i % reducer.Z))
-
-    def in_grads():
-        half, cut = devices // 2, low_share * devices // 2
-        wide = 2 * WIDE
-
-        def fill(xx):
-            at = pl.ds(pl.multiple_of(xx * cut, 128), cut)
-            items = pl.ds(xx * half, half)
-            for base, grads, n in ((0, gm, count + 8 * seqs), (inner, gz, count)):
-                for c0 in range(0, inner, wide):
-                    part = dot_tn(xn[0:n, at], grads[:, c0 : c0 + wide]).reshape(half, low_share, wide)
-                    reducer.items[IN][items, :, base + c0 : base + c0 + wide] = part.astype(bf16)
-
-        me = reducer.me
+            @pl.when(i // reducer.Z == g)
+            def _(g=g):
+                for a in (OUT, GATE):
+                    reducer.step(a, g, i % reducer.Z)
+
+    def late_grads():
         for xx in (1 - me.x, me.x):
-            fill(xx)
-            reducer.give(IN, [(xx, 1 - me.y), (xx, me.y)])
+            in_grads(IN, gm, count + 8 * seqs, xx)
 
     back_kernel(dims, tok, halo, ext, hist_ref, later, gy, gz, ghid, u, dt, proj_ref, win, tail, vec_ref, gain_ref,
                 dtok_ref, dhalo, None, dsmall, dvec, dnorm,
                 hbuf, ccol, bcol, gbsum, gcsum, carry, gdt, gu, gproj, gpad, gm, xn, gpre, sem,
-                hooks=Hooks(rest=lambda: moves.wait("ext", "win", "tail", "tok", "halo"), group=group),
-                in_grads=in_grads)
+                hooks=Hooks(rest=lambda: moves.wait("ext", "win", "tail", "halo"), group=group),
+                in_grads=late_grads)
     edge = reducer.copy(dhalo, next_ref, edge_sem.at[0], edge_sem.at[1], (b, s - 1))
     none = pltpu.make_async_copy(blank, next_ref, edge_sem.at[2])
     blank[...] = jnp.zeros_like(blank)
@@ -1511,10 +1515,11 @@
                 for a in (IN, REST):
                     reducer.step(a, g, k)
                 if g == 3:
-                    for a, ref in ((IN, in_out), (REST, tail_out), (OUT, out_out)):
+                    for a, ref in ((OUT, out_out), (GATE, in_out.at[:, inner:]), (IN, in_out.at[:, :inner]),
+                                   (REST, tail_out)):
                         reducer.line(a, k, ref)
     relay.settle()
-    for a in (OUT, IN, REST):
+    for a in (OUT, GATE, IN, REST):
         reducer.settle(a)
     pl.when(has_after)(edge.wait_recv)
     pl.when(has_before)(edge.wait_send)
@@ -1559,12 +1564,7 @@
     used = sum(a.shape[0] for a in lines)
     room = -(-used // 8) * 8
     fast = tuned(batch, seq)
-    if fast:
-        in_full, out_full, tail_full, halo = gather_all(
-            batch, seq, room, in_proj, out_proj, tokens, state_proj, step_proj, router_proj.T, lines,
-            (norm_gain[None], moe_gain[None]))
-        halo = halo.reshape(seqs * 8, width)
-    else:
+    if not fast:
         features = jnp.concatenate([router_proj, norm_gain[:, None], moe_gain[:, None]], axis=1)
         tail = jnp.concatenate(
             [
@@ -1616,21 +1616,33 @@
     drouter_s, dskip_s, dgain_s = like(width, tile), like(1, inner), like(1, width)
     wide = inner // WIDE
     if fast:
-        (ext, z, u, dt, y, gated, hist, proj, dsum, vec, gain, router, hid, moe_in, gate, sent) = pl.pallas_call(
-            partial(forward_kernel, dims, share, low_share, experts, capacity, room, seq),
-            out_shape=[ext_s, acts, acts, acts, acts, low_s, hist_s, proj_s, dsum_s, vec_s, gain_s, router_s,
-                       hid_s, moe_s, gate_s, rows_s],
-            in_specs=[VM] * 6 + [HBM] * 2,
-            out_specs=[HBM] * 7 + [VM] * 9,
+        in_s, out_s = like(width, 2 * inner, dtype=bf16), like(inner, width, dtype=bf16)
+        tail_s, halo_b = like(inner, 2 * tile, dtype=bf16), like(edge_rows, width, dtype=bf16)
+        (in_full, out_full, tail_full, halo, ext, z, u, dt, y, gated, hist, proj, dsum, vec, gain, router, hid, moe_in,
+         gate, sent) = pl.pallas_call(
+            partial(forward_kernel, dims, share, low_share, experts, capacity, room, batch, seq),
+            out_shape=[in_s, out_s, tail_s, halo_b, ext_s, acts, acts, acts, acts, low_s, hist_s, proj_s, dsum_s, vec_s,
+                       gain_s, router_s, hid_s, moe_s, gate_s, rows_s],
+            in_specs=[VM] * 16 + [HBM],
+            out_specs=[HBM] * 11 + [VM] * 9,
             scratch_shapes=[
-                vmem(in_full), vmem(out_full), vmem(ext_s), vmem(acts), vmem(acts), vmem(acts), vmem(acts), vmem(low_s),
-                vmem(state_s), vmem(state_s), normed, *leave_scratch, dma((2 * wide + 7,)),
+                vmem(in_s), vmem(out_s), vmem(tail_s), vmem(halo_b), vmem(ext_s), vmem(acts), vmem(acts), vmem(acts),
+                vmem(acts), vmem(low_s), vmem(state_s), vmem(state_s), normed, *leave_scratch,
+                pltpu.VMEM((share, 2 * tile), bf16),
+                pltpu.VMEM((room, share), f32),
+                pltpu.VMEM((8, low_share), f32),
+                vmem(halo_b),
+                dma((3, n_sends(seq // 2))),
+                dma((3, devices)),
+                dma((3, seqs)),
+                dma((2 * wide + 12,)),
                 *relay_scratch(seqs, states, inner),
             ],
             compiler_params=pltpu.CompilerParams(
                 collective_id=3, has_side_effects=True, vmem_limit_bytes=58 << 20),
             name="forward",
-        )(tok, halo, tail_full, cot, routes, slot_index, in_full, out_full)
+        )(tok, cot, routes, slot_index, state_proj, step_proj, router_proj.T, *lines, norm_gain[None], moe_gain[None],
+          in_proj, out_proj, tokens)
     else:
         vec = tail_full[:, tile : tile + room].T.astype(f32)
         router = tail_full[:, tile:].reshape(devices, share, tile)[:, :low_share].reshape(width, tile)
@@ -1661,15 +1673,15 @@
     back = back.reshape(total, 2 * width)
 
     if fast:
-        own = [(share, width), (low_share, 2 * inner), (share, 2 * tile)]
+        own = [(share, width), (low_share, inner), (low_share, inner), (share, 2 * tile)]
         block_out, d_tok, from_next, s_in, s_out, s_tail = pl.pallas_call(
             partial(backward_kernel, dims, share, low_share, experts, capacity, room, batch, seq),
-            out_shape=[moe_s, tok_s, halo_s, like(*own[1]), like(*own[0]), like(*own[2])],
+            out_shape=[moe_s, tok_s, halo_s, like(low_share, 2 * inner), like(*own[0]), like(*own[3])],
             in_specs=[VM] * 12 + [HBM] * 12,
             out_specs=[VM] * 2 + [HBM] + [VM] * 3,
             scratch_shapes=[
-                vmem(low_s), vmem(out_full), vmem(acts), vmem(acts), vmem(acts), vmem(acts), vmem(ext_s), vmem(in_full),
-                vmem(tail_full), vmem(tok), vmem(halo), vmem(acts), vmem(low_s), vmem(tok_s), vmem(state_s),
+                vmem(low_s), vmem(out_s), vmem(acts), vmem(acts), vmem(acts), vmem(acts), vmem(ext_s), vmem(in_s),
+                vmem(tail_s), vmem(tok), vmem(halo_b), vmem(acts), vmem(low_s), vmem(tok_s), vmem(state_s),
                 vmem(state_s), vmem(halo_s), vmem(dsmall_s), vmem(vec_s), vmem(dgain_s), vmem(dgain_s),
                 vmem(drouter_s), vmem(dskip_s), vmem(halo_s), *back_scratch, dma((12,)), dma((3,)),
                 *relay_scratch(seqs, states, inner), *reduce_scratch(devices, seq // 2, own),
@@ -1701,25 +1713,21 @@
 
     skip_row = states + taps + 2
     if fast:
-        steps = 4
-        slab = lambda a: pl.BlockSpec((a.shape[0] // steps, a.shape[1]), lambda i: (i, 0))
-        whole = lambda *shape: pl.BlockSpec(shape, lambda i: (0,) * len(shape))
-        piece = pl.BlockSpec((seqs, rows // steps, width), lambda i: (0, i, 0))
         shapes = [
             s_in.shape, (taps, share), (1, share), (share, rank + 2 * states), (rank, share), (1, share),
             (states, share), (1, share), s_out.shape, (1, low_share), (1, low_share), (experts, low_share),
         ]
+        block_out, d_tok = block_out.reshape(tokens.shape), d_tok.reshape(tokens.shape)
         block_out, d_tok, *sums, d_up, d_down = pl.pallas_call(
             partial(finish_kernel, dims, low_share, experts),
-            out_shape=[like(*tokens.shape, dtype=bf16), like(*tokens.shape)] + [like(*a) for a in shapes] + [like(*d_up.shape), like(*d_down.shape)],
-            grid=(steps,),
-            in_specs=[whole(*s_in.shape), whole(*s_out.shape), whole(*s_tail.shape), whole(seqs, 8, width), piece, piece]
-            + [slab(a) for a in (d_up, d_down)],
-            out_specs=[piece, piece] + [whole(*a) for a in shapes] + [slab(d_up), slab(d_down)],
+            out_shape=[like(*tokens.shape, dtype=bf16), like(*tokens.shape)] + [like(*a) for a in shapes]
+            + [like(*d_up.shape), like(*d_down.shape)],
+            in_specs=[VM] * 4 + [HBM] * 4,
+            out_specs=[HBM] * 2 + [VM] * 12 + [HBM] * 2,
+            scratch_shapes=[vmem(block_out), vmem(d_tok), vmem(d_up), vmem(d_down), dma((20,))],
             compiler_params=params(),
             name="finish",
-        )(s_in, s_out, s_tail, from_next.reshape(seqs, 8, width), d_tok.reshape(tokens.shape),
-          block_out.reshape(tokens.shape), d_up, d_down)
+        )(s_tail, from_next.reshape(seqs, 8, width), s_in, s_out, block_out, d_tok, d_up, d_down)
         for i in (2, 5, 7, 9, 10):
             sums[i] = sums[i][0]
         sums[11] = sums[11].T

time: 264 us -> 251 us (0.951)
  Pallas kernels: 263 us -> 250 us
    pallas_call x1 -> x0, Pallas kernels: 43.6 us -> none  [gather_all(): pl.pallas_call(functools.partial(gather_kernel, batch, seq), out_shape=[j...]
    pallas_call x1, Pallas kernels: 35.1 us -> 70.9 us  [body(): pl.pallas_call(partial(forward_kernel, dims, share, low_share, experts, c...]
    pallas_call x1, Pallas kernels: 97.8 us -> 89.8 us  [body(): pl.pallas_call(partial(backward_kernel, dims, share, low_share, experts,...]
where the time goes in v3:
time: 251 us
  Pallas kernels  250 us (100%)
    pallas_call x1, Pallas kernels, body(): pl.pallas_call(partial(backward_kernel, dims, share, low_share, experts,...  89.8 us
    pallas_call x1, Pallas kernels, moe_rows(): pl.pallas_call(functools.partial(moe_kernel, seq), out_shape=[like(seq, c...  82 us
    pallas_call x1, Pallas kernels, body(): pl.pallas_call(partial(forward_kernel, dims, share, low_share, experts, c...  70.9 us
    pallas_call x1, Pallas kernels, body(): pl.pallas_call(partial(finish_kernel, dims, low_share, experts), out_shap...  7.13 us

profile of v3, /device:TPU:0, one launch (start us, length us, event | category | flops | bytes accessed | tf_op | source)
XLA Modules:
  0.0 250.7 jit_solution(10143125101803199333)
XLA Ops:
  0.7 70.9 %forward.1 = (bf16[768,3072]{1,0:T(8,128)(2,1)}, bf16[1536,768]{1,0:T(8,128)(2,1)}, bf16[1536,256]{1,0:T(8,128)(2,1)}, bf16[16,768]{1,0:T(8,128)(2,1)}, f32[2,13...) custom-call(bf16[256,768]{1,0:T(8,128)(2,1)} %bitcast.23, ...), custom_call_target="tpu_custom_call" | custom-call | tf_op jit(solution)/shard_map/forward/pallas_call | solution.py:1622
  71.6 82.0 %experts.1 = (bf16[8,40,1536]{2,1,0:T(8,128)(2,1)}, bf16[2,320,1536]{2,1,0:T(8,128)(2,1)}, f32[768,768]{1,0:T(8,128)}, f32[768,768]{1,0:T(8,128)}) custom-call(bf16[8,40,1536]{2,1,0:T(8,128)(2,1)} %bitcast.30, bf16[768,768]{1,0:T(8,128)(2,1)} %bitcast.27, bf16[768,768]{1,0:T(8,128)(2,1)} %bitcast.28), custom_call_target="tpu_custom_call" | custom-call | tf_op jit(solution)/shard_map/experts/pallas_call | solution.py:1244
  153.5 89.8 %backward.1 = (bf16[256,768]{1,0:T(8,128)(2,1)}, f32[256,768]{1,0:T(8,128)}, f32[16,768]{1,0:T(8,128)}, f32[24,3072]{1,0:T(8,128)}, f32[48,768]{1,0:T(8,128)}, /*index=5*/f32[48,256]{1,0:T(8,128)}) custom-call(bf16[320,1536]{1,0:T(8,128)(2,1)} %bitcast.29, bf16[256,768]{1,0:T(8,128)(2,1)} %bitcast.26, f32[256,768]{1,0:T(8,128)} %get-tuple-element.63.hid_ref, ...), custom_call_target="tpu_custom_call" | custom-call | tf_op jit(solution)/shard_map/backward/pallas_call | solution.py:1677
  243.3 7.1 %finish.1 = (bf16[2,128,768]{2,1,0:T(8,128)(2,1)}, f32[2,128,768]{2,1,0:T(8,128)}, f32[24,3072]{1,0:T(8,128)}, f32[4,48]{1,0:T(4,128)}, f32[1,48]{1,0:T(1,128)},...) custom-call(f32[48,256]{1,0:T(8,128)} %get-tuple-element.82.tail_ref, ...), custom_call_target="tpu_custom_call" | custom-call | tf_op jit(solution)/shard_map/finish/pallas_call | solution.py:1721

commit v4 on v3

--- a/solution.py
+++ b/solution.py
@@ -184,15 +184,14 @@
         self.me = me = Place(batch, seq)
         self.Z, self.z = me.Z, me.z
         self.sib = me.at(c=1 - me.c)
-        self.up, self.down = me.at(z=me.z + 1), me.at(z=me.z - 1)
         self.nx, self.ny = me.at(x=1 - me.x), me.at(y=1 - me.y)
         pick = lambda a, b: tuple(jnp.where(me.c == 0, p, q) for p, q in zip(a, b))
         self.near, self.far = pick(self.ny, self.nx), pick(self.nx, self.ny)
         self.mine, self.others = self.groups(me.c), self.groups(1 - me.c)
 
     def peers(self):
-        return [(None, self.sib), (None, self.nx), (None, self.ny),
-                (self.z < self.Z - 1, self.up), (self.z > 0, self.down)]
+        column = [(None, self.me.at(z=self.turn(k))) for k in range(self.Z - 1)]
+        return [(None, self.sib), (None, self.nx), (None, self.ny)] + column
 
     def groups(self, c):
         me = self.me
@@ -258,36 +257,22 @@
             self.to_far(a, g, k).start()
         elif g == 2:
             self.to_near(a, k).start()
+        else:
+            pl.when(k < self.Z - 1)(lambda: self.onward(a, k).start())
 
     def onward(self, a, k):
         t = self.turn(k)
-        rising = t > self.z
-        side = jnp.where(rising, 0, 1)
-        dev = (self.me.at()[0], jnp.where(rising, self.up[1], self.down[1]))
-        return self.copy(self.item(a, self.me.c, self.mine[3], t), self.line_bufs[a].at[side, t],
-                         self.line_send.at[a, k], self.line_recv.at[a, side, t], dev)
-
-    def line(self, a, k, out_ref):
-        t = self.turn(k)
-        item = self.item(a, self.me.c, self.mine[3], t)
-
-        def take(side):
-            ref = self.line_bufs[a].at[side, t]
-            self.copy(ref, ref, self.sib_send.at[a, 0], self.line_recv.at[a, side, t], self.sib).wait_recv()
-            return ref[...].astype(f32)
-        if k < self.Z - 1:
-            rising = t > self.z
-
-            @pl.when(jnp.where(rising, self.z, self.Z - 1 - self.z) > 0)
-            def _():
-                item[...] = (item[...].astype(f32) + take(jnp.where(rising, 0, 1))).astype(bf16)
-            self.onward(a, k).start()
-        else:
-            out_ref[...] = item[...].astype(f32)
-            for side, pred in ((0, self.z > 0), (1, self.z < self.Z - 1)):
-                @pl.when(pred)
-                def _(side=side):
-                    out_ref[...] = out_ref[...] + take(side)
+        return self.copy(self.item(a, self.me.c, self.mine[3], t), self.line_bufs[a].at[self.z],
+                         self.line_send.at[a, k], self.line_recv.at[a, self.z], self.me.at(z=t))
+
+    def result(self, a, out_ref):
+        total = self.item(a, self.me.c, self.mine[3], self.z)[...].astype(f32)
+        for k in range(self.Z - 1):
+            t = self.turn(k)
+            ref = self.line_bufs[a].at[t]
+            self.copy(ref, ref, self.sib_send.at[a, 0], self.line_recv.at[a, t], self.sib).wait_recv()
+            total = total + ref[...].astype(f32)
+        out_ref[...] = total
 
     def settle(self, a):
         def one(k, carry):
@@ -306,9 +291,9 @@
 
 def reduce_scratch(count, Z, shapes):
     half, n, dma = count // 2, len(shapes), pltpu.SemaphoreType.DMA
-    bufs = [pltpu.VMEM(lead + s, bf16) for lead in ((count,), (half,), (2 * Z,), (Z,), (2, Z)) for s in shapes]
+    bufs = [pltpu.VMEM(lead + s, bf16) for lead in ((count,), (half,), (2 * Z,), (Z,), (Z,)) for s in shapes]
     return bufs + [dma((n, half)), dma((n, half)), dma((n, 2 * Z)), dma((n, 2 * Z)), dma((n, Z)), dma((n, Z)),
-                   dma((n, Z)), dma((n, 2, Z))]
+                   dma((n, Z)), dma((n, Z))]
 
 
 def pack_tail(tail, low_share, experts, skip_row, dsmall_ref, dvec_ref, dskip_ref, drouter_ref, dnorm_ref, dmoe_ref):
@@ -1514,10 +1499,8 @@
             if 0 <= k < reducer.Z:
                 for a in (IN, REST):
                     reducer.step(a, g, k)
-                if g == 3:
-                    for a, ref in ((OUT, out_out), (GATE, in_out.at[:, inner:]), (IN, in_out.at[:, :inner]),
-                                   (REST, tail_out)):
-                        reducer.line(a, k, ref)
+    for a, ref in ((OUT, out_out), (GATE, in_out.at[:, inner:]), (IN, in_out.at[:, :inner]), (REST, tail_out)):
+        reducer.result(a, ref)
     relay.settle()
     for a in (OUT, GATE, IN, REST):
         reducer.settle(a)

time: 251 us -> 242 us (0.964)
  Pallas kernels: 250 us -> 241 us
    pallas_call x1, Pallas kernels: 89.8 us -> 80.8 us  [body(): pl.pallas_call(partial(backward_kernel, dims, share, low_share, experts,...]
where the time goes in v4:
time: 242 us
  Pallas kernels  241 us (100%)
    pallas_call x1, Pallas kernels, moe_rows(): pl.pallas_call(functools.partial(moe_kernel, seq), out_shape=[like(seq, c...  82 us
    pallas_call x1, Pallas kernels, body(): pl.pallas_call(partial(backward_kernel, dims, share, low_share, experts,...  80.8 us
    pallas_call x1, Pallas kernels, body(): pl.pallas_call(partial(forward_kernel, dims, share, low_share, experts, c...  70.9 us
    pallas_call x1, Pallas kernels, body(): pl.pallas_call(partial(finish_kernel, dims, low_share, experts), out_shap...  7.13 us

profile of v4, /device:TPU:0, one launch (start us, length us, event | category | flops | bytes accessed | tf_op | source)
XLA Modules:
  0.0 241.7 jit_solution(2554809275897748323)
XLA Ops:
  0.7 70.9 %forward.1 = (bf16[768,3072]{1,0:T(8,128)(2,1)}, bf16[1536,768]{1,0:T(8,128)(2,1)}, bf16[1536,256]{1,0:T(8,128)(2,1)}, bf16[16,768]{1,0:T(8,128)(2,1)}, f32[2,13...) custom-call(bf16[256,768]{1,0:T(8,128)(2,1)} %bitcast.23, ...), custom_call_target="tpu_custom_call" | custom-call | tf_op jit(solution)/shard_map/forward/pallas_call | solution.py:1605
  71.6 82.0 %experts.1 = (bf16[8,40,1536]{2,1,0:T(8,128)(2,1)}, bf16[2,320,1536]{2,1,0:T(8,128)(2,1)}, f32[768,768]{1,0:T(8,128)}, f32[768,768]{1,0:T(8,128)}) custom-call(bf16[8,40,1536]{2,1,0:T(8,128)(2,1)} %bitcast.30, bf16[768,768]{1,0:T(8,128)(2,1)} %bitcast.27, bf16[768,768]{1,0:T(8,128)(2,1)} %bitcast.28), custom_call_target="tpu_custom_call" | custom-call | tf_op jit(solution)/shard_map/experts/pallas_call | solution.py:1229
  153.5 80.8 %backward.1 = (bf16[256,768]{1,0:T(8,128)(2,1)}, f32[256,768]{1,0:T(8,128)}, f32[16,768]{1,0:T(8,128)}, f32[24,3072]{1,0:T(8,128)}, f32[48,768]{1,0:T(8,128)}, /*index=5*/f32[48,256]{1,0:T(8,128)}) custom-call(bf16[320,1536]{1,0:T(8,128)(2,1)} %bitcast.29, bf16[256,768]{1,0:T(8,128)(2,1)} %bitcast.26, f32[256,768]{1,0:T(8,128)} %get-tuple-element.63.hid_ref, ...), custom_call_target="tpu_custom_call" | custom-call | tf_op jit(solution)/shard_map/backward/pallas_call | solution.py:1660
  234.4 7.1 %finish.1 = (bf16[2,128,768]{2,1,0:T(8,128)(2,1)}, f32[2,128,768]{2,1,0:T(8,128)}, f32[24,3072]{1,0:T(8,128)}, f32[4,48]{1,0:T(4,128)}, f32[1,48]{1,0:T(1,128)},...) custom-call(f32[48,256]{1,0:T(8,128)} %get-tuple-element.82.tail_ref, ...), custom_call_target="tpu_custom_call" | custom-call | tf_op jit(solution)/shard_map/finish/pallas_call | solution.py:1704

commit v5 on v4

--- a/solution.py
+++ b/solution.py
@@ -1372,24 +1372,24 @@
 
     def weights(j):
         moves.wait(("win", j))
-        if j == 4:
-            gather.hop((OUT,), 1)
+        if j in (2, 5):
+            gather.hop((OUT,), 1 + j // 5)
 
     def projected():
         for name, src, dst in (("ext", ext, ext_hbm), ("z", z, z_hbm), ("u", u, u_hbm), ("dt", dt, dt_hbm)):
             moves.start(name, src, dst)
-        gather.hop((OUT,), 2)
+        gather.hop((OUT,), 3)
 
     def scanned(i):
         relay.start(i)
-        gather.hop((OUT,), 3 + i)
+        gather.hop((OUT,), 4 + i)
 
     enter_packed(dims, share, low_share, experts, tok_ref, halo, win, tail_all, ext, z, u, dt, proj_ref, end,
                  dsum_ref, vec_ref, gain_ref, router_ref, xn,
                  hooks=Hooks(weights=weights, projected=projected, scanned=scanned))
     for i in range(relay.count):
         relay.finish(i)
-    for h in range(3 + relay.count, gather.Z + 3):
+    for h in range(4 + relay.count, gather.Z + 3):
         gather.hop((OUT,), h)
 
     def half(i):

time: 242 us -> 238 us (0.983)
  Pallas kernels: 241 us -> 237 us
    pallas_call x1, Pallas kernels: 82 us -> 73.2 us  [moe_rows(): pl.pallas_call(functools.partial(moe_kernel, seq), out_shape=[like(seq, c...]
    pallas_call x1, Pallas kernels: 70.9 us -> 73.4 us  [body(): pl.pallas_call(partial(forward_kernel, dims, share, low_share, experts, c...]
where the time goes in v5:
time: 238 us; the launch traced here: 237 us
  Pallas kernels  237 us (100%)
    pallas_call x1, Pallas kernels, body(): pl.pallas_call(partial(backward_kernel, dims, share, low_share, experts,...  82.8 us
    pallas_call x1, Pallas kernels, body(): pl.pallas_call(partial(forward_kernel, dims, share, low_share, experts, c...  73.4 us
    pallas_call x1, Pallas kernels, moe_rows(): pl.pallas_call(functools.partial(moe_kernel, seq), out_shape=[like(seq, c...  73.2 us
    pallas_call x1, Pallas kernels, body(): pl.pallas_call(partial(finish_kernel, dims, low_share, experts), out_shap...  7.13 us

profile of v5, /device:TPU:0, one launch (start us, length us, event | category | flops | bytes accessed | tf_op | source)
XLA Modules:
  0.0 237.4 jit_solution(4163298817498723070)
XLA Ops:
  0.7 73.4 %forward.1 = (bf16[768,3072]{1,0:T(8,128)(2,1)}, bf16[1536,768]{1,0:T(8,128)(2,1)}, bf16[1536,256]{1,0:T(8,128)(2,1)}, bf16[16,768]{1,0:T(8,128)(2,1)}, f32[2,13...) custom-call(bf16[256,768]{1,0:T(8,128)(2,1)} %bitcast.23, ...), custom_call_target="tpu_custom_call" | custom-call | tf_op jit(solution)/shard_map/forward/pallas_call | solution.py:1605
  74.1 73.2 %experts.1 = (bf16[8,40,1536]{2,1,0:T(8,128)(2,1)}, bf16[2,320,1536]{2,1,0:T(8,128)(2,1)}, f32[768,768]{1,0:T(8,128)}, f32[768,768]{1,0:T(8,128)}) custom-call(bf16[8,40,1536]{2,1,0:T(8,128)(2,1)} %bitcast.30, bf16[768,768]{1,0:T(8,128)(2,1)} %bitcast.27, bf16[768,768]{1,0:T(8,128)(2,1)} %bitcast.28), custom_call_target="tpu_custom_call" | custom-call | tf_op jit(solution)/shard_map/experts/pallas_call | solution.py:1229
  147.3 82.8 %backward.1 = (bf16[256,768]{1,0:T(8,128)(2,1)}, f32[256,768]{1,0:T(8,128)}, f32[16,768]{1,0:T(8,128)}, f32[24,3072]{1,0:T(8,128)}, f32[48,768]{1,0:T(8,128)}, /*index=5*/f32[48,256]{1,0:T(8,128)}) custom-call(bf16[320,1536]{1,0:T(8,128)(2,1)} %bitcast.29, bf16[256,768]{1,0:T(8,128)(2,1)} %bitcast.26, f32[256,768]{1,0:T(8,128)} %get-tuple-element.63.hid_ref, ...), custom_call_target="tpu_custom_call" | custom-call | tf_op jit(solution)/shard_map/backward/pallas_call | solution.py:1660
  230.1 7.1 %finish.1 = (bf16[2,128,768]{2,1,0:T(8,128)(2,1)}, f32[2,128,768]{2,1,0:T(8,128)}, f32[24,3072]{1,0:T(8,128)}, f32[4,48]{1,0:T(4,128)}, f32[1,48]{1,0:T(1,128)},...) custom-call(f32[48,256]{1,0:T(8,128)} %get-tuple-element.82.tail_ref, ...), custom_call_target="tpu_custom_call" | custom-call | tf_op jit(solution)/shard_map/finish/pallas_call | solution.py:1704

commit v6 on v5

--- a/solution.py
+++ b/solution.py
@@ -312,15 +312,16 @@
 
 def finish_kernel(dims, low_share, experts, tail_ref, halo_ref, in_ref, out_ref, block_hbm, tok_hbm, up_hbm, down_hbm,
                   block_out, tok_out, din, dconv, dbias, dstate, dstep, dstep_bias, ddecay, dskip, dout, dnorm, dmoe,
-                  drouter, dup, ddown, block, tok, up, down, sems):
+                  drouter, dup, ddown, block, tok, up, down, up_wide, down_wide, sems):
     seqs, rows, inner, states, rank, taps = dims
     moves = Moves(sems)
-    routes = []
+    routes, widened = [], {}
     for i in range(4):
-        for src, at, dst in ((up_hbm, up, dup), (down_hbm, down, ddown)):
+        for src, at, wide, dst in ((up_hbm, up, up_wide, dup), (down_hbm, down, down_wide, ddown)):
             n = src.shape[0] // 4
             piece = pl.ds(i * n, n)
             routes.append((len(routes), src.at[piece], at.at[piece], dst.at[piece]))
+            widened[routes[-1][0]] = wide.at[piece]
     routes.append(("tok", tok_hbm, tok, tok_out))
     routes.append(("block", block_hbm, block, block_out))
     for name, src, at, _ in routes:
@@ -349,6 +350,9 @@
         moves.wait(name)
         if name == "tok":
             tok[:, rows - 8 :] = tok[:, rows - 8 :] + halo_ref[...]
+        if name in widened:
+            widened[name][...] = at[...].astype(f32)
+            at = widened[name]
         moves.start("out", at, dst)
     moves.wait_all()
 
@@ -929,14 +933,14 @@
                 dvec_ref[0:states, sl] = dd[k]
         square = (states, small.shape[1])
         where, entry = lanes(square), subs(square)
-        line = subs((GROUP, small.shape[1]))
-        out = jnp.zeros(small.shape, f32)
-        for t in range(GROUP):
-            gb = jnp.broadcast_to(jnp.sum(gbsum[t], axis=1, keepdims=True), square)
-            gc = jnp.broadcast_to(jnp.sum(gcsum[t], axis=1, keepdims=True), square)
-            put = jnp.where(where == entry + rank, gb, jnp.where(where == entry + rank + states, gc, 0.0))
-            out = jnp.where(line == t, jnp.sum(put, axis=0, keepdims=True), out)
-        gproj[pl.ds(at, GROUP), :] = out
+        for half in range(GROUP // 8):
+            parts = []
+            for t in range(half * 8, half * 8 + 8):
+                gb = jnp.broadcast_to(jnp.sum(gbsum[t], axis=1, keepdims=True), square)
+                gc = jnp.broadcast_to(jnp.sum(gcsum[t], axis=1, keepdims=True), square)
+                put = jnp.where(where == entry + rank, gb, jnp.where(where == entry + rank + states, gc, 0.0))
+                parts.append(fold(put))
+            gproj[pl.ds(pl.multiple_of(at + half * 8, 8), 8), :] = row_sums(parts)
         return carry
     lax.fori_loop(0, steps, group, 0)
     dvec_ref[0:states] = dvec_ref[0:states] * (1.0 / LOG2E)
@@ -1024,7 +1028,7 @@
 
 def moe_kernel(seq, rows_ref, up_ref, down_ref,
                back_ref, land_ref, dup_ref, ddown_ref,
-               xbuf, part, act, ghid, hid, gact, far_buf, own_sum, up2_ref, down2_ref, dup2, ddown2, dup3, ddown3,
+               xbuf, part, act, ghid, hid, gact, far_buf, own_sum, up2_ref, down2_ref, dup2, ddown2, dup3, ddown3, dup_sum, ddown_sum,
                local_sem, disp_sem, pass_sem, recv_sem, load_sem, far_send, far_recv,
                final_send, final_recv, final_local, swap_send, swap_recv):
     me = Place(4, seq)
@@ -1187,12 +1191,12 @@
         ddown2[n : n + WIDE, :] = dot_tn(act[:, share + n : share + n + WIDE], g_all()).astype(bf16)
     grads[1].start()
     for n in range(0, share, WIDE):
-        dup_ref[:, n : n + WIDE] = dot_tn(x_all(), ghid[:, n : n + WIDE])
-        ddown_ref[n : n + WIDE, :] = dot_tn(act[:, n : n + WIDE], g_all())
+        dup_sum[:, n : n + WIDE] = dot_tn(x_all(), ghid[:, n : n + WIDE])
+        ddown_sum[n : n + WIDE, :] = dot_tn(act[:, n : n + WIDE], g_all())
     grads[0].wait_recv()
-    dup_ref[...] += dup3[...].astype(f32)
+    dup_ref[...] = (dup_sum[...] + dup3[...].astype(f32)).astype(bf16)
     grads[1].wait_recv()
-    ddown_ref[...] += ddown3[...].astype(f32)
+    ddown_ref[...] = (ddown_sum[...] + ddown3[...].astype(f32)).astype(bf16)
     for cp in weights + grads:
         cp.wait_send()
 
@@ -1231,8 +1235,8 @@
             out_shape=[
                 like(seq, capacity, wide, dtype=bf16),
                 like(2, seq * capacity, wide, dtype=bf16),
-                like(width, hidden_share),
-                like(hidden_share, width),
+                like(width, hidden_share, dtype=bf16),
+                like(hidden_share, width, dtype=bf16),
             ],
             in_specs=[VM] * 3,
             out_specs=[HBM, HBM] + [VM] * 2,
@@ -1248,6 +1252,8 @@
                 *quarter,
                 *quarter,
                 *quarter,
+                pltpu.VMEM((width, hidden_share), f32),
+                pltpu.VMEM((hidden_share, width), f32),
                 dma,
                 dma((2 * Z,)),
                 dma((seq,)),
@@ -1707,7 +1713,10 @@
             + [like(*d_up.shape), like(*d_down.shape)],
             in_specs=[VM] * 4 + [HBM] * 4,
             out_specs=[HBM] * 2 + [VM] * 12 + [HBM] * 2,
-            scratch_shapes=[vmem(block_out), vmem(d_tok), vmem(d_up), vmem(d_down), dma((20,))],
+            scratch_shapes=[
+                vmem(block_out), vmem(d_tok), vmem(d_up), vmem(d_down), vmem(like(*d_up.shape)), vmem(like(*d_down.shape)),
+                dma((20,)),
+            ],
             compiler_params=params(),
             name="finish",
         )(s_tail, from_next.reshape(seqs, 8, width), s_in, s_out, block_out, d_tok, d_up, d_down)

time: 238 us -> 235 us (0.987)
  Pallas kernels: 237 us -> 234 us
where the time goes in v6:
time: 235 us
  Pallas kernels  234 us (100%)
    pallas_call x1, Pallas kernels, body(): pl.pallas_call(partial(backward_kernel, dims, share, low_share, experts,...  82.7 us
    pallas_call x1, Pallas kernels, body(): pl.pallas_call(partial(forward_kernel, dims, share, low_share, experts, c...  73.4 us
    pallas_call x1, Pallas kernels, moe_rows(): pl.pallas_call(functools.partial(moe_kernel, seq), out_shape=[like(seq, c...  72.5 us
    pallas_call x1, Pallas kernels, body(): pl.pallas_call(partial(finish_kernel, dims, low_share, experts), out_shap...  5.59 us

profile of v6, /device:TPU:0, one launch (start us, length us, event | category | flops | bytes accessed | tf_op | source)
XLA Modules:
  0.0 235.1 jit_solution(14205143080702198023)
XLA Ops:
  0.7 73.4 %forward.1 = (bf16[768,3072]{1,0:T(8,128)(2,1)}, bf16[1536,768]{1,0:T(8,128)(2,1)}, bf16[1536,256]{1,0:T(8,128)(2,1)}, bf16[16,768]{1,0:T(8,128)(2,1)}, f32[2,13...) custom-call(bf16[256,768]{1,0:T(8,128)(2,1)} %bitcast.23, ...), custom_call_target="tpu_custom_call" | custom-call | tf_op jit(solution)/shard_map/forward/pallas_call | solution.py:1611
  74.1 72.5 %experts.1 = (bf16[8,40,1536]{2,1,0:T(8,128)(2,1)}, bf16[2,320,1536]{2,1,0:T(8,128)(2,1)}, bf16[768,768]{1,0:T(8,128)(2,1)}, bf16[768,768]{1,0:T(8,128)(2,1)}) custom-call(bf16[8,40,1536]{2,1,0:T(8,128)(2,1)} %bitcast.30, bf16[768,768]{1,0:T(8,128)(2,1)} %bitcast.27, bf16[768,768]{1,0:T(8,128)(2,1)} %bitcast.28), custom_call_target="tpu_custom_call" | custom-call | tf_op jit(solution)/shard_map/experts/pallas_call | solution.py:1233
  146.6 82.7 %backward.1 = (bf16[256,768]{1,0:T(8,128)(2,1)}, f32[256,768]{1,0:T(8,128)}, f32[16,768]{1,0:T(8,128)}, f32[24,3072]{1,0:T(8,128)}, f32[48,768]{1,0:T(8,128)}, /*index=5*/f32[48,256]{1,0:T(8,128)}) custom-call(bf16[320,1536]{1,0:T(8,128)(2,1)} %bitcast.29, bf16[256,768]{1,0:T(8,128)(2,1)} %bitcast.26, f32[256,768]{1,0:T(8,128)} %get-tuple-element.63.hid_ref, ...), custom_call_target="tpu_custom_call" | custom-call | tf_op jit(solution)/shard_map/backward/pallas_call | solution.py:1666
  229.3 5.6 %finish.1 = (bf16[2,128,768]{2,1,0:T(8,128)(2,1)}, f32[2,128,768]{2,1,0:T(8,128)}, f32[24,3072]{1,0:T(8,128)}, f32[4,48]{1,0:T(4,128)}, f32[1,48]{1,0:T(1,128)},...) custom-call(f32[48,256]{1,0:T(8,128)} %get-tuple-element.82.tail_ref, ...), custom_call_target="tpu_custom_call" | custom-call | tf_op jit(solution)/shard_map/finish/pallas_call | solution.py:1710
